TPU v7x, 32 devices: a whole 2x2x4 slice. The times are simulated.
32 devices in a mesh: seq: 4 (over y, x), wshard: 8 (over z, core).
Axes of the slice: x: 2, y: 2, z: 4, core: 2. Of those that a mesh axis runs over, the one named last changes fastest.
Arguments:
- tokens: bfloat16 [8, 3072, 768], P('wshard', 'seq'), may hold values from -6 to 6
- teacher: bfloat16 [8, 3072, 768], P('wshard', 'seq'), may hold values from -6 to 6
- lengths: int32 [8, 4], P('wshard'), may hold values from 128 to 512, as said below
- w_query: bfloat16 [768, 768], P('wshard'), may hold values from -0.0546875 to 0.0546875
- w_key: bfloat16 [768, 768], P('wshard'), may hold values from -0.21875 to 0.21875
- w_value: bfloat16 [768, 768], P('wshard'), may hold values from -0.21875 to 0.21875
- w_out: bfloat16 [768, 768], P('wshard'), may hold values from -0.625 to 0.625
- w_in: bfloat16 [768, 3072], P('wshard'), may hold values from -0.21875 to 0.21875
- w_ff: bfloat16 [3072, 768], P('wshard'), may hold values from -0.15625 to 0.15625
- gain_attn: bfloat16 [768], P('wshard'), may hold values from 0.5 to 1.5
- gain_ff: bfloat16 [768], P('wshard'), may hold values from 0.5 to 1.5
- bias_table: bfloat16 [32, 12], replicated, may hold values from -4 to 4
Outputs:
- output: bfloat16 [8, 3072, 768], P('wshard', 'seq')
- tokens_grad: float32 [8, 3072, 768], P('wshard', 'seq')
- w_query_grad: float32 [768, 768], P('wshard')
- w_key_grad: float32 [768, 768], P('wshard')
- w_value_grad: float32 [768, 768], P('wshard')
- w_out_grad: float32 [768, 768], P('wshard')
- w_in_grad: float32 [768, 3072], P('wshard')
- w_ff_grad: float32 [3072, 768], P('wshard')
- gain_attn_grad: float32 [768], P('wshard')
- gain_ff_grad: float32 [768], P('wshard')
- bias_table_grad: float32 [32, 12], replicated
Inputs may be any that keep to these rules, and one draw needn't show every extreme that they name: `lengths`: in every group one of the 4 continuations, drawn at random, has exactly 512 valid tokens; the others have 512 // 4 or more.
All inputs are finite; a program needn't handle non-finite values.
Results may differ from a plain program's by a relative error of at most 0.025.
The roundings to bfloat16 on the way count: a program that leaves them out, or rounds other values in their place, can miss the bound.
Values may be sent and summed in bfloat16 or wider, within the bound.
No kernel may reach another device: no remote copies, remote signals or barrier semaphores. Data moves between devices by JAX's collectives and lax.ppermute only.
A program may use at most 192 MiB of HBM per device.

v0:
```python
import jax
import jax.numpy as jnp
from jax import lax
from jax.sharding import PartitionSpec as P

DH = 64
NB = 32
PLEN = 1024
CLEN = 512
CONT = 4


EPSILON = 1e-06
NEGATIVE = -1e30
THRESHOLDS = (12, 16, 23, 32, 46, 64, 91)


def python_bucket(offset_value):
    magnitude = abs(offset_value)
    base_bucket = NB // 2 if offset_value > 0 else 0
    if magnitude < 8:
        return base_bucket + magnitude
    return base_bucket + 8 + sum((1 for edge_value in THRESHOLDS if magnitude >= edge_value))


def bucket_steps():
    first_bucket = python_bucket(-200)
    previous = first_bucket
    step_list = []
    for offset_value in range(-199, 201):
        current = python_bucket(offset_value)
        if current != previous:
            step_list.append((offset_value, previous, current))
            previous = current
    return (first_bucket, step_list)


def contract_rows(left, right):
    return lax.dot_general(
        left, right, (((0,), (0,)), ((), ())), preferred_element_type=jnp.float32
    )


def contract_cols(left, right):
    return lax.dot_general(
        left, right, (((1,), (1,)), ((), ())), preferred_element_type=jnp.float32
    )


def bias_block(column, offsets):
    first_bucket, step_list = bucket_steps()
    bias_values = jnp.zeros(offsets.shape, jnp.float32) + column[first_bucket]
    for start_offset, before, after in step_list:
        bias_values = bias_values + jnp.where(
            offsets >= start_offset, column[after] - column[before], 0.0
        )
    return bias_values


def bias_gradient(offsets, d_scores):
    first_bucket, step_list = bucket_steps()
    bucket_ids = lax.iota(jnp.int32, NB)
    d_column = jnp.where(bucket_ids == first_bucket, jnp.sum(d_scores), 0.0)
    for start_offset, before, after in step_list:
        above = jnp.sum(jnp.where(offsets >= start_offset, d_scores, 0.0))
        d_column = (
            d_column
            + jnp.where(bucket_ids == after, above, 0.0)
            - jnp.where(bucket_ids == before, above, 0.0)
        )
    return d_column


def block_scores(queries, key_rows, column, first_pos, live_keys):
    height, breadth = (queries.shape[0], key_rows.shape[0])
    offsets = (
        lax.iota(jnp.int32, breadth)[None, :] - (first_pos + lax.iota(jnp.int32, height))[:, None]
    )
    raw_scores = contract_cols(queries, key_rows)
    return (
        offsets,
        jnp.where(live_keys[None, :], raw_scores + bias_block(column, offsets), NEGATIVE),
    )


def block_forward(queries, key_rows, value_rows, column, first_pos, live_keys):
    offsets, scores = block_scores(queries, key_rows, column, first_pos, live_keys)
    row_max = jnp.max(scores, axis=1, keepdims=True)
    shifted_exp = jnp.exp(scores - row_max)
    totals = jnp.sum(shifted_exp, axis=1, keepdims=True)
    weights_low = (shifted_exp / totals).astype(jnp.bfloat16)
    context = jnp.dot(weights_low, value_rows, preferred_element_type=jnp.float32)
    return (context, (row_max + jnp.log(totals))[:, 0])


def block_backward(
    queries, key_rows, value_rows, d_context, log_total, column, first_pos, live_keys
):
    offsets, scores = block_scores(queries, key_rows, column, first_pos, live_keys)
    softmax_full = jnp.exp(scores - log_total[:, None])
    d_values = contract_rows(softmax_full.astype(jnp.bfloat16), d_context)
    d_probs = contract_cols(d_context, value_rows)
    row_dot = jnp.sum(softmax_full * d_probs, axis=1, keepdims=True)
    d_scores = (softmax_full * (d_probs - row_dot)).astype(jnp.bfloat16)
    d_queries = jnp.dot(d_scores, key_rows, preferred_element_type=jnp.float32)
    d_keys = contract_rows(d_scores, queries)
    d_column = bias_gradient(offsets, d_scores.astype(jnp.float32))
    return (d_queries, d_keys, d_values, d_column)


def continuation_rows(full_rows, cont_index):
    start_row = PLEN + cont_index * CLEN
    return jnp.concatenate([full_rows[:PLEN], full_rows[start_row : start_row + CLEN]], axis=0)


def live_mask(spans, cont_index):
    return lax.iota(jnp.int32, PLEN + CLEN) < PLEN + spans[cont_index]


def head_forward(queries, key_rows, value_rows, column, spans):
    prompt_live = jnp.ones((PLEN,), jnp.bool_)
    context, log_total = block_forward(
        queries[:PLEN], key_rows[:PLEN], value_rows[:PLEN], column, 0, prompt_live
    )
    contexts, log_totals = ([context], [log_total])
    for cont_index in range(CONT):
        start_row = PLEN + cont_index * CLEN
        context, log_total = block_forward(
            queries[start_row : start_row + CLEN],
            continuation_rows(key_rows, cont_index),
            continuation_rows(value_rows, cont_index),
            column,
            PLEN,
            live_mask(spans, cont_index),
        )
        contexts.append(context)
        log_totals.append(log_total)
    return (jnp.concatenate(contexts, axis=0), jnp.concatenate(log_totals, axis=0))


def head_backward(queries, key_rows, value_rows, d_context, log_total, column, spans):
    prompt_live = jnp.ones((PLEN,), jnp.bool_)
    d_query_p, d_key_p, d_value_p, d_column = block_backward(
        queries[:PLEN],
        key_rows[:PLEN],
        value_rows[:PLEN],
        d_context[:PLEN],
        log_total[:PLEN],
        column,
        0,
        prompt_live,
    )
    query_parts, key_parts, value_parts = ([d_query_p], [], [])
    for cont_index in range(CONT):
        start_row = PLEN + cont_index * CLEN
        d_query_c, d_key_c, d_value_c, d_column_c = block_backward(
            queries[start_row : start_row + CLEN],
            continuation_rows(key_rows, cont_index),
            continuation_rows(value_rows, cont_index),
            d_context[start_row : start_row + CLEN],
            log_total[start_row : start_row + CLEN],
            column,
            PLEN,
            live_mask(spans, cont_index),
        )
        query_parts.append(d_query_c)
        d_key_p = d_key_p + d_key_c[:PLEN]
        d_value_p = d_value_p + d_value_c[:PLEN]
        key_parts.append(d_key_c[PLEN:])
        value_parts.append(d_value_c[PLEN:])
        d_column = d_column + d_column_c
    return (
        jnp.concatenate(query_parts, axis=0),
        jnp.concatenate([d_key_p] + key_parts, axis=0),
        jnp.concatenate([d_value_p] + value_parts, axis=0),
        d_column,
    )


def heads_forward(queries, key_rows, value_rows, bias_cols, first_head, spans):
    local_heads = queries.shape[1] // DH

    def one_head(head_index, loop_state):
        contexts, log_totals = loop_state
        column_start = head_index * DH

        def take_head(source):
            return lax.dynamic_slice_in_dim(source, column_start, DH, 1)

        column = lax.dynamic_index_in_dim(bias_cols, first_head + head_index, 1, keepdims=False)
        context, log_total = head_forward(
            take_head(queries), take_head(key_rows), take_head(value_rows), column, spans
        )
        contexts = lax.dynamic_update_slice_in_dim(
            contexts, context.astype(jnp.bfloat16), column_start, 1
        )
        log_totals = lax.dynamic_update_slice_in_dim(log_totals, log_total[None, :], head_index, 0)
        return (contexts, log_totals)

    initial = (
        jnp.zeros(queries.shape, jnp.bfloat16),
        jnp.zeros((local_heads, queries.shape[0]), jnp.float32),
    )
    return lax.fori_loop(0, local_heads, one_head, initial)


def heads_backward(
    queries, key_rows, value_rows, d_context, log_totals, bias_cols, first_head, spans
):
    local_heads = queries.shape[1] // DH

    def one_head(head_index, loop_state):
        d_queries, d_keys, d_values, d_table = loop_state
        column_start = head_index * DH

        def take_head(source):
            return lax.dynamic_slice_in_dim(source, column_start, DH, 1)

        column = lax.dynamic_index_in_dim(bias_cols, first_head + head_index, 1, keepdims=False)
        log_total = lax.dynamic_index_in_dim(log_totals, head_index, 0, keepdims=False)
        head_grads = head_backward(
            take_head(queries),
            take_head(key_rows),
            take_head(value_rows),
            take_head(d_context),
            log_total,
            column,
            spans,
        )
        d_queries = lax.dynamic_update_slice_in_dim(
            d_queries, head_grads[0].astype(jnp.bfloat16), column_start, 1
        )
        d_keys = lax.dynamic_update_slice_in_dim(
            d_keys, head_grads[1].astype(jnp.bfloat16), column_start, 1
        )
        d_values = lax.dynamic_update_slice_in_dim(
            d_values, head_grads[2].astype(jnp.bfloat16), column_start, 1
        )
        d_table = lax.dynamic_update_slice_in_dim(d_table, head_grads[3][:, None], head_index, 1)
        return (d_queries, d_keys, d_values, d_table)

    initial = (
        jnp.zeros(queries.shape, jnp.bfloat16),
        jnp.zeros(queries.shape, jnp.bfloat16),
        jnp.zeros(queries.shape, jnp.bfloat16),
        jnp.zeros((NB, local_heads), jnp.float32),
    )
    return lax.fori_loop(0, local_heads, one_head, initial)


def norm_forward(inputs, gain):
    inverse = lax.rsqrt(jnp.mean(inputs * inputs, axis=1, keepdims=True) + EPSILON)
    return (inverse, (inputs * inverse * gain).astype(jnp.bfloat16))


def norm_backward(inputs, inverse, gain, d_normed):
    scaled = inputs * inverse
    d_gain = jnp.sum(d_normed * scaled, axis=0)
    d_scaled = d_normed * gain
    return (
        inverse * (d_scaled - scaled * jnp.mean(d_scaled * scaled, axis=1, keepdims=True)),
        d_gain,
    )


def local(
    tokens,
    teacher,
    lengths,
    w_query,
    w_key,
    w_value,
    w_out,
    w_in,
    w_ff,
    gain_attn,
    gain_ff,
    bias_table,
):
    inputs = tokens[0].astype(jnp.float32)
    targets = teacher[0].astype(jnp.float32)
    spans = lengths[0]
    gathered = (
        lax.all_gather(w_query, "wshard", axis=0, tiled=True),
        lax.all_gather(w_key, "wshard", axis=0, tiled=True),
        lax.all_gather(w_value, "wshard", axis=0, tiled=True),
        lax.all_gather(w_out, "wshard", axis=0, tiled=True),
        lax.all_gather(w_in, "wshard", axis=0, tiled=True),
        lax.all_gather(w_ff, "wshard", axis=0, tiled=True),
        lax.all_gather(gain_attn, "wshard", axis=0, tiled=True),
        lax.all_gather(gain_ff, "wshard", axis=0, tiled=True),
    )
    full_query, full_key, full_value, full_out, full_in, full_ff, full_gain1, full_gain2 = gathered
    inverse_one, normed_one = norm_forward(inputs, full_gain1.astype(jnp.float32))
    queries = jnp.dot(normed_one, full_query, preferred_element_type=jnp.float32).astype(
        jnp.bfloat16
    )
    key_rows = jnp.dot(normed_one, full_key, preferred_element_type=jnp.float32).astype(
        jnp.bfloat16
    )
    value_rows = jnp.dot(normed_one, full_value, preferred_element_type=jnp.float32).astype(
        jnp.bfloat16
    )
    head_queries, head_keys, head_values = (
        lax.all_to_all(queries, "seq", split_axis=1, concat_axis=0, tiled=True),
        lax.all_to_all(key_rows, "seq", split_axis=1, concat_axis=0, tiled=True),
        lax.all_to_all(value_rows, "seq", split_axis=1, concat_axis=0, tiled=True),
    )
    local_heads = head_queries.shape[1] // DH
    first_head = lax.axis_index("seq") * local_heads
    bias_cols = bias_table.astype(jnp.float32)
    head_context, log_totals = heads_forward(
        head_queries, head_keys, head_values, bias_cols, first_head, spans
    )
    context = lax.all_to_all(head_context, "seq", split_axis=0, concat_axis=1, tiled=True)
    middle = inputs + jnp.dot(context, full_out, preferred_element_type=jnp.float32)
    inverse_two, normed_two = norm_forward(middle, full_gain2.astype(jnp.float32))
    hidden_pre = jnp.dot(normed_two, full_in, preferred_element_type=jnp.float32)
    hidden_act = jnp.maximum(hidden_pre, 0.0).astype(jnp.bfloat16)
    final_rows = middle + jnp.dot(hidden_act, full_ff, preferred_element_type=jnp.float32)
    local_rows = inputs.shape[0]
    row_index = lax.axis_index("seq") * local_rows + lax.iota(jnp.int32, local_rows)
    slot_index = jnp.maximum(row_index - PLEN, 0)
    owner_match = (slot_index // CLEN)[:, None] == lax.iota(jnp.int32, CONT)[None, :]
    row_limit = jnp.sum(jnp.where(owner_match, spans[None, :], 0), axis=1)
    valid_rows = (row_index < PLEN) | (slot_index % CLEN < row_limit)
    row_count = PLEN + jnp.sum(spans).astype(jnp.float32)
    factor = (PLEN + CONT * CLEN) / row_count
    d_final = jnp.where(valid_rows[:, None], factor * (final_rows - targets), 0.0)
    full_query, full_key, full_value, full_out, full_in, full_ff, full_gain1, full_gain2 = (
        lax.all_gather(w_query, "wshard", axis=0, tiled=True),
        lax.all_gather(w_key, "wshard", axis=0, tiled=True),
        lax.all_gather(w_value, "wshard", axis=0, tiled=True),
        lax.all_gather(w_out, "wshard", axis=0, tiled=True),
        lax.all_gather(w_in, "wshard", axis=0, tiled=True),
        lax.all_gather(w_ff, "wshard", axis=0, tiled=True),
        lax.all_gather(gain_attn, "wshard", axis=0, tiled=True),
        lax.all_gather(gain_ff, "wshard", axis=0, tiled=True),
    )
    d_branch_two = d_final.astype(jnp.bfloat16)
    grad_ff = contract_rows(hidden_act, d_branch_two)
    d_hidden = contract_cols(d_branch_two, full_ff)
    d_pre = jnp.where(hidden_pre > 0, d_hidden, 0.0).astype(jnp.bfloat16)
    grad_in = contract_rows(normed_two, d_pre)
    d_middle, grad_gain2 = norm_backward(
        middle, inverse_two, full_gain2.astype(jnp.float32), contract_cols(d_pre, full_in)
    )
    d_middle = d_final + d_middle
    d_branch_one = d_middle.astype(jnp.bfloat16)
    grad_out = contract_rows(context, d_branch_one)
    d_context = contract_cols(d_branch_one, full_out).astype(jnp.bfloat16)
    head_d_context = lax.all_to_all(d_context, "seq", split_axis=1, concat_axis=0, tiled=True)
    head_d_query, head_d_key, head_d_value, d_bias_local = heads_backward(
        head_queries,
        head_keys,
        head_values,
        head_d_context,
        log_totals,
        bias_cols,
        first_head,
        spans,
    )
    d_queries, d_keys, d_values = (
        lax.all_to_all(head_d_query, "seq", split_axis=0, concat_axis=1, tiled=True),
        lax.all_to_all(head_d_key, "seq", split_axis=0, concat_axis=1, tiled=True),
        lax.all_to_all(head_d_value, "seq", split_axis=0, concat_axis=1, tiled=True),
    )
    grad_query = contract_rows(normed_one, d_queries)
    grad_key = contract_rows(normed_one, d_keys)
    grad_value = contract_rows(normed_one, d_values)
    d_normed_one = (
        contract_cols(d_queries, full_query)
        + contract_cols(d_keys, full_key)
        + contract_cols(d_values, full_value)
    )
    d_inputs, grad_gain1 = norm_backward(
        inputs, inverse_one, full_gain1.astype(jnp.float32), d_normed_one
    )
    d_tokens = d_middle + d_inputs
    shares = (
        lax.psum_scatter(grad_query, "wshard", scatter_dimension=0, tiled=True),
        lax.psum_scatter(grad_key, "wshard", scatter_dimension=0, tiled=True),
        lax.psum_scatter(grad_value, "wshard", scatter_dimension=0, tiled=True),
        lax.psum_scatter(grad_out, "wshard", scatter_dimension=0, tiled=True),
        lax.psum_scatter(grad_in, "wshard", scatter_dimension=0, tiled=True),
        lax.psum_scatter(grad_ff, "wshard", scatter_dimension=0, tiled=True),
        lax.psum_scatter(grad_gain1, "wshard", scatter_dimension=0, tiled=True),
        lax.psum_scatter(grad_gain2, "wshard", scatter_dimension=0, tiled=True),
    )
    summed = (
        lax.psum(shares[0].astype(jnp.bfloat16), "seq").astype(jnp.float32),
        lax.psum(shares[1].astype(jnp.bfloat16), "seq").astype(jnp.float32),
        lax.psum(shares[2].astype(jnp.bfloat16), "seq").astype(jnp.float32),
        lax.psum(shares[3].astype(jnp.bfloat16), "seq").astype(jnp.float32),
        lax.psum(shares[4].astype(jnp.bfloat16), "seq").astype(jnp.float32),
        lax.psum(shares[5].astype(jnp.bfloat16), "seq").astype(jnp.float32),
        lax.psum(shares[6].astype(jnp.bfloat16), "seq").astype(jnp.float32),
        lax.psum(shares[7].astype(jnp.bfloat16), "seq").astype(jnp.float32),
    )
    total_heads = bias_table.shape[1]
    d_bias_full = lax.dynamic_update_slice_in_dim(
        jnp.zeros((NB, total_heads), jnp.float32), d_bias_local, first_head, 1
    )
    bias_grad = lax.psum(d_bias_full, ("seq", "wshard"))
    return (
        final_rows.astype(jnp.bfloat16)[None],
        d_tokens[None],
        summed[0],
        summed[1],
        summed[2],
        summed[3],
        summed[4],
        summed[5],
        summed[6],
        summed[7],
        bias_grad,
    )


def solution(mesh):
    placed = (
        P("wshard", "seq", None),
        P("wshard", "seq", None),
        P("wshard", None),
        P("wshard", None),
        P("wshard", None),
        P("wshard", None),
        P("wshard", None),
        P("wshard", None),
        P("wshard", None),
        P("wshard"),
        P("wshard"),
        P(),
    )
    return jax.shard_map(
        local,
        mesh=mesh,
        in_specs=placed,
        out_specs=(
            P("wshard", "seq", None),
            P("wshard", "seq", None),
            P("wshard", None),
            P("wshard", None),
            P("wshard", None),
            P("wshard", None),
            P("wshard", None),
            P("wshard", None),
            P("wshard"),
            P("wshard"),
            P(),
        ),
        check_vma=False,
    )
```

profile of v0, /device:TPU:0, one launch (start us, length us, event | category | flops | bytes accessed | tf_op | source)
XLA Modules:
  0.0 2085.6 jit_solution(17480468597170808971)
XLA Ops:
  14.2 18.7 all-reduce.5
  42.4 16.8 all-gather.9.cloned.1.call-done
  67.1 16.4 all-gather.7.cloned.1.call-done
  110.7 360.4 %while.38 = (s32[]{:T(128)}, bf16[3072,192]{0,1:T(8,128)(2,1)}, f32[3,3072]{1,0:T(4,128)}, bf16[3072,192]{1,0:T(8,128)(2,1)}, bf16[3072,192]{1,0:T(8,128)(2,1)},...) while((s32[]{:T(128)}, bf16[3072,192]{0,1:T(8,128)(2,1)}, ...), condition=%wide.region_12.13_spmd, body=%wide.region_1.12_spmd.sunk | while | flops 1490488832 | bytes 67488528 | solution.py:204
  203.9 15.6 fusion.679
  321.0 15.4 fusion.679
  438.1 15.4 fusion.679
  564.9 1102.6 %while.39 = (s32[]{:T(128)}, bf16[3072,192]{0,1:T(8,128)(2,1)}, bf16[3072,192]{0,1:T(8,128)(2,1)}, bf16[3072,192]{0,1:T(8,128)(2,1)}, f32[32,3]{0,1:T(4,128)}, /...) while((s32[]{:T(128)}, bf16[3072,192]{0,1:T(8,128)(2,1)}, ...), condition=%wide.region_178.179_spmd, body=%wide.region_17.178_spmd.sunk | while | flops 3424083456 | bytes 214939120 | solution.py:248
  610.8 12.6 multiply_reduce_fusion.14
  664.2 110.6 %fusion.739 = (f32[]{:T(128)}, f32[]{:T(128)}, f32[]{:T(128)}, f32[]{:T(128)}, f32[]{:T(128)}, /*index=5*/f32[]{:T(128)}, f32[]{:T(128)}, f32[]{:T(128)}, f32[]{...) fusion(s32[512]{0:T(512)S(1)} %iota_add_fusion.6, ...), kind=kLoop, calls=%fused_computation.469.clone.1 | loop fusion | flops 228851712 | bytes 31468016 | tf_op jit(solution)/shard_map/while/body/eval_jaxpr/reduce_sum | solution.py:65
  786.2 15.7 multiply_reduce_fusion.13
  801.9 15.1 convert_reduce_fusion.6
  819.6 96.8 %subtract_add_fusion.2 = f32[32,1]{0,1:T(1,128)S(1)} fusion(f32[]{:T(128)} %get-tuple-element.1624, f32[]{:T(128)} %get-tuple-element.1625, f32[]{:T(128)} %get-tuple-element.1626, f32[]{:T(128)} %get-tuple-element.1627, f32[]{:T(128)} %get-tuple-element.1628, f32[]{:T(128)} %get-tuple-element.1629, f32[]{:T(128)} %get-tuple-element.1630, ...), kind=kLoop, calls=%fused_computation.647.clone.1 | loop fusion | flops 20480 | bytes 748 | tf_op jit(solution)/shard_map/while/body/eval_jaxpr/add | solution.py:171
  975.4 12.6 multiply_reduce_fusion.14
  990.5 12.2 multiply_reduce_fusion.15
  1028.8 110.6 %fusion.739 = (f32[]{:T(128)}, f32[]{:T(128)}, f32[]{:T(128)}, f32[]{:T(128)}, f32[]{:T(128)}, /*index=5*/f32[]{:T(128)}, f32[]{:T(128)}, f32[]{:T(128)}, f32[]{...) fusion(s32[512]{0:T(512)S(1)} %iota_add_fusion.6, ...), kind=kLoop, calls=%fused_computation.469.clone.1 | loop fusion | flops 228851712 | bytes 31468016 | tf_op jit(solution)/shard_map/while/body/eval_jaxpr/reduce_sum | solution.py:65
  1150.8 15.7 multiply_reduce_fusion.13
  1166.5 15.1 convert_reduce_fusion.6
  1184.3 96.8 %subtract_add_fusion.2 = f32[32,1]{0,1:T(1,128)S(1)} fusion(f32[]{:T(128)} %get-tuple-element.1624, f32[]{:T(128)} %get-tuple-element.1625, f32[]{:T(128)} %get-tuple-element.1626, f32[]{:T(128)} %get-tuple-element.1627, f32[]{:T(128)} %get-tuple-element.1628, f32[]{:T(128)} %get-tuple-element.1629, f32[]{:T(128)} %get-tuple-element.1630, ...), kind=kLoop, calls=%fused_computation.647.clone.1 | loop fusion | flops 20480 | bytes 748 | tf_op jit(solution)/shard_map/while/body/eval_jaxpr/add | solution.py:171
  1340.0 12.6 multiply_reduce_fusion.14
  1393.4 110.6 %fusion.739 = (f32[]{:T(128)}, f32[]{:T(128)}, f32[]{:T(128)}, f32[]{:T(128)}, f32[]{:T(128)}, /*index=5*/f32[]{:T(128)}, f32[]{:T(128)}, f32[]{:T(128)}, f32[]{...) fusion(s32[512]{0:T(512)S(1)} %iota_add_fusion.6, ...), kind=kLoop, calls=%fused_computation.469.clone.1 | loop fusion | flops 228851712 | bytes 31468016 | tf_op jit(solution)/shard_map/while/body/eval_jaxpr/reduce_sum | solution.py:65
  1515.4 15.7 multiply_reduce_fusion.13
  1531.1 15.1 convert_reduce_fusion.6
  1548.8 96.8 %subtract_add_fusion.2 = f32[32,1]{0,1:T(1,128)S(1)} fusion(f32[]{:T(128)} %get-tuple-element.1624, f32[]{:T(128)} %get-tuple-element.1625, f32[]{:T(128)} %get-tuple-element.1626, f32[]{:T(128)} %get-tuple-element.1627, f32[]{:T(128)} %get-tuple-element.1628, f32[]{:T(128)} %get-tuple-element.1629, f32[]{:T(128)} %get-tuple-element.1630, ...), kind=kLoop, calls=%fused_computation.647.clone.1 | loop fusion | flops 20480 | bytes 748 | tf_op jit(solution)/shard_map/while/body/eval_jaxpr/add | solution.py:171
  1669.0 17.4 all_to_all.152
  1689.3 16.0 all_to_all.153
  1709.1 14.9 all_to_all.154
  1751.0 39.4 %psum.71 = f32[32,12]{0,1:T(8,128)} all-reduce(f32[32,12]{0,1:T(8,128)S(1)} %dynamic_update_slice.57), channel_id=1, replica_groups=mesh['seq'=4,'wshard'=8] {'seq','wshard'}, use_global_device_ids=true, to_apply=%region_198.199 | all-reduce | flops 384 | bytes 3072 | tf_op jit(solution)/shard_map/psum | solution.py:404
  1801.3 99.2 %reduce-scatter.17.cloned.1.call-done = f32[384,768]{1,0:T(8,128)} async-done(((f32[3072,768]{1,0:T(8,128)}), f32[384,768]{1,0:T(8,128)}) %reduce-scatter.17.cloned.1.call-update) | async-done | bytes 1179664 | tf_op jit(solution)/shard_map/reduce_scatter | solution.py:386
  1902.7 97.9 %reduce-scatter.15.cloned.1.call-done = f32[96,3072]{1,0:T(8,128)} async-done(((f32[768,3072]{1,0:T(8,128)}), f32[96,3072]{1,0:T(8,128)}) %reduce-scatter.15.cloned.1.call-update) | async-done | bytes 1179664 | tf_op jit(solution)/shard_map/reduce_scatter | solution.py:385
  2010.0 14.6 all-reduce.4
  2046.4 22.4 %all-reduce.10.cloned.1.call-done = (bf16[96,768]{1,0:T(8,128)(2,1)}, bf16[96,768]{1,0:T(8,128)(2,1)}, bf16[96,768]{1,0:T(8,128)(2,1)}, bf16[96,768]{1,0:T(8,128...) async-done(((bf16[96,768]{1,0:T(8,128)(2,1)}, bf16[96,768]{1,0:T(8,128)(2,1)}, bf16[96,768]{1,0:T(8,128)(2,1)}, bf16[96,768]{1,0:T(8,128)(2,1)}, ...) | async-done | bytes 1769488 | tf_op jit(solution)/shard_map/psum | solution.py:391
  (568 shorter events, 635.0 us)
Async XLA Ops:
  7.2 28.0 %all-gather.11.cloned.1.call-start = ((), (), s32[]{:S(2)}) async-start(), calls=%async_computation.16 | async-start | bytes 1327104 | tf_op jit(solution)/shard_map/all_gather | solution.py:286
  7.9 51.3 %all-gather.9.cloned.1.call-start = ((), (), s32[]{:S(2)}) async-start(), calls=%async_computation.15 | async-start | bytes 1327104 | tf_op jit(solution)/shard_map/all_gather | solution.py:285
  8.7 74.8 %all-gather.7.cloned.1.call-start = ((), (), s32[]{:S(2)}) async-start(), calls=%async_computation.14 | async-start | bytes 1327104 | tf_op jit(solution)/shard_map/all_gather | solution.py:284
  9.4 472.3 %all-gather.13.cloned.1.call-start = ((), (), s32[]{:S(2)}) async-start(), calls=%async_computation.17 | async-start | bytes 1327104 | tf_op jit(solution)/shard_map/all_gather | solution.py:287
  10.0 487.0 %all-gather.15.cloned.1.call-start = ((), (), s32[]{:S(2)}) async-start(), calls=%async_computation.18 | async-start | bytes 5308416 | tf_op jit(solution)/shard_map/all_gather | solution.py:288
  33.0 50.4 %copy-start.50 = (f32[768]{0:T(1024)}, f32[768]{0:T(1024)S(1)}, u32[]{:S(2)}) copy-start(f32[768]{0:T(1024)S(1)} %convert_element_type.329) | copy-start | bytes 9220
  34.6 48.9 %copy-start.16 = (bf16[1,768,768]{1,2,0:T(8,128)(2,1)}, bf16[1,768,768]{1,2,0:T(8,128)(2,1)S(1)}, u32[]{:S(2)}) copy-start(bf16[1,768,768]{1,2,0:T(8,128)(2,1)S(1)} %copy.87) | copy-start | bytes 3538948
  34.9 48.5 %copy-start.52 = (f32[768]{0:T(1024)}, f32[768]{0:T(1024)S(1)}, u32[]{:S(2)}) copy-start(f32[768]{0:T(1024)S(1)} %add_rsqrt_fusion.1) | copy-start | bytes 9220
  38.7 24.0 %all-to-all-start.2 = ((bf16[768,4,192]{0,2,1:T(8,128)(2,1)}), bf16[768,4,192]{0,2,1:T(8,128)(2,1)S(1)}, u32[]{:S(2)}, u32[]{:S(2)}) async-start(bf16[768,4,192]{0,2,1:T(8,128)(2,1)} %bitcast.383), calls=%async_computation.2 | async-start | bytes 2359296 | tf_op jit(solution)/shard_map/all_to_all | solution.py:307
  62.7 24.2 %all-to-all-start.1 = ((bf16[768,4,192]{0,2,1:T(8,128)(2,1)}), bf16[768,4,192]{0,2,1:T(8,128)(2,1)}, u32[]{:S(2)}, u32[]{:S(2)}) async-start(bf16[768,4,192]{0,2,1:T(8,128)(2,1)} %bitcast.382), calls=%async_computation.1 | async-start | bytes 2359296 | tf_op jit(solution)/shard_map/all_to_all | solution.py:306
  87.0 20.1 all-to-all-start
  91.2 416.5 %all-gather.17.cloned.1.call-start = ((), (), s32[]{:S(2)}) async-start(), calls=%async_computation.19 | async-start | bytes 5308416 | tf_op jit(solution)/shard_map/all_gather | solution.py:289
  110.9 55.3 %copy-start.8 = (bf16[3072,192]{1,0:T(8,128)(2,1)}, bf16[3072,192]{1,0:T(8,128)(2,1)S(1)}, u32[]{:S(2)}) copy-start(bf16[3072,192]{1,0:T(8,128)(2,1)S(1)} %get-tuple-element.1828) | copy-start | bytes 3538948 | tf_op jit(solution)/shard_map/while
  228.0 55.2 %copy-start.8 = (bf16[3072,192]{1,0:T(8,128)(2,1)}, bf16[3072,192]{1,0:T(8,128)(2,1)S(1)}, u32[]{:S(2)}) copy-start(bf16[3072,192]{1,0:T(8,128)(2,1)S(1)} %get-tuple-element.1828) | copy-start | bytes 3538948 | tf_op jit(solution)/shard_map/while
  345.2 55.2 %copy-start.8 = (bf16[3072,192]{1,0:T(8,128)(2,1)}, bf16[3072,192]{1,0:T(8,128)(2,1)S(1)}, u32[]{:S(2)}) copy-start(bf16[3072,192]{1,0:T(8,128)(2,1)S(1)} %get-tuple-element.1828) | copy-start | bytes 3538948 | tf_op jit(solution)/shard_map/while
  473.5 19.2 all-to-all-start.3
  479.1 57.1 %copy-start.46 = (f32[768]{0:T(1024)}, f32[768]{0:T(1024)S(1)}, u32[]{:S(2)}) copy-start(f32[768]{0:T(1024)S(1)} %convert_element_type.335) | copy-start | bytes 9220
  497.0 39.3 %copy-start.48 = (f32[768]{0:T(1024)}, f32[768]{0:T(1024)S(1)}, u32[]{:S(2)}) copy-start(f32[768]{0:T(1024)S(1)} %add_rsqrt_fusion) | copy-start | bytes 9220
  541.9 18.0 all-to-all-start.4
  545.4 1245.0 %reduce-scatter.13.cloned.1.call-start = ((), (), s32[]{:S(2)}) async-start(), calls=%async_computation.23 | async-start | bytes 2654208 | tf_op jit(solution)/shard_map/reduce_scatter | solution.py:384
  550.1 1242.0 %reduce-scatter.7.cloned.1.call-start = ((), (), s32[]{:S(2)}) async-start(), calls=%async_computation.20 | async-start | bytes 2654208 | tf_op jit(solution)/shard_map/reduce_scatter | solution.py:381
  565.1 219.3 %copy-start.10 = (bf16[3072,192]{1,0:T(8,128)(2,1)}, bf16[3072,192]{1,0:T(8,128)(2,1)S(1)}, u32[]{:S(2)}) copy-start(bf16[3072,192]{1,0:T(8,128)(2,1)S(1)} %get-tuple-element.1903) | copy-start | bytes 3538948 | tf_op jit(solution)/shard_map/while
  929.7 219.3 %copy-start.10 = (bf16[3072,192]{1,0:T(8,128)(2,1)}, bf16[3072,192]{1,0:T(8,128)(2,1)S(1)}, u32[]{:S(2)}) copy-start(bf16[3072,192]{1,0:T(8,128)(2,1)S(1)} %get-tuple-element.1903) | copy-start | bytes 3538948 | tf_op jit(solution)/shard_map/while
  1294.3 219.3 %copy-start.10 = (bf16[3072,192]{1,0:T(8,128)(2,1)}, bf16[3072,192]{1,0:T(8,128)(2,1)S(1)}, u32[]{:S(2)}) copy-start(bf16[3072,192]{1,0:T(8,128)(2,1)S(1)} %get-tuple-element.1903) | copy-start | bytes 3538948 | tf_op jit(solution)/shard_map/while
  1338.3 29.5 %copy-start.25 = (bf16[512,64]{1,0:T(8,128)(2,1)}, bf16[512,64]{1,0:T(8,128)(2,1)S(1)}, u32[]{:S(2)}) copy-start(bf16[512,64]{1,0:T(8,128)(2,1)S(1)} %get-tuple-element.1612) | copy-start | bytes 196612 | tf_op jit(solution)/shard_map/while
  1689.1 104.5 %reduce-scatter.9.cloned.1.call-start = ((), (), s32[]{:S(2)}) async-start(), calls=%async_computation.21 | async-start | bytes 2654208 | tf_op jit(solution)/shard_map/reduce_scatter | solution.py:382
  1708.9 90.8 %reduce-scatter.11.cloned.1.call-start = ((), (), s32[]{:S(2)}) async-start(), calls=%async_computation.22 | async-start | bytes 2654208 | tf_op jit(solution)/shard_map/reduce_scatter | solution.py:383
  1727.6 173.0 %reduce-scatter.17.cloned.1.call-start = ((), (), s32[]{:S(2)}) async-start(), calls=%async_computation.25 | async-start | bytes 10616832 | tf_op jit(solution)/shard_map/reduce_scatter | solution.py:386
  1737.7 262.9 %reduce-scatter.15.cloned.1.call-start = ((), (), s32[]{:S(2)}) async-start(), calls=%async_computation.24 | async-start | bytes 10616832 | tf_op jit(solution)/shard_map/reduce_scatter | solution.py:385
  1748.2 320.6 %all-reduce.10.cloned.1.call-start = ((), (), s32[]{:S(2)}) async-start(), calls=%async_computation.26 | async-start | bytes 3538944 | tf_op jit(solution)/shard_map/psum | solution.py:391
  1793.7 209.1 %copy-start.41 = (bf16[4,768,192]{1,2,0:T(8,128)(2,1)S(1)}, bf16[4,768,192]{1,2,0:T(8,128)(2,1)}, u32[]{:S(2)}) copy-start(bf16[4,768,192]{1,2,0:T(8,128)(2,1)} %copy-done.40) | copy-start | bytes 3538948
  2007.0 32.6 %copy-start.15 = (f32[768,768]{0,1:T(8,128)S(1)}, f32[768,768]{0,1:T(8,128)}, u32[]{:S(2)}) copy-start(f32[768,768]{0,1:T(8,128)} %copy-done.14) | copy-start | bytes 7077892
  (100 other events, 652.7 us)
Sparse Core Ops, SparseCore 0:
  9.7 25.5 all-gather.10
  36.9 22.3 all-gather.8
  60.8 22.5 all-gather.6
  84.9 22.2 all-gather.12
  108.7 51.1 all-gather.14
  161.4 50.5 all-gather.16
  550.2 36.2 reduce-scatter.12
  1689.3 34.5 reduce-scatter.6
  1726.2 35.3 reduce-scatter.8
  1763.7 35.9 reduce-scatter.10
  1802.0 98.5 reduce-scatter.16
  1902.7 97.8 reduce-scatter.14
  2005.0 63.7 all-reduce.9
where the time goes:
time: 2100 us; the launch traced here: 2090 us
  other arithmetic  707 us (34%)
  matrix products  565 us (27%)
  waiting for transfers between devices  290 us (14%)
  loops' own time  246 us (12%)
  blocking collectives  132 us (6%)
  local copies, waits for them, and re-layouts  105 us (5%)
    dot_general x51, matrix products, contract_cols(): lax.dot_general(left, right, (((1,), (1,)), ((), ())), preferred_element_...  423 us
    reduce_sum x3, other arithmetic, bias_gradient(): above = jnp.sum(jnp.where(offsets >= start_offset, d_scores, 0.0))  332 us
    add x3, other arithmetic, head_backward(): d_column = d_column + d_column_c  290 us
    another operation x1, loops' own time, heads_backward(): return lax.fori_loop(0, local_heads, one_head, initial)  123 us
    another operation x1, loops' own time, heads_forward(): return lax.fori_loop(0, local_heads, one_head, initial)  123 us
    reduce_scatter x1, waiting for transfers between devices, local(): lax.psum_scatter(grad_ff, 'wshard', scatter_dimension=0, tiled=True)  99.2 us
    reduce_scatter x1, waiting for transfers between devices, local(): lax.psum_scatter(grad_in, 'wshard', scatter_dimension=0, tiled=True)  97.9 us
    dot_general x36, matrix products, contract_rows(): lax.dot_general(left, right, (((0,), (0,)), ((), ())), preferred_element_...  79 us
  transfers between devices with their start and end apart: 18, of which 10 were waited for; matrix products, arithmetic and copies ran while one was open for 63% of the time, Pallas kernels for 0%

commit v1 on v0

v1 whole, which is shorter than its diff:
```python
import jax
import jax.numpy as jnp
import numpy as np
from jax import lax
from jax.experimental import pallas as pl
from jax.experimental.pallas import tpu as pltpu
from jax.sharding import PartitionSpec as P

DH = 64
NB = 32
PLEN = 1024
CLEN = 512
CONT = 4
QB = 256
NQ = 3
ROWS = QB * NQ
KROWS = PLEN + 2 * CLEN
TILE = 128
NEGATIVE = -1e30
f32 = jnp.float32
bf16 = jnp.bfloat16


def dot_nt(a, b):
    return lax.dot_general(a, b, (((1,), (1,)), ((), ())), preferred_element_type=f32)


def dot_nn(a, b):
    return lax.dot_general(a, b, (((1,), (0,)), ((), ())), preferred_element_type=f32)


def low_lanes(shape):
    return lax.broadcasted_iota(jnp.int32, shape, 1) < DH


def add_bias(s, bias_ref, head, kc, qc):
    rows = []
    for a in range(s.shape[0] // TILE):
        cols = []
        for b in range(s.shape[1] // TILE):
            d = jnp.clip(kc + a - qc[b], -2, 2) + 2
            cols.append(bias_ref[head, pl.ds(pl.multiple_of(d * TILE, TILE), TILE), :])
        rows.append(jnp.concatenate(cols, axis=1))
    return s + jnp.concatenate(rows, axis=0)


def forward_kernel(meta, q_ref, k_ref, v_ref, qaug_ref, kaug_ref, bias_ref, ctx_ref, rest_ref, lse_ref,
                   k_scr, vt_scr, s_scr):
    low_k = low_lanes((KROWS, TILE))
    low_q = low_lanes((QB, TILE))
    k_scr[0] = jnp.where(low_k, k_ref[...], kaug_ref[...])
    k_scr[1] = jnp.where(low_k, kaug_ref[...], k_ref[...])
    vt_scr[...] = v_ref[...].T
    KC = 512
    for qb in range(NQ):
        qc = meta[qb]
        slot = pl.multiple_of(PLEN + meta[NQ + qb] * CLEN, CLEN)
        q = q_ref[qb * QB:(qb + 1) * QB, :]
        qa = qaug_ref[qb * QB:(qb + 1) * QB, :]
        outs = []
        for h in range(2):
            qh = jnp.where(low_q, q, qa) if h == 0 else jnp.where(low_q, qa, q)
            m = None
            for c in range(3):
                kk = k_scr[h, c * KC:(c + 1) * KC, :] if c < 2 else k_scr[h, pl.ds(slot, KC), :]
                s = dot_nt(kk, qh)
                s = add_bias(s, bias_ref, h, 4 * c, (qc, qc + 1))
                s_scr[h, c * KC:(c + 1) * KC, :] = s
                mc = jnp.max(s, axis=0, keepdims=True)
                m = mc if m is None else jnp.maximum(m, mc)
            l = None
            acc = None
            for c in range(3):
                p = jnp.exp(s_scr[h, c * KC:(c + 1) * KC, :] - m)
                lc = jnp.sum(p, axis=0, keepdims=True)
                l = lc if l is None else l + lc
                vv = (vt_scr[h * DH:(h + 1) * DH, c * KC:(c + 1) * KC] if c < 2
                      else vt_scr[h * DH:(h + 1) * DH, pl.ds(slot, KC)])
                o = dot_nn(vv, p.astype(bf16))
                acc = o if acc is None else acc + o
            outs.append(acc / l)
            lse_ref[0, h:h + 1, qb * QB:(qb + 1) * QB] = m + jnp.log(l)
        ctx = jnp.concatenate(outs, axis=0).T
        ctx_low = ctx.astype(bf16)
        ctx_ref[qb * QB:(qb + 1) * QB, :] = ctx_low
        rest_ref[qb * QB:(qb + 1) * QB, :] = (ctx - ctx_low.astype(f32)).astype(bf16)


def attention_forward(meta, q, kv, qaug, kaug, bias):
    pairs = q.shape[1] // TILE
    spec = lambda rows, first=0: pl.BlockSpec((rows, TILE), lambda i, meta: (0, first + i))
    fixed = lambda rows: pl.BlockSpec((rows, TILE), lambda i, meta: (0, 0))
    return pl.pallas_call(
        forward_kernel,
        grid_spec=pltpu.PrefetchScalarGridSpec(
            num_scalar_prefetch=1,
            grid=(pairs,),
            in_specs=[spec(ROWS), spec(KROWS), spec(KROWS, pairs), fixed(ROWS), fixed(KROWS),
                      pl.BlockSpec((2, 5 * TILE, TILE), lambda i, meta: (i, 0, 0))],
            out_specs=[spec(ROWS), spec(ROWS), pl.BlockSpec((1, 2, ROWS), lambda i, meta: (i, 0, 0))],
            scratch_shapes=[
                pltpu.VMEM((2, KROWS, TILE), bf16),
                pltpu.VMEM((TILE, KROWS), bf16),
                pltpu.VMEM((2, PLEN + CLEN, QB), f32),
            ],
        ),
        out_shape=[jax.ShapeDtypeStruct((ROWS, pairs * TILE), bf16),
                   jax.ShapeDtypeStruct((ROWS, pairs * TILE), bf16),
                   jax.ShapeDtypeStruct((pairs, 2, ROWS), f32)],
        compiler_params=pltpu.CompilerParams(dimension_semantics=("arbitrary",),
                                             vmem_limit_bytes=56 << 20),
        name="attention_forward",
    )(meta, q, kv, kv, qaug, kaug, bias)


PAD = TILE


def fold_rows(rows):
    return jnp.sum(rows.reshape(rows.shape[0] // 8, 8, rows.shape[1]), axis=0)


def backward_kernel(meta, q_ref, k_ref, v_ref, do_ref, ctx_ref, rest_ref, lse_ref, qaug_ref, kaug_ref,
                    bias_ref, pick_ref, dq_ref, dk_ref, dv_ref, near_ref,
                    k_scr, kt_scr, q_scr, do_scr, delta_scr, ds_scr, dks_scr, dvs_scr, far_scr):
    low_k = low_lanes((KROWS, TILE))
    low_q = low_lanes((ROWS, TILE))
    k_scr[0] = jnp.where(low_k, k_ref[...], kaug_ref[...])
    k_scr[1] = jnp.where(low_k, kaug_ref[...], k_ref[...])
    kt_scr[...] = k_ref[...].T
    q_scr[0] = jnp.where(low_q, q_ref[...], qaug_ref[...])
    q_scr[1] = jnp.where(low_q, qaug_ref[...], q_ref[...])
    zero = jnp.zeros((ROWS, TILE), bf16)
    do_scr[0] = jnp.where(low_q, do_ref[...], zero)
    do_scr[1] = jnp.where(low_q, zero, do_ref[...])
    prod = do_ref[...].astype(f32) * (ctx_ref[...].astype(f32) + rest_ref[...].astype(f32))
    hi = prod.astype(bf16)
    lo = (prod - hi.astype(f32)).astype(bf16)
    pick_row = lax.broadcasted_iota(jnp.int32, (8, TILE), 0)
    pick_low = low_lanes((8, TILE))
    pick = jnp.where((pick_row == 0) & pick_low | (pick_row == 1) & ~pick_low, 1.0, 0.0).astype(bf16)
    delta_scr[...] = dot_nt(pick, hi) + dot_nt(pick, lo)
    for h in range(2):
        ds_scr[h, 0:PAD, :] = jnp.zeros((PAD, ROWS), bf16)
        ds_scr[h, PAD + PLEN + CLEN:, :] = jnp.zeros((PAD, ROWS), bf16)

    def piece(h, kk, vv, kc, qb):
        cols = slice(qb * QB, (qb + 1) * QB)
        s = dot_nt(kk, q_scr[h, cols, :])
        qc = meta[qb]
        s = add_bias(s, bias_ref, h, kc, (qc, qc + 1))
        p = jnp.exp(s - lse_ref[0, h:h + 1, cols])
        dp = dot_nt(vv, do_scr[h, cols, :])
        ds = (p * (dp - delta_scr[h:h + 1, cols])).astype(bf16)
        return p.astype(bf16), ds

    low_c = low_lanes((QB, TILE))

    def prompt_chunk(c, carry):
        start = pl.multiple_of(c * QB, QB)
        dv = None
        dks = []
        for h in range(2):
            kk = k_scr[h, pl.ds(start, QB), :]
            vv = v_ref[pl.ds(start, QB), :]
            dk = None
            for qb in range(NQ):
                cols = slice(qb * QB, (qb + 1) * QB)
                p, ds = piece(h, kk, vv, 2 * c, qb)
                ds_scr[h, pl.ds(PAD + start, QB), cols] = ds
                a = dot_nn(p, do_scr[h, cols, :])
                b = dot_nn(ds, q_scr[h, cols, :])
                dv = a if dv is None else dv + a
                dk = b if dk is None else dk + b
            dks.append(dk)
        dv_ref[pl.ds(start, QB), :] = dv.astype(bf16)
        dk_ref[pl.ds(start, QB), :] = jnp.where(low_c, dks[0], dks[1]).astype(bf16)
        sums = jnp.where(low_c, dks[1], dks[0])
        far_scr[2 * c] = fold_rows(sums[:TILE])
        far_scr[2 * c + 1] = fold_rows(sums[TILE:])
        return carry

    lax.fori_loop(0, PLEN // QB, prompt_chunk, 0)
    dvs_scr[...] = jnp.zeros_like(dvs_scr)
    dks_scr[...] = jnp.zeros_like(dks_scr)
    for qb in range(NQ):
        cols = slice(qb * QB, (qb + 1) * QB)
        slot = pl.multiple_of(meta[NQ + qb] * CLEN, CLEN)
        for half in range(CLEN // QB):
            start = pl.multiple_of(slot + half * QB, QB)
            dv = None
            for h in range(2):
                kk = k_scr[h, pl.ds(PLEN + start, QB), :]
                vv = v_ref[pl.ds(PLEN + start, QB), :]
                p, ds = piece(h, kk, vv, 8 + 2 * half, qb)
                ds_scr[h, PAD + PLEN + half * QB:PAD + PLEN + (half + 1) * QB, cols] = ds
                a = dot_nn(p, do_scr[h, cols, :])
                dv = a if dv is None else dv + a
                dks_scr[h, pl.ds(start, QB), :] += dot_nn(ds, q_scr[h, cols, :])
            dvs_scr[pl.ds(start, QB), :] += dv
    dv_ref[PLEN:, :] = dvs_scr[...].astype(bf16)
    low_s = low_lanes((2 * CLEN, TILE))
    dk_ref[PLEN:, :] = jnp.where(low_s, dks_scr[0], dks_scr[1]).astype(bf16)
    sums = jnp.where(low_s, dks_scr[1], dks_scr[0])
    for t in range(2 * CLEN // TILE):
        far_scr[8 + t] = fold_rows(sums[t * TILE:(t + 1) * TILE])

    dqt = []
    for h in range(2):
        parts = []
        for qb in range(NQ):
            cols = slice(qb * QB, (qb + 1) * QB)
            slot = pl.multiple_of(PLEN + meta[NQ + qb] * CLEN, CLEN)
            rows = slice(h * DH, (h + 1) * DH)
            a = dot_nn(kt_scr[rows, 0:PLEN], ds_scr[h, PAD:PAD + PLEN, cols])
            b = dot_nn(kt_scr[rows, pl.ds(slot, CLEN)], ds_scr[h, PAD + PLEN:PAD + PLEN + CLEN, cols])
            parts.append(a + b)
        dqt.append(jnp.concatenate(parts, axis=1))
    dq_ref[...] = jnp.concatenate(dqt, axis=0).T.astype(bf16)

    row_id = lax.broadcasted_iota(jnp.int32, (TILE, TILE), 0)
    lane_id = lax.broadcasted_iota(jnp.int32, (TILE, TILE), 1)
    flip = jnp.where(row_id + lane_id == TILE - 1, 1.0, 0.0).astype(bf16)
    for h in range(2):
        acc = None
        for sub in range(2 * NQ):
            qc = meta[sub // 2] + sub % 2
            start = pl.multiple_of(qc * TILE, TILE)
            part = ds_scr[h, pl.ds(start, 3 * TILE), sub * TILE:(sub + 1) * TILE].astype(f32)
            acc = part if acc is None else acc + part
        top = acc.astype(bf16)
        acc = dot_nn(top, flip) + dot_nn((acc - top.astype(f32)).astype(bf16), flip)
        sums = []
        for d in range(3):
            rolled = pltpu.roll(acc[d * TILE:(d + 1) * TILE], 0, 1, stride=1, stride_axis=0)
            wrapped = jnp.where(lane_id < row_id, rolled, 0.0)
            sums += [fold_rows(rolled), fold_rows(wrapped)]
        for side in range(2):
            total = None
            for t in range(16):
                term = far_scr[t] * pick_ref[h, side, t]
                total = term if total is None else total + term
            sums.append(total)
        for i, eight in enumerate(sums):
            near_ref[0, h, i] = eight


def attention_backward(meta, q, kv, do, ctx, rest, lse, qaug, kaug, bias, pick):
    pairs = q.shape[1] // TILE
    spec = lambda rows, first=0: pl.BlockSpec((rows, TILE), lambda i, meta: (0, first + i))
    fixed = lambda rows: pl.BlockSpec((rows, TILE), lambda i, meta: (0, 0))
    width = pairs * TILE
    return pl.pallas_call(
        backward_kernel,
        grid_spec=pltpu.PrefetchScalarGridSpec(
            num_scalar_prefetch=1,
            grid=(pairs,),
            in_specs=[spec(ROWS), spec(KROWS), spec(KROWS, pairs), spec(ROWS), spec(ROWS), spec(ROWS),
                      pl.BlockSpec((1, 2, ROWS), lambda i, meta: (i, 0, 0)),
                      fixed(ROWS), fixed(KROWS),
                      pl.BlockSpec((2, 5 * TILE, TILE), lambda i, meta: (i, 0, 0)),
                      pl.BlockSpec((2, 2, 16, 8, TILE), lambda i, meta: (0, 0, 0, 0, 0))],
            out_specs=[spec(ROWS), spec(KROWS), spec(KROWS),
                       pl.BlockSpec((1, 2, 8, 8, TILE), lambda i, meta: (i, 0, 0, 0, 0))],
            scratch_shapes=[
                pltpu.VMEM((2, KROWS, TILE), bf16),
                pltpu.VMEM((TILE, KROWS), bf16),
                pltpu.VMEM((2, ROWS, TILE), bf16),
                pltpu.VMEM((2, ROWS, TILE), bf16),
                pltpu.VMEM((8, ROWS), f32),
                pltpu.VMEM((2, PLEN + CLEN + 2 * PAD, ROWS), bf16),
                pltpu.VMEM((2, 2 * CLEN, TILE), f32),
                pltpu.VMEM((2 * CLEN, TILE), f32),
                pltpu.VMEM((16, 8, TILE), f32),
            ],
        ),
        out_shape=[jax.ShapeDtypeStruct((ROWS, width), bf16),
                   jax.ShapeDtypeStruct((KROWS, width), bf16),
                   jax.ShapeDtypeStruct((KROWS, width), bf16),
                   jax.ShapeDtypeStruct((pairs, 2, 8, 8, TILE), f32)],
        compiler_params=pltpu.CompilerParams(dimension_semantics=("arbitrary",),
                                             vmem_limit_bytes=60 << 20),
        name="attention_backward",
    )(meta, q, kv, kv, do, ctx, rest, lse, qaug, kaug, bias, pick)


EPSILON = 1e-06
THRESHOLDS = (12, 16, 23, 32, 46, 64, 91)
OWNER_BLOCK = (0, 3, 1, 2)


def python_bucket(offset):
    magnitude = abs(offset)
    base = NB // 2 if offset > 0 else 0
    if magnitude < 8:
        return base + magnitude
    return base + 8 + sum(1 for edge in THRESHOLDS if magnitude >= edge)


def bias_tiles(table):
    shape = (5, TILE, TILE)
    offset = (TILE * (lax.broadcasted_iota(jnp.int32, shape, 0) - 2)
              + lax.broadcasted_iota(jnp.int32, shape, 1) - lax.broadcasted_iota(jnp.int32, shape, 2))
    columns = table.astype(f32).T[:, :, None, None, None]
    previous = python_bucket(-200)
    tiles = jnp.broadcast_to(columns[:, previous], (table.shape[1],) + shape)
    for n in range(-199, 201):
        current = python_bucket(n)
        if current != previous:
            tiles = jnp.where(offset >= n, columns[:, current], tiles)
            previous = current
    return tiles.reshape(table.shape[1], 5 * TILE, TILE)


def bias_spread():
    spread = np.zeros((8, TILE, NB), np.float32)
    for lane in range(TILE):
        for d in range(3):
            inside = python_bucket(TILE * (d - 1) + lane - (TILE - 1))
            passed = python_bucket(TILE * d + lane - (TILE - 1))
            spread[2 * d, lane, inside] += 1
            spread[2 * d + 1, lane, passed] += 1
            spread[2 * d + 1, lane, inside] -= 1
    spread[6, :, python_bucket(-200)] = 1
    spread[7, :, python_bucket(200)] = 1
    return spread.reshape(8 * TILE, NB)


def placement(me, spans):
    block = NQ * me + jnp.arange(NQ, dtype=jnp.int32)
    prompt = block < PLEN // QB
    cont = jnp.maximum(block - PLEN // QB, 0) // 2
    half = jnp.maximum(block - PLEN // QB, 0) % 2
    tile = jnp.where(prompt, 2 * block, PLEN // TILE + 2 * half)
    slot = jnp.where(prompt, 0, cont - (me - 1))
    chosen = cont[:, None] == jnp.arange(CONT, dtype=jnp.int32)[None, :]
    limit = jnp.where(prompt, 0, jnp.sum(jnp.where(chosen, spans[None, :], 0), axis=1))
    meta = jnp.concatenate([tile, slot]).astype(jnp.int32)
    shape = (KROWS, TILE)
    key = lax.broadcasted_iota(jnp.int32, shape, 0)
    sub = lax.broadcasted_iota(jnp.int32, shape, 1) % DH
    kaug = jnp.zeros(shape, f32)
    for q in range(NQ):
        first = PLEN + CLEN * slot[q]
        seen = (key < PLEN) | ((key >= first) & (key < first + limit[q]))
        kaug = jnp.where((sub // 2 == q) & ~seen, NEGATIVE, kaug)
    shape = (ROWS, TILE)
    qaug = lax.broadcasted_iota(jnp.int32, shape, 1) % DH == lax.broadcasted_iota(jnp.int32, shape, 0) // TILE
    shape = (2, 2, 16, 8, TILE)
    head, side, row, lane = (lax.broadcasted_iota(jnp.int32, shape, a) for a in (0, 1, 2, 4))
    sub = lane - jnp.where(head == 0, DH, 0)
    key_tile = jnp.where(row < 8, row, 8 + (row - 8) % 4)
    query_tile = jnp.full(shape, -1000, jnp.int32)
    for q in range(2 * NQ):
        query_tile = jnp.where(sub == q, tile[q // 2] + q % 2, query_tile)
    apart = key_tile - query_tile
    far = jnp.where(side == 0, apart <= -2, (apart >= 2) & (apart < 100))
    return meta, qaug.astype(bf16), kaug.astype(bf16), far.astype(f32)


def rms(rows):
    return lax.rsqrt(jnp.mean(rows * rows, axis=1, keepdims=True) + EPSILON)


def normed_rows(rows, gain):
    rows = rows.astype(f32)
    return (rows * rms(rows) * gain).astype(bf16)


def norm_backward(inputs, inverse, gain, d_normed):
    scaled = inputs * inverse
    d_gain = jnp.sum(d_normed * scaled, axis=0)
    d_scaled = d_normed * gain
    return (inverse * (d_scaled - scaled * jnp.mean(d_scaled * scaled, axis=1, keepdims=True)), d_gain)


def contract_rows(left, right):
    return lax.dot_general(left, right, (((0,), (0,)), ((), ())), preferred_element_type=f32)


def block_of(rows, i):
    return rows[i * QB:(i + 1) * QB]


def send(rows, pairs):
    return lax.ppermute(rows, "seq", pairs)


def pick_by(me, *choices):
    out = choices[-1]
    for i in range(len(choices) - 2, -1, -1):
        out = jnp.where(me == i, choices[i], out)
    return out


def gather_rows(me, own):
    mine = [block_of(own, i) for i in range(NQ)]
    pair = pick_by(me, mine[0], mine[0], mine[2], mine[0])
    cross = send(pair, [(1, 0), (2, 3), (3, 2)])
    down = [send(mine[i], [(0, 1)]) for i in range(NQ)]
    side = [send(pick_by(me, mine[i], mine[0], mine[i], mine[i]), [(0, 2)] + ([(1, 3)] if i == 0 else []))
            for i in range(NQ)]
    last = side[0]
    prompt = []
    first_relay = send(down[0], [(1, 3)])
    second_relay = send(side[1], [(2, 3)])
    half = QB // 2
    third_a = send(down[2][:half], [(1, 3)])
    third_b = send(side[2][half:], [(2, 3)])
    fourth = send(last, [(3, 2)])
    relays = [first_relay, second_relay, jnp.concatenate([third_a, third_b], axis=0)]
    for i in range(NQ):
        prompt.append(pick_by(me, mine[i], down[i], side[i], relays[i]))
    prompt.append(pick_by(me, cross, mine[0], fourth, last))
    slots = [
        pick_by(me, mine[0], mine[1], mine[0], cross),
        pick_by(me, mine[1], mine[2], mine[1], mine[0]),
        pick_by(me, mine[1], mine[1], mine[2], mine[1]),
        pick_by(me, mine[2], mine[2], cross, mine[2]),
    ]
    return jnp.concatenate(prompt + slots, axis=0)


def sum_prompt(me, partial):
    owner = jnp.array(OWNER_BLOCK, jnp.int32)

    def take(device):
        start = owner[device] * QB
        return lax.dynamic_slice_in_dim(partial, start, QB, 0)

    total = take(me).astype(f32)
    for flip in (1, 2, 3):
        total = total + send(take(me ^ flip), [(i, i ^ flip) for i in range(4)]).astype(f32)
    parts = [block_of(partial, i) for i in range(8)]
    crossed = send(jnp.where(me == 2, parts[7], parts[4]), [(2, 3), (3, 2)])
    zero = jnp.zeros_like(parts[0])
    joined = (jnp.where(me == 2, parts[6], parts[5]).astype(f32) + crossed.astype(f32)).astype(bf16)
    rows = [
        total.astype(bf16),
        pick_by(me, zero, zero, parts[4], joined),
        pick_by(me, zero, parts[4], parts[5], parts[6]),
        pick_by(me, zero, parts[5], joined, parts[7]),
    ]
    return jnp.concatenate(rows, axis=0)


def local(tokens, teacher, lengths, w_query, w_key, w_value, w_out, w_in, w_ff, gain_attn, gain_ff, bias_table):
    me = lax.axis_index("seq")
    own = tokens[0]
    inputs = own.astype(f32)
    targets = teacher[0].astype(f32)
    spans = lengths[0]
    width = own.shape[1]
    pairs = width // TILE

    def gather(w):
        return lax.all_gather(w, "wshard", axis=0, tiled=True)

    full_qkv = gather(jnp.concatenate([w_query, w_key, w_value], axis=1))
    full_out, full_in, full_ff = gather(w_out), gather(w_in), gather(w_ff)
    gains = gather(jnp.stack([gain_attn, gain_ff], axis=1)).astype(f32).T
    gain_one, gain_two = gains[0], gains[1]
    meta, qaug, kaug, far = placement(me, spans)
    bias = bias_tiles(bias_table)
    seen = gather_rows(me, own)
    inverse_one = rms(inputs)
    normed_own = (inputs * inverse_one * gain_one).astype(bf16)
    normed_seen = normed_rows(seen, gain_one)
    queries = jnp.dot(normed_own, full_qkv[:, :width], preferred_element_type=f32).astype(bf16)
    keys_values = jnp.dot(normed_seen, full_qkv[:, width:], preferred_element_type=f32).astype(bf16)
    context, rest, lse = attention_forward(meta, queries, keys_values, qaug, kaug, bias)
    middle = inputs + jnp.dot(context, full_out, preferred_element_type=f32)
    inverse_two = rms(middle)
    normed_two = (middle * inverse_two * gain_two).astype(bf16)
    hidden_act = jnp.maximum(jnp.dot(normed_two, full_in, preferred_element_type=f32), 0.0).astype(bf16)
    final_rows = middle + jnp.dot(hidden_act, full_ff, preferred_element_type=f32)
    local_rows = inputs.shape[0]
    row_index = me * local_rows + lax.iota(jnp.int32, local_rows)
    slot_index = jnp.maximum(row_index - PLEN, 0)
    owner_match = (slot_index // CLEN)[:, None] == lax.iota(jnp.int32, CONT)[None, :]
    row_limit = jnp.sum(jnp.where(owner_match, spans[None, :], 0), axis=1)
    valid_rows = (row_index < PLEN) | (slot_index % CLEN < row_limit)
    row_count = PLEN + jnp.sum(spans).astype(f32)
    factor = (PLEN + CONT * CLEN) / row_count
    d_final = jnp.where(valid_rows[:, None], factor * (final_rows - targets), 0.0)
    d_branch_two = d_final.astype(bf16)
    grad_ff = contract_rows(hidden_act, d_branch_two)
    d_pre = jnp.where(hidden_act > 0, dot_nt(d_branch_two, full_ff), 0.0).astype(bf16)
    grad_in = contract_rows(normed_two, d_pre)
    d_middle, grad_gain2 = norm_backward(middle, inverse_two, gain_two, dot_nt(d_pre, full_in))
    d_middle = d_final + d_middle
    d_branch_one = d_middle.astype(bf16)
    grad_out = contract_rows(context, d_branch_one)
    d_context = dot_nt(d_branch_one, full_out).astype(bf16)
    d_queries, d_keys, d_values, near = attention_backward(
        meta, queries, keys_values, d_context, context, rest, lse, qaug, kaug, bias, far)
    d_kv = sum_prompt(me, jnp.concatenate([d_keys, d_values], axis=1))
    prompt_start = jnp.array(OWNER_BLOCK, jnp.int32)[me] * QB
    normed_sum = jnp.concatenate([lax.dynamic_slice_in_dim(normed_seen, prompt_start, QB, 0), normed_own], axis=0)
    d_qkv = jnp.concatenate([
        jnp.concatenate([jnp.zeros((QB, width), bf16), d_queries], axis=0), d_kv], axis=1)
    grad_qkv = contract_rows(normed_sum, d_qkv)
    f_rows = dot_nt(d_qkv, full_qkv)
    f_first = f_rows[:QB]
    f_sent = f_first.astype(bf16)
    from_two = send(f_sent, [(2, 0)]).astype(f32)
    from_three = send(f_sent, [(3, 0)]).astype(f32)
    f_own = f_rows[QB:] + jnp.concatenate([jnp.where(me < 2, f_first, 0.0), from_two, from_three], axis=0)
    d_inputs, grad_gain1 = norm_backward(inputs, inverse_one, gain_one, f_own)
    d_tokens = d_middle + d_inputs

    def reduce(g):
        share = lax.psum_scatter(g.astype(bf16), "wshard", scatter_dimension=0, tiled=True)
        return lax.psum(share, "seq").astype(f32)

    share_ff, share_in, share_out, share_qkv = reduce(grad_ff), reduce(grad_in), reduce(grad_out), reduce(grad_qkv)
    heads = bias_table.shape[1]
    bias_local = jnp.dot(jnp.sum(near, axis=3).reshape(heads, 8 * TILE), jnp.asarray(bias_spread()),
                         precision=lax.Precision.HIGHEST)
    small = jnp.concatenate([grad_gain1, grad_gain2, bias_local.reshape(-1)])
    small = lax.psum(small, ("seq", "wshard"))
    mine = lax.axis_index("wshard")
    part = gain_attn.shape[0]
    gain_share = [lax.dynamic_slice_in_dim(small, i * width + mine * part, part) for i in range(2)]
    bias_grad = small[2 * width:].reshape(heads, NB).T
    return (
        final_rows.astype(bf16)[None],
        d_tokens[None],
        share_qkv[:, :width],
        share_qkv[:, width:2 * width],
        share_qkv[:, 2 * width:],
        share_out,
        share_in,
        share_ff,
        gain_share[0],
        gain_share[1],
        bias_grad,
    )


def solution(mesh):
    rows = P("wshard", "seq", None)
    weight = P("wshard", None)
    placed = (rows, rows) + (weight,) * 7 + (P("wshard"), P("wshard"), P())
    return jax.shard_map(
        local,
        mesh=mesh,
        in_specs=placed,
        out_specs=(rows, rows) + (weight,) * 6 + (P("wshard"), P("wshard"), P()),
        check_vma=False,
    )
```

time: 2100 us -> 599 us (0.29)
  other arithmetic: 707 us -> 67.6 us
  matrix products: 565 us -> 91.5 us
  loops' own time: 246 us -> 0 us
  Pallas kernels: 0 us -> 97.6 us
  waiting for transfers between devices: 290 us -> 197 us
  blocking collectives: 132 us -> 50 us
  local copies, waits for them, and re-layouts: 105 us -> 30.2 us
    dot_general x87 -> x10, matrix products: 486 us -> 59.9 us  [the longest x4 24.1 us: dot_nt(): lax.dot_general(a, b, (((1,), (1,)), ((), ())), preferred_element_type=f32)]
    reduce_sum x23 -> x6, other arithmetic: 387 us -> 4.96 us  [the longest x1 1.71 us: local(): jnp.sum(near, axis=3).reshape(heads, 8 * TILE)]
    add x9 -> x1, other arithmetic: 290 us -> 0.07 us  [bias_tiles(): TILE * (lax.broadcasted_iota(jnp.int32, shape, 0) - 2)]
    another operation x2 -> x0, loops' own time: 246 us -> none  [the longest x1 123 us: heads_backward(): return lax.fori_loop(0, local_heads, one_head, initial)]
    pallas_call x0 -> x2, Pallas kernels: none -> 97.6 us  [the longest x1 63.7 us: attention_backward(): pl.pallas_call(backward_kernel, grid_spec=pltpu.PrefetchScalarGridSpec(nu...]
    reduce_scatter x6 -> x4, waiting for transfers between devices: 201 us -> 117 us  [reduce(): lax.psum_scatter(g.astype(bf16), 'wshard', scatter_dimension=0, tiled=True)]
    ppermute x0 -> x18, waiting for transfers between devices: none -> 62.3 us  [send(): return lax.ppermute(rows, 'seq', pairs)]
    all_to_all x3 -> x0, blocking collectives: 48.3 us -> none  [the longest x1 17.4 us: local(): lax.all_to_all(head_d_query, 'seq', split_axis=0, concat_axis=1, tiled=True)]
  transfers between devices with their start and end apart: 18 -> 27, of which waited for: 10 -> 10; matrix products, arithmetic and copies ran while one was open for 63% -> 24% of each run, Pallas kernels for 0% -> 6%
where the time goes in v1:
time: 599 us; the launch traced here: 589 us
  waiting for transfers between devices  197 us (33%)
  Pallas kernels  97.6 us (16%)
  matrix products  91.5 us (15%)
  other arithmetic  67.6 us (11%)
  blocking collectives  50 us (8%)
  starting transfers between devices  30.5 us (5%)
  local copies, waits for them, and re-layouts  30.2 us (5%)
  between operations  24 us (4%)
    reduce_scatter x4, waiting for transfers between devices, reduce(): lax.psum_scatter(g.astype(bf16), 'wshard', scatter_dimension=0, tiled=True)  117 us
    pallas_call x1, Pallas kernels, attention_backward(): pl.pallas_call(backward_kernel, grid_spec=pltpu.PrefetchScalarGridSpec(nu...  63.7 us
    ppermute x18, waiting for transfers between devices, send(): return lax.ppermute(rows, 'seq', pairs)  62.3 us
    psum x1, blocking collectives, local(): small = lax.psum(small, ('seq', 'wshard'))  38 us
    pallas_call x1, Pallas kernels, attention_forward(): pl.pallas_call(forward_kernel, grid_spec=pltpu.PrefetchScalarGridSpec(num...  33.9 us
    dot_general x4, matrix products, contract_rows(): lax.dot_general(left, right, (((0,), (0,)), ((), ())), preferred_element_...  31.6 us
    ppermute x18, starting transfers between devices, send(): return lax.ppermute(rows, 'seq', pairs)  29.9 us
    dot_general x4, matrix products, dot_nt(): lax.dot_general(a, b, (((1,), (1,)), ((), ())), preferred_element_type=f32)  24.1 us
  transfers between devices with their start and end apart: 27, of which 10 were waited for; matrix products, arithmetic and copies ran while one was open for 24% of the time, Pallas kernels for 6%

profile of v1, /device:TPU:0, one launch (start us, length us, event | category | flops | bytes accessed | tf_op | source)
XLA Modules:
  0.0 588.6 jit_solution(17431992182470137489)
XLA Ops:
  13.2 4.9 collective-permute-start.1
  18.1 4.2 collective-permute-start
  38.9 16.4 %select_select_fusion.bias_ref = f32[12,640,128]{2,1,0:T(8,128)} fusion(f32[12]{0:T(128)S(1)} %get-tuple-element.85, f32[12]{0:T(128)S(1)} %get-tuple-element.86, f32[12]{0:T(128)S(1)} %get-tuple-element.87, f32[12]{0:T(128)S(1)} %get-tuple-element.88, f32[12]{0:T(128)S(1)} %get-tuple-element.89, f32[12]{0:T(128)S(1)} %get-tuple-element.90, ...), kind=kLoop, calls=%fused_computation.14 | loop fusion | flops 29491200 | bytes 6391248 | tf_op jit(solution)/shard_map/jit(_where)/select_n | solution.py:310
  55.3 12.0 %all-gather = bf16[8,96,2]{1,2,0:T(2,128)(2,1)S(1)} all-gather(bf16[1,96,2]{1,2,0:T(2,128)(2,1)S(1)} %maximum_bitcast_fusion), channel_id=1, replica_groups=mesh['seq'=4,'wshard'=8] {'wshard'}, dimensions={0}, use_global_device_ids=true | all-gather | bytes 3456 | tf_op jit(solution)/shard_map/all_gather | solution.py:457
  79.1 3.2 select_convert_fusion.2.pick_ref
  89.1 5.5 collective-permute-done.4
  99.2 3.4 collective-permute-done.7
  105.4 10.0 %collective-permute-done.10 = bf16[256,768]{0,1:T(8,128)(2,1)S(1)} collective-permute-done((bf16[256,768]{0,1:T(8,128)(2,1)S(1)}, bf16[256,768]{0,1:T(8,128)(2,1)S(1)}, u32[]{:S(2)}, u32[]{:S(2)}) %collective-permute-start.10) | collective-permute-done | bytes 393248 | tf_op jit(solution)/shard_map/ppermute | solution.py:386
  119.5 3.6 convolution_convert_fusion.6.q_ref
  123.0 7.3 %convolution_convert_fusion.k_ref.v_ref = bf16[2048,1536]{1,0:T(8,128)(2,1)} fusion(bf16[2048,768]{0,1:T(8,128)(2,1)S(1)} %copy-done.8, bf16[768,2304]{1,0:T(8,128)(2,1)S(1)} %copy-done.40), kind=kOutput, calls=%fused_computation.6 | convolution fusion | flops 4834983936 | bytes 11796480 | tf_op jit(solution)/shard_map/dot_general | solution.py:470
  130.3 33.9 %attention_forward.1 = (bf16[768,768]{1,0:T(8,128)(2,1)}, bf16[768,768]{1,0:T(8,128)(2,1)}, f32[6,2,768]{2,1,0:T(2,128)}) custom-call(s32[6]{0:T(128)} %pad_add_fusion.meta, bf16[768,768]{1,0:T(8,128)(2,1)} %convolution_convert_fusion.6.q_ref, bf16[2048,1536]{1,0:T(8,128)(2,1)} %convolution_convert_fusion.k_ref.v_ref, ...), custom_call_target="tpu_custom_call" | custom-call | tf_op jit(solution)/shard_map/attention_forward/pallas_call | solution.py:93
  164.2 4.2 multiply_reduce_fusion.2
  168.5 9.4 %maximum_convert_fusion = bf16[768,3072]{1,0:T(8,128)(2,1)} fusion(bf16[768,3072]{1,0:T(8,128)(2,1)} %all-gather.10.cloned.1.call-done, f32[768,768]{0,1:T(8,128)} %get-tuple-element.186, f32[768]{0:T(1024)S(1)} %copy-done.19, f32[768]{0:T(1024)S(1)} %add_rsqrt_fusion.1), kind=kOutput, calls=%fused_computation.2 | convolution fusion | flops 3630366720 | bytes 11802624 | tf_op jit(solution)/shard_map/dot_general | solution.py:475
  177.8 4.9 all-gather.12.cloned.1.call-done
  182.8 10.0 %fusion.23 = (bf16[768,768]{0,1:T(8,128)(2,1)}, f32[768,768]{0,1:T(8,128)S(1)}) fusion(bf16[1,768,768]{1,2,0:T(8,128)(2,1)S(1)} %copy.83, f32[]{:T(128)S(6)} %div.84, pred[768]{0:T(1024)(128)(4,1)S(1)} %copy-done.27, f32[768,768]{0,1:T(8,128)} %get-tuple-element.186, bf16[768,3072]{1,0:T(8,128)(2,1)} %maximum_convert_fusion, ...), kind=kOutput, calls=%fused_computation.56 | convolution fusion | flops 3627417600 | bytes 16515844 | tf_op jit(solution)/shard_map/dot_general | solution.py:476
  192.8 7.2 %select_convert_fusion = bf16[768,3072]{1,0:T(8,128)(2,1)} fusion(bf16[768,3072]{1,0:T(8,128)(2,1)S(1)} %copy-done.45, bf16[768,768]{0,1:T(8,128)(2,1)} %get-tuple-element.187, bf16[3072,768]{1,0:T(8,128)(2,1)S(1)} %copy-done.39), kind=kOutput, calls=%fused_computation.1 | convolution fusion | flops 3630956544 | bytes 15335424 | tf_op jit(solution)/shard_map/dot_general | solution.py:25
  200.0 7.1 %multiply_reduce_fusion = (f32[768]{0:T(1024)}, f32[768]{0:T(1024)S(1)}, f32[768,768]{0,1:T(8,128)S(1)}) fusion(f32[768,768]{0,1:T(8,128)S(1)} %copy-done.10, f32[768]{0:T(1024)S(1)} %add_rsqrt_fusion.1, f32[768]{0:T(1024)S(1)} %copy-done.19, bf16[768,3072]{1,0:T(8,128)(2,1)} %select_convert_fusion, bf16[768,3072]{1,0:T(8,128)(2,1)S(1)} %copy-done.38), kind=kOutput, calls=%fused_computation.39 | convolution fusion | flops 3627416064 | bytes 14168064 | tf_op jit(solution)/shard_map/dot_general | solution.py:25
  211.3 63.7 %attention_backward.1 = (bf16[768,768]{1,0:T(8,128)(2,1)}, bf16[2048,768]{1,0:T(8,128)(2,1)}, bf16[2048,768]{1,0:T(8,128)(2,1)}, f32[6,2,8,8,128]{4,3,2,1,0:T(8,128)}) custom-call(s32[6]{0:T(128)} %pad_add_fusion.meta, bf16[768,768]{1,0:T(8,128)(2,1)} %convolution_convert_fusion.6.q_ref, bf16[2048,1536]{1,0:T(8,128)(2,1)} %convolution_convert_fusion.k_ref.v_ref, ...), custom_call_target="tpu_custom_call" | custom-call | tf_op jit(solution)/shard_map/attention_backward/pallas_call | solution.py:253
  285.3 3.3 collective-permute-start.14
  295.1 9.4 %collective-permute-done.12 = bf16[256,1536]{1,0:T(8,128)(2,1)} collective-permute-done((bf16[256,1536]{1,0:T(8,128)(2,1)}, bf16[256,1536]{1,0:T(8,128)(2,1)}, u32[]{:S(2)}, u32[]{:S(2)}) %collective-permute-start.12) | collective-permute-done | bytes 786464 | tf_op jit(solution)/shard_map/ppermute | solution.py:386
  304.5 34.0 %collective-permute-done.14 = bf16[256,1536]{1,0:T(8,128)(2,1)} collective-permute-done((bf16[256,1536]{1,0:T(8,128)(2,1)}, bf16[256,1536]{1,0:T(8,128)(2,1)}, u32[]{:S(2)}, u32[]{:S(2)}) %collective-permute-start.14) | collective-permute-done | bytes 786464 | tf_op jit(solution)/shard_map/ppermute | solution.py:386
  341.7 11.5 %convolution_convert_fusion.3 = bf16[768,2304]{1,0:T(8,128)(2,1)} fusion(bf16[768,768]{0,1:T(8,128)(2,1)S(1)} %copy-done.12, bf16[256,768]{0,1:T(8,128)(2,1)S(1)} %constant_dynamic-slice_fusion, bf16[768,768]{1,0:T(8,128)(2,1)S(1)} %copy-done.42, bf16[256,1536]{1,0:T(8,128)(2,1)S(1)} %get-tuple-element.122, bf16[256,1536]{1,0:T(8,128)(2,1)S(1)} %copy-done.17, ...), kind=kOutput, calls=%fused_computation.12 | convolution fusion | flops 3657105408 | bytes 9437184 | tf_op jit(solution)/shard_map/dot_general | solution.py:378
  353.2 9.1 %convolution_convert_fusion.2 = bf16[768,3072]{1,0:T(8,128)(2,1)} fusion(bf16[768,3072]{1,0:T(8,128)(2,1)} %select_convert_fusion, f32[768,768]{0,1:T(8,128)} %get-tuple-element.186, f32[768]{0:T(1024)S(1)} %copy-done.19, f32[768]{0:T(1024)S(1)} %add_rsqrt_fusion.1), kind=kOutput, calls=%fused_computation.11 | convolution fusion | flops 3628007424 | bytes 11802624 | tf_op jit(solution)/shard_map/dot_general | solution.py:378
  362.6 8.9 %convolution_convert_fusion.1 = bf16[3072,768]{1,0:T(8,128)(2,1)} fusion(bf16[768,3072]{1,0:T(8,128)(2,1)} %maximum_convert_fusion, bf16[768,768]{0,1:T(8,128)(2,1)} %get-tuple-element.187), kind=kOutput, calls=%fused_computation.10 | convolution fusion | flops 3626237952 | bytes 10616832 | tf_op jit(solution)/shard_map/dot_general | solution.py:378
  377.1 7.6 %fusion.101 = f32[1024,768]{0,1:T(8,128)S(1)} fusion(bf16[768,2304]{1,0:T(8,128)(2,1)} %all-gather.6.cloned.1.call-done, bf16[768,768]{1,0:T(8,128)(2,1)} %get-tuple-element.21, bf16[256,1536]{1,0:T(8,128)(2,1)} %copy-done.15, bf16[256,1536]{1,0:T(8,128)(2,1)} %get-tuple-element.125, bf16[256,1536]{1,0:T(8,128)(2,1)} %copy-done.14, ...), kind=kOutput, calls=%fused_computation.249 | convolution fusion | flops 3652190208 | bytes 11010048 | tf_op jit(solution)/shard_map/dot_general | solution.py:25
  389.7 5.3 reduce-scatter.5.cloned.1.call-done
  395.0 55.9 %reduce-scatter.9.cloned.1.call-done = bf16[96,3072]{1,0:T(8,128)(2,1)} async-done(((bf16[768,3072]{1,0:T(8,128)(2,1)}), bf16[96,3072]{1,0:T(8,128)(2,1)}) %reduce-scatter.9.cloned.1.call-update) | async-done | bytes 589840 | tf_op jit(solution)/shard_map/reduce_scatter | solution.py:513
  450.9 55.8 %reduce-scatter.11.cloned.1.call-done = bf16[384,768]{1,0:T(8,128)(2,1)} async-done(((bf16[3072,768]{1,0:T(8,128)(2,1)}), bf16[384,768]{1,0:T(8,128)(2,1)}) %reduce-scatter.11.cloned.1.call-update) | async-done | bytes 589840 | tf_op jit(solution)/shard_map/reduce_scatter | solution.py:513
  514.5 38.0 %psum.39 = f32[1920]{0:T(1024)} all-reduce(f32[1920]{0:T(1024)S(1)} %pad_maximum_fusion.1), channel_id=1, replica_groups=mesh['seq'=4,'wshard'=8] {'seq','wshard'}, use_global_device_ids=true, to_apply=%region_19.20 | all-reduce | flops 1920 | bytes 15360 | tf_op jit(solution)/shard_map/psum | solution.py:521
  553.9 4.5 fusion.14
  558.3 3.0 copy.89
  563.4 11.2 %all-reduce.4.cloned.1.call-done = (bf16[96,2304]{1,0:T(8,128)(2,1)}, bf16[96,768]{1,0:T(8,128)(2,1)}, bf16[96,3072]{1,0:T(8,128)(2,1)}, bf16[384,768]{1,0:T(8,128)(2,1)}) async-done(((bf16[96,2304]{1,0:T(8,128)(2,1)}, bf16[96,768]{1,0:T(8,128)(2,1)}, bf16[96,3072]{1,0:T(8,128)(2,1)}, bf16[384,768]{1,0:T(8,128)(2,1)}), (bf16[96,2304]{1,0:T(8,128)(2,1)}, bf16[96,768]{1,0:T(8,128)(2,1)}, ...) | async-done | bytes 1769488 | tf_op jit(solution)/shard_map/psum | solution.py:514
  (229 shorter events, 96.2 us)
Async XLA Ops:
  7.2 112.3 %all-gather.6.cloned.1.call-start = ((), (), s32[]{:S(2)}) async-start(), calls=%async_computation.4 | async-start | bytes 3981312 | tf_op jit(solution)/shard_map/all_gather | solution.py:457
  9.1 155.1 %all-gather.8.cloned.1.call-start = ((), (), s32[]{:S(2)}) async-start(), calls=%async_computation.5 | async-start | bytes 1327104 | tf_op jit(solution)/shard_map/all_gather | solution.py:457
  9.8 158.6 %all-gather.10.cloned.1.call-start = ((), (), s32[]{:S(2)}) async-start(), calls=%async_computation.6 | async-start | bytes 5308416 | tf_op jit(solution)/shard_map/all_gather | solution.py:457
  10.6 172.2 %all-gather.12.cloned.1.call-start = ((), (), s32[]{:S(2)}) async-start(), calls=%async_computation.7 | async-start | bytes 5308416 | tf_op jit(solution)/shard_map/all_gather | solution.py:457
  13.2 69.2 %collective-permute-start.1 = (bf16[256,768]{0,1:T(8,128)(2,1)}, bf16[256,768]{0,1:T(8,128)(2,1)S(1)}, u32[]{:S(2)}, u32[]{:S(2)}) collective-permute-start(bf16[256,768]{0,1:T(8,128)(2,1)} %get-tuple-element.136), channel_id=1, source_target_pairs={{0,16},{8,24},{1,17},{9,25},{2,18},{10,26},{3,19},{11,27},{4,20},{... | collective-permute-start | bytes 1179656 | tf_op jit(solution)/shard_map/ppermute | solution.py:386
  18.1 51.1 %collective-permute-start = (bf16[256,768]{0,1:T(8,128)(2,1)}, bf16[256,768]{0,1:T(8,128)(2,1)}, u32[]{:S(2)}, u32[]{:S(2)}) collective-permute-start(bf16[256,768]{0,1:T(8,128)(2,1)} %get-tuple-element.136), channel_id=1, source_target_pairs={{0,8},{1,9},{2,10},{3,11},{4,12},{5,13},{6,14},{7,15}} | collective-permute-start | bytes 1179656 | tf_op jit(solution)/shard_map/ppermute | solution.py:386
  22.2 75.6 %collective-permute-start.6 = (bf16[256,768]{0,1:T(8,128)(2,1)}, bf16[256,768]{0,1:T(8,128)(2,1)S(1)}, u32[]{:S(2)}, u32[]{:S(2)}) collective-permute-start(bf16[256,768]{0,1:T(8,128)(2,1)} %get-tuple-element.134), channel_id=1, source_target_pairs={{0,8},{1,9},{2,10},{3,11},{4,12},{5,13},{6,14},{7,15}} | collective-permute-start | bytes 1179656 | tf_op jit(solution)/shard_map/ppermute | solution.py:386
  23.5 80.5 %collective-permute-start.3 = (bf16[256,768]{0,1:T(8,128)(2,1)S(1)}, bf16[256,768]{0,1:T(8,128)(2,1)}, u32[]{:S(2)}, u32[]{:S(2)}) collective-permute-start(bf16[256,768]{0,1:T(8,128)(2,1)S(1)} %get-tuple-element.135), channel_id=1, source_target_pairs={{0,8},{1,9},{2,10},{3,11},{4,12},{5,13},{6,14},{7,15}} | collective-permute-start | bytes 1179656 | tf_op jit(solution)/shard_map/ppermute | solution.py:386
  25.6 364.1 %reduce-scatter.7.cloned.1.call-start = ((), (), s32[]{:S(2)}) async-start(), calls=%async_computation.9 | async-start | bytes 1327104 | tf_op jit(solution)/shard_map/reduce_scatter | solution.py:513
  69.2 13.2 %collective-permute-start.2 = (bf16[256,768]{0,1:T(8,128)(2,1)}, bf16[256,768]{0,1:T(8,128)(2,1)}, u32[]{:S(2)}, u32[]{:S(2)}) collective-permute-start(bf16[256,768]{0,1:T(8,128)(2,1)} %collective-permute-done), channel_id=1, source_target_pairs={{8,24},{9,25},{10,26},{11,27},{12,28},{13,29},{14,30},{15,31}} | collective-permute-start | bytes 1179656 | tf_op jit(solution)/shard_map/ppermute | solution.py:386
  78.3 104.5 %copy-start.6 = (bf16[1,768,768]{1,2,0:T(8,128)(2,1)}, bf16[1,768,768]{1,2,0:T(8,128)(2,1)S(1)}, u32[]{:S(2)}) copy-start(bf16[1,768,768]{1,2,0:T(8,128)(2,1)S(1)} %copy.83) | copy-start | bytes 3538948
  83.8 10.7 %collective-permute-start.4 = (bf16[256,768]{0,1:T(8,128)(2,1)S(1)}, bf16[256,768]{0,1:T(8,128)(2,1)S(1)}, u32[]{:S(2)}, u32[]{:S(2)}) collective-permute-start(bf16[256,768]{0,1:T(8,128)(2,1)S(1)} %get-tuple-element.131), channel_id=1, source_target_pairs={{0,16},{1,17},{2,18},{3,19},{4,20},{5,21},{6,22},{7,23}} | collective-permute-start | bytes 1179656 | tf_op jit(solution)/shard_map/ppermute | solution.py:386
  87.8 14.9 %collective-permute-start.7 = (bf16[256,768]{0,1:T(8,128)(2,1)S(1)}, bf16[256,768]{0,1:T(8,128)(2,1)S(1)}, u32[]{:S(2)}, u32[]{:S(2)}) collective-permute-start(bf16[256,768]{0,1:T(8,128)(2,1)S(1)} %get-tuple-element.132), channel_id=1, source_target_pairs={{0,16},{1,17},{2,18},{3,19},{4,20},{5,21},{6,22},{7,23}} | collective-permute-start | bytes 1179656 | tf_op jit(solution)/shard_map/ppermute | solution.py:386
  94.5 10.3 %collective-permute-start.5 = (bf16[256,768]{0,1:T(8,128)(2,1)S(1)}, bf16[256,768]{0,1:T(8,128)(2,1)S(1)}, u32[]{:S(2)}, u32[]{:S(2)}) collective-permute-start(bf16[256,768]{0,1:T(8,128)(2,1)S(1)} %collective-permute-done.4), channel_id=1, source_target_pairs={{16,24},{17,25},{18,26},{19,27},{20,28},{21,29},{22,30},{23,31}} | collective-permute-start | bytes 1179656 | tf_op jit(solution)/shard_map/ppermute | solution.py:386
  97.9 7.3 %collective-permute-start.8 = (bf16[128,768]{0,1:T(8,128)(2,1)S(1)}, bf16[128,768]{0,1:T(8,128)(2,1)S(1)}, u32[]{:S(2)}, u32[]{:S(2)}) collective-permute-start(bf16[128,768]{0,1:T(8,128)(2,1)S(1)} %slice.264), channel_id=1, source_target_pairs={{8,24},{9,25},{10,26},{11,27},{12,28},{13,29},{14,30},{15,31}} | collective-permute-start | bytes 589832 | tf_op jit(solution)/shard_map/ppermute | solution.py:386
  98.5 6.8 %collective-permute-start.11 = (bf16[256,768]{0,1:T(8,128)(2,1)S(1)}, bf16[256,768]{0,1:T(8,128)(2,1)S(1)}, u32[]{:S(2)}, u32[]{:S(2)}) collective-permute-start(bf16[256,768]{0,1:T(8,128)(2,1)S(1)} %collective-permute-done.1), channel_id=1, source_target_pairs={{24,16},{25,17},{26,18},{27,19},{28,20},{29,21},{30,22},{31,23}} | collective-permute-start | bytes 1179656 | tf_op jit(solution)/shard_map/ppermute | solution.py:386
  102.7 12.7 %collective-permute-start.10 = (bf16[256,768]{0,1:T(8,128)(2,1)S(1)}, bf16[256,768]{0,1:T(8,128)(2,1)S(1)}, u32[]{:S(2)}, u32[]{:S(2)}) collective-permute-start(bf16[256,768]{0,1:T(8,128)(2,1)S(1)} %get-tuple-element.130), channel_id=1, source_target_pairs={{8,0},{16,24},{24,16},{9,1},{17,25},{25,17},{10,2},{18,26},{26,18}... | collective-permute-start | bytes 1179656 | tf_op jit(solution)/shard_map/ppermute | solution.py:386
  104.0 1.2 collective-permute-start.9
  282.0 10.6 %collective-permute-start.15 = (bf16[256,1536]{1,0:T(8,128)(2,1)}, bf16[256,1536]{1,0:T(8,128)(2,1)}, u32[]{:S(2)}, u32[]{:S(2)}) collective-permute-start(bf16[256,1536]{1,0:T(8,128)(2,1)} %get-tuple-element.124), channel_id=1, source_target_pairs={{16,24},{24,16},{17,25},{25,17},{18,26},{26,18},{19,27},{27,19},{2... | collective-permute-start | bytes 2359304 | tf_op jit(solution)/shard_map/ppermute | solution.py:386
  283.7 20.7 %collective-permute-start.12 = (bf16[256,1536]{1,0:T(8,128)(2,1)}, bf16[256,1536]{1,0:T(8,128)(2,1)}, u32[]{:S(2)}, u32[]{:S(2)}) collective-permute-start(bf16[256,1536]{1,0:T(8,128)(2,1)} %get-tuple-element.123), channel_id=1, source_target_pairs={{0,8},{8,0},{16,24},{24,16},{1,9},{9,1},{17,25},{25,17},{2,10},{10... | collective-permute-start | bytes 2359304 | tf_op jit(solution)/shard_map/ppermute | solution.py:386
  285.3 53.2 %collective-permute-start.14 = (bf16[256,1536]{1,0:T(8,128)(2,1)}, bf16[256,1536]{1,0:T(8,128)(2,1)}, u32[]{:S(2)}, u32[]{:S(2)}) collective-permute-start(bf16[256,1536]{1,0:T(8,128)(2,1)} %get-tuple-element.126), channel_id=1, source_target_pairs={{0,24},{8,16},{16,8},{24,0},{1,25},{9,17},{17,9},{25,1},{2,26},{10... | collective-permute-start | bytes 2359304 | tf_op jit(solution)/shard_map/ppermute | solution.py:386
  288.6 49.9 %collective-permute-start.13 = (bf16[256,1536]{1,0:T(8,128)(2,1)}, bf16[256,1536]{1,0:T(8,128)(2,1)}, u32[]{:S(2)}, u32[]{:S(2)}) collective-permute-start(bf16[256,1536]{1,0:T(8,128)(2,1)} %get-tuple-element.127), channel_id=1, source_target_pairs={{0,16},{8,24},{16,0},{24,8},{1,17},{9,25},{17,1},{25,9},{2,18},{10... | collective-permute-start | bytes 2359304 | tf_op jit(solution)/shard_map/ppermute | solution.py:386
  290.9 104.1 %reduce-scatter.5.cloned.1.call-start = ((), (), s32[]{:S(2)}) async-start(), calls=%async_computation.8 | async-start | bytes 3981312 | tf_op jit(solution)/shard_map/reduce_scatter | solution.py:513
  295.1 45.7 %copy-start.14 = (bf16[256,1536]{1,0:T(8,128)(2,1)}, bf16[256,1536]{1,0:T(8,128)(2,1)S(1)}, u32[]{:S(2)}) copy-start(bf16[256,1536]{1,0:T(8,128)(2,1)S(1)} %get-tuple-element.121) | copy-start | bytes 2359300
  295.1 46.6 %copy-start.12 = (bf16[768,768]{0,1:T(8,128)(2,1)S(1)}, bf16[768,768]{0,1:T(8,128)(2,1)}, u32[]{:S(2)}) copy-start(bf16[768,768]{0,1:T(8,128)(2,1)} %fusion.9) | copy-start | bytes 3538948
  295.1 46.6 %copy-start.17 = (bf16[256,1536]{1,0:T(8,128)(2,1)S(1)}, bf16[256,1536]{1,0:T(8,128)(2,1)}, u32[]{:S(2)}) copy-start(bf16[256,1536]{1,0:T(8,128)(2,1)} %get-tuple-element.125) | copy-start | bytes 2359300
  295.1 46.6 %copy-start.42 = (bf16[768,768]{1,0:T(8,128)(2,1)S(1)}, bf16[768,768]{1,0:T(8,128)(2,1)}, u32[]{:S(2)}) copy-start(bf16[768,768]{1,0:T(8,128)(2,1)} %get-tuple-element.21) | copy-start | bytes 3538948
  353.1 97.8 %reduce-scatter.9.cloned.1.call-start = ((), (), s32[]{:S(2)}) async-start(), calls=%async_computation.10 | async-start | bytes 5308416 | tf_op jit(solution)/shard_map/reduce_scatter | solution.py:513
  362.3 144.4 %reduce-scatter.11.cloned.1.call-start = ((), (), s32[]{:S(2)}) async-start(), calls=%async_computation.11 | async-start | bytes 5308416 | tf_op jit(solution)/shard_map/reduce_scatter | solution.py:513
  371.5 203.2 %all-reduce.4.cloned.1.call-start = ((), (), s32[]{:S(2)}) async-start(), calls=%async_computation.12 | async-start | bytes 3538944 | tf_op jit(solution)/shard_map/psum | solution.py:514
  387.1 123.1 %collective-permute-start.17 = (bf16[256,768]{0,1:T(8,128)(2,1)}, bf16[256,768]{0,1:T(8,128)(2,1)}, u32[]{:S(2)}, u32[]{:S(2)}) collective-permute-start(bf16[256,768]{0,1:T(8,128)(2,1)} %slice.412), channel_id=1, source_target_pairs={{24,0},{25,1},{26,2},{27,3},{28,4},{29,5},{30,6},{31,7}} | collective-permute-start | bytes 1179656 | tf_op jit(solution)/shard_map/ppermute | solution.py:386
  388.4 123.2 %collective-permute-start.16 = (bf16[256,768]{0,1:T(8,128)(2,1)}, bf16[256,768]{0,1:T(8,128)(2,1)}, u32[]{:S(2)}, u32[]{:S(2)}) collective-permute-start(bf16[256,768]{0,1:T(8,128)(2,1)} %slice.412), channel_id=1, source_target_pairs={{16,0},{17,1},{18,2},{19,3},{20,4},{21,5},{22,6},{23,7}} | collective-permute-start | bytes 1179656 | tf_op jit(solution)/shard_map/ppermute | solution.py:386
  (41 other events, 472.6 us)
Sparse Core Ops, SparseCore 0:
  10.2 44.2 all-gather.5
  56.1 21.5 all-gather.7
  79.4 51.3 all-gather.9
  132.2 50.5 all-gather.11
  291.0 31.4 reduce-scatter.6
  353.2 41.7 reduce-scatter.4
  397.4 53.4 reduce-scatter.8
  453.3 53.3 reduce-scatter.10
  510.6 64.0 all-reduce.3

commit v2 on v1

--- a/solution.py
+++ b/solution.py
@@ -4,6 +4,7 @@
 from jax import lax
 from jax.experimental import pallas as pl
 from jax.experimental.pallas import tpu as pltpu
+from jax.experimental.layout import Layout, with_layout_constraint
 from jax.sharding import PartitionSpec as P
 
 DH = 64
@@ -86,18 +87,20 @@
         rest_ref[qb * QB:(qb + 1) * QB, :] = (ctx - ctx_low.astype(f32)).astype(bf16)
 
 
-def attention_forward(meta, q, kv, qaug, kaug, bias):
-    pairs = q.shape[1] // TILE
-    spec = lambda rows, first=0: pl.BlockSpec((rows, TILE), lambda i, meta: (0, first + i))
+def attention_forward(meta, q, kv, qaug, kaug, bias, first, pairs):
+    own = pl.BlockSpec((ROWS, TILE), lambda i, meta: (0, first + i))
+    out = pl.BlockSpec((ROWS, TILE), lambda i, meta: (0, i))
+    keys = pl.BlockSpec((KROWS, TILE), lambda i, meta: (0, 2 * (first + i)))
+    values = pl.BlockSpec((KROWS, TILE), lambda i, meta: (0, 2 * (first + i) + 1))
     fixed = lambda rows: pl.BlockSpec((rows, TILE), lambda i, meta: (0, 0))
     return pl.pallas_call(
         forward_kernel,
         grid_spec=pltpu.PrefetchScalarGridSpec(
             num_scalar_prefetch=1,
             grid=(pairs,),
-            in_specs=[spec(ROWS), spec(KROWS), spec(KROWS, pairs), fixed(ROWS), fixed(KROWS),
-                      pl.BlockSpec((2, 5 * TILE, TILE), lambda i, meta: (i, 0, 0))],
-            out_specs=[spec(ROWS), spec(ROWS), pl.BlockSpec((1, 2, ROWS), lambda i, meta: (i, 0, 0))],
+            in_specs=[own, keys, values, fixed(ROWS), fixed(KROWS),
+                      pl.BlockSpec((2, 5 * TILE, TILE), lambda i, meta: (first + i, 0, 0))],
+            out_specs=[out, out, pl.BlockSpec((1, 2, ROWS), lambda i, meta: (i, 0, 0))],
             scratch_shapes=[
                 pltpu.VMEM((2, KROWS, TILE), bf16),
                 pltpu.VMEM((TILE, KROWS), bf16),
@@ -109,6 +112,8 @@
                    jax.ShapeDtypeStruct((pairs, 2, ROWS), f32)],
         compiler_params=pltpu.CompilerParams(dimension_semantics=("arbitrary",),
                                              vmem_limit_bytes=56 << 20),
+        cost_estimate=pl.CostEstimate(flops=pairs * 5_000_000_000, bytes_accessed=pairs * 2_000_000,
+                                      transcendentals=pairs * 2 * ROWS * (PLEN + CLEN)),
         name="attention_forward",
     )(meta, q, kv, kv, qaug, kaug, bias)
 
@@ -121,7 +126,7 @@
 
 
 def backward_kernel(meta, q_ref, k_ref, v_ref, do_ref, ctx_ref, rest_ref, lse_ref, qaug_ref, kaug_ref,
-                    bias_ref, pick_ref, dq_ref, dk_ref, dv_ref, near_ref,
+                    bias_ref, pick_ref, dq_ref, dkv_ref, near_ref,
                     k_scr, kt_scr, q_scr, do_scr, delta_scr, ds_scr, dks_scr, dvs_scr, far_scr):
     low_k = low_lanes((KROWS, TILE))
     low_q = low_lanes((ROWS, TILE))
@@ -173,8 +178,8 @@
                 dv = a if dv is None else dv + a
                 dk = b if dk is None else dk + b
             dks.append(dk)
-        dv_ref[pl.ds(start, QB), :] = dv.astype(bf16)
-        dk_ref[pl.ds(start, QB), :] = jnp.where(low_c, dks[0], dks[1]).astype(bf16)
+        dkv_ref[pl.ds(start, QB), TILE:] = dv.astype(bf16)
+        dkv_ref[pl.ds(start, QB), :TILE] = jnp.where(low_c, dks[0], dks[1]).astype(bf16)
         sums = jnp.where(low_c, dks[1], dks[0])
         far_scr[2 * c] = fold_rows(sums[:TILE])
         far_scr[2 * c + 1] = fold_rows(sums[TILE:])
@@ -198,9 +203,9 @@
                 dv = a if dv is None else dv + a
                 dks_scr[h, pl.ds(start, QB), :] += dot_nn(ds, q_scr[h, cols, :])
             dvs_scr[pl.ds(start, QB), :] += dv
-    dv_ref[PLEN:, :] = dvs_scr[...].astype(bf16)
+    dkv_ref[PLEN:, TILE:] = dvs_scr[...].astype(bf16)
     low_s = low_lanes((2 * CLEN, TILE))
-    dk_ref[PLEN:, :] = jnp.where(low_s, dks_scr[0], dks_scr[1]).astype(bf16)
+    dkv_ref[PLEN:, :TILE] = jnp.where(low_s, dks_scr[0], dks_scr[1]).astype(bf16)
     sums = jnp.where(low_s, dks_scr[1], dks_scr[0])
     for t in range(2 * CLEN // TILE):
         far_scr[8 + t] = fold_rows(sums[t * TILE:(t + 1) * TILE])
@@ -245,22 +250,23 @@
             near_ref[0, h, i] = eight
 
 
-def attention_backward(meta, q, kv, do, ctx, rest, lse, qaug, kaug, bias, pick):
-    pairs = q.shape[1] // TILE
-    spec = lambda rows, first=0: pl.BlockSpec((rows, TILE), lambda i, meta: (0, first + i))
+def attention_backward(meta, q, kv, do, ctx, rest, lse, qaug, kaug, bias, pick, first, pairs):
+    own = pl.BlockSpec((ROWS, TILE), lambda i, meta: (0, first + i))
+    keys = pl.BlockSpec((KROWS, TILE), lambda i, meta: (0, 2 * (first + i)))
+    values = pl.BlockSpec((KROWS, TILE), lambda i, meta: (0, 2 * (first + i) + 1))
     fixed = lambda rows: pl.BlockSpec((rows, TILE), lambda i, meta: (0, 0))
-    width = pairs * TILE
     return pl.pallas_call(
         backward_kernel,
         grid_spec=pltpu.PrefetchScalarGridSpec(
             num_scalar_prefetch=1,
             grid=(pairs,),
-            in_specs=[spec(ROWS), spec(KROWS), spec(KROWS, pairs), spec(ROWS), spec(ROWS), spec(ROWS),
-                      pl.BlockSpec((1, 2, ROWS), lambda i, meta: (i, 0, 0)),
+            in_specs=[own, keys, values, own, own, own,
+                      pl.BlockSpec((1, 2, ROWS), lambda i, meta: (first + i, 0, 0)),
                       fixed(ROWS), fixed(KROWS),
-                      pl.BlockSpec((2, 5 * TILE, TILE), lambda i, meta: (i, 0, 0)),
+                      pl.BlockSpec((2, 5 * TILE, TILE), lambda i, meta: (first + i, 0, 0)),
                       pl.BlockSpec((2, 2, 16, 8, TILE), lambda i, meta: (0, 0, 0, 0, 0))],
-            out_specs=[spec(ROWS), spec(KROWS), spec(KROWS),
+            out_specs=[pl.BlockSpec((ROWS, TILE), lambda i, meta: (0, i)),
+                       pl.BlockSpec((KROWS, 2 * TILE), lambda i, meta: (0, i)),
                        pl.BlockSpec((1, 2, 8, 8, TILE), lambda i, meta: (i, 0, 0, 0, 0))],
             scratch_shapes=[
                 pltpu.VMEM((2, KROWS, TILE), bf16),
@@ -274,12 +280,13 @@
                 pltpu.VMEM((16, 8, TILE), f32),
             ],
         ),
-        out_shape=[jax.ShapeDtypeStruct((ROWS, width), bf16),
-                   jax.ShapeDtypeStruct((KROWS, width), bf16),
-                   jax.ShapeDtypeStruct((KROWS, width), bf16),
+        out_shape=[jax.ShapeDtypeStruct((ROWS, pairs * TILE), bf16),
+                   jax.ShapeDtypeStruct((KROWS, 2 * pairs * TILE), bf16),
                    jax.ShapeDtypeStruct((pairs, 2, 8, 8, TILE), f32)],
         compiler_params=pltpu.CompilerParams(dimension_semantics=("arbitrary",),
-                                             vmem_limit_bytes=60 << 20),
+                                             vmem_limit_bytes=56 << 20),
+        cost_estimate=pl.CostEstimate(flops=pairs * 10_000_000_000, bytes_accessed=pairs * 3_000_000,
+                                      transcendentals=pairs * 2 * ROWS * (PLEN + CLEN)),
         name="attention_backward",
     )(meta, q, kv, kv, do, ctx, rest, lse, qaug, kaug, bias, pick)
 
@@ -295,21 +302,6 @@
     if magnitude < 8:
         return base + magnitude
     return base + 8 + sum(1 for edge in THRESHOLDS if magnitude >= edge)
-
-
-def bias_tiles(table):
-    shape = (5, TILE, TILE)
-    offset = (TILE * (lax.broadcasted_iota(jnp.int32, shape, 0) - 2)
-              + lax.broadcasted_iota(jnp.int32, shape, 1) - lax.broadcasted_iota(jnp.int32, shape, 2))
-    columns = table.astype(f32).T[:, :, None, None, None]
-    previous = python_bucket(-200)
-    tiles = jnp.broadcast_to(columns[:, previous], (table.shape[1],) + shape)
-    for n in range(-199, 201):
-        current = python_bucket(n)
-        if current != previous:
-            tiles = jnp.where(offset >= n, columns[:, current], tiles)
-            previous = current
-    return tiles.reshape(table.shape[1], 5 * TILE, TILE)
 
 
 def bias_spread():
@@ -326,7 +318,50 @@
     return spread.reshape(8 * TILE, NB)
 
 
-def placement(me, spans):
+def setup_kernel(meta, limit, table, bias_ref, qaug_ref, kaug_ref, far_ref):
+    head = pl.program_id(0)
+    heads = pl.num_programs(0)
+    near = (lax.broadcasted_iota(jnp.int32, (TILE, TILE), 0)
+            - lax.broadcasted_iota(jnp.int32, (TILE, TILE), 1))
+    for d in range(-2, 3):
+        first, last = TILE * d - TILE + 1, TILE * d + TILE - 1
+        previous = python_bucket(first)
+        tile = jnp.full((TILE, TILE), table[previous * heads + head], f32)
+        for n in range(first + 1, last + 1):
+            current = python_bucket(n)
+            if current != previous:
+                tile = jnp.where(near >= n - TILE * d, table[current * heads + head], tile)
+                previous = current
+        bias_ref[0, (d + 2) * TILE:(d + 3) * TILE, :] = tile
+
+    @pl.when(head == 0)
+    def _():
+        shape = (ROWS, TILE)
+        sub = lax.broadcasted_iota(jnp.int32, shape, 1) & (DH - 1)
+        qaug_ref[...] = jnp.where(sub == lax.broadcasted_iota(jnp.int32, shape, 0) // TILE, 1.0, 0.0).astype(bf16)
+        shape = (KROWS, TILE)
+        key = lax.broadcasted_iota(jnp.int32, shape, 0)
+        sub = lax.broadcasted_iota(jnp.int32, shape, 1) & (DH - 1)
+        kaug = jnp.zeros(shape, f32)
+        for q in range(NQ):
+            first = PLEN + CLEN * meta[NQ + q]
+            hidden = (key >= PLEN) & ((key < first) | (key >= first + limit[q]))
+            kaug = jnp.where(((sub == 2 * q) | (sub == 2 * q + 1)) & hidden, NEGATIVE, kaug)
+        kaug_ref[...] = kaug.astype(bf16)
+        lane = lax.broadcasted_iota(jnp.int32, (8, TILE), 1)
+        for h in range(2):
+            for row in range(16):
+                key_tile = row if row < 8 else 8 + (row - 8) % 4
+                for side in range(2):
+                    out = jnp.zeros((8, TILE), f32)
+                    for q in range(2 * NQ):
+                        apart = key_tile - (meta[q // 2] + q % 2)
+                        is_far = (apart <= -2) if side == 0 else (apart >= 2)
+                        out = jnp.where(lane == q + (DH if h == 0 else 0), jnp.where(is_far, 1.0, 0.0), out)
+                    far_ref[h, side, row] = out
+
+
+def setup(me, spans, table):
     block = NQ * me + jnp.arange(NQ, dtype=jnp.int32)
     prompt = block < PLEN // QB
     cont = jnp.maximum(block - PLEN // QB, 0) // 2
@@ -334,28 +369,32 @@
     tile = jnp.where(prompt, 2 * block, PLEN // TILE + 2 * half)
     slot = jnp.where(prompt, 0, cont - (me - 1))
     chosen = cont[:, None] == jnp.arange(CONT, dtype=jnp.int32)[None, :]
-    limit = jnp.where(prompt, 0, jnp.sum(jnp.where(chosen, spans[None, :], 0), axis=1))
+    limit = jnp.where(prompt, 0, jnp.sum(jnp.where(chosen, spans[None, :], 0), axis=1)).astype(jnp.int32)
     meta = jnp.concatenate([tile, slot]).astype(jnp.int32)
-    shape = (KROWS, TILE)
-    key = lax.broadcasted_iota(jnp.int32, shape, 0)
-    sub = lax.broadcasted_iota(jnp.int32, shape, 1) % DH
-    kaug = jnp.zeros(shape, f32)
-    for q in range(NQ):
-        first = PLEN + CLEN * slot[q]
-        seen = (key < PLEN) | ((key >= first) & (key < first + limit[q]))
-        kaug = jnp.where((sub // 2 == q) & ~seen, NEGATIVE, kaug)
-    shape = (ROWS, TILE)
-    qaug = lax.broadcasted_iota(jnp.int32, shape, 1) % DH == lax.broadcasted_iota(jnp.int32, shape, 0) // TILE
-    shape = (2, 2, 16, 8, TILE)
-    head, side, row, lane = (lax.broadcasted_iota(jnp.int32, shape, a) for a in (0, 1, 2, 4))
-    sub = lane - jnp.where(head == 0, DH, 0)
-    key_tile = jnp.where(row < 8, row, 8 + (row - 8) % 4)
-    query_tile = jnp.full(shape, -1000, jnp.int32)
-    for q in range(2 * NQ):
-        query_tile = jnp.where(sub == q, tile[q // 2] + q % 2, query_tile)
-    apart = key_tile - query_tile
-    far = jnp.where(side == 0, apart <= -2, (apart >= 2) & (apart < 100))
-    return meta, qaug.astype(bf16), kaug.astype(bf16), far.astype(f32)
+    heads = table.shape[1]
+    whole = lambda *shape: pl.BlockSpec(shape, lambda i, *_: (0,) * len(shape))
+    bias, qaug, kaug, far = pl.pallas_call(
+        setup_kernel,
+        grid_spec=pltpu.PrefetchScalarGridSpec(
+            num_scalar_prefetch=3,
+            grid=(heads,),
+            in_specs=[],
+            out_specs=[pl.BlockSpec((1, 5 * TILE, TILE), lambda i, *_: (i, 0, 0)),
+                       whole(ROWS, TILE), whole(KROWS, TILE), whole(2, 2, 16, 8, TILE)],
+        ),
+        out_shape=[jax.ShapeDtypeStruct((heads, 5 * TILE, TILE), f32),
+                   jax.ShapeDtypeStruct((ROWS, TILE), bf16),
+                   jax.ShapeDtypeStruct((KROWS, TILE), bf16),
+                   jax.ShapeDtypeStruct((2, 2, 16, 8, TILE), f32)],
+        compiler_params=pltpu.CompilerParams(dimension_semantics=("arbitrary",)),
+        cost_estimate=pl.CostEstimate(flops=30_000_000, bytes_accessed=5_000_000, transcendentals=0),
+        name="setup",
+    )(meta, limit, table.astype(f32).reshape(-1))
+    return meta, bias, qaug, kaug, far
+
+
+def by_rows(x):
+    return with_layout_constraint(x, Layout(tuple(range(x.ndim))))
 
 
 def rms(rows):
@@ -365,13 +404,6 @@
 def normed_rows(rows, gain):
     rows = rows.astype(f32)
     return (rows * rms(rows) * gain).astype(bf16)
-
-
-def norm_backward(inputs, inverse, gain, d_normed):
-    scaled = inputs * inverse
-    d_gain = jnp.sum(d_normed * scaled, axis=0)
-    d_scaled = d_normed * gain
-    return (inverse * (d_scaled - scaled * jnp.mean(d_scaled * scaled, axis=1, keepdims=True)), d_gain)
 
 
 def contract_rows(left, right):
@@ -393,32 +425,142 @@
     return out
 
 
-def gather_rows(me, own):
+def exchange_rows(me, own):
+    low, high = own[:ROWS // 2], own[ROWS // 2:]
+    return (send(jnp.where(me == 2, high, low), [(0, 1), (1, 0), (2, 3), (3, 2)]),
+            send(jnp.where(me == 0, high, low), [(0, 2), (1, 3)]))
+
+
+def exchange_again(me, own, across, down):
+    low, high = own[:ROWS // 2], own[ROWS // 2:]
+    return (send(jnp.where(me == 0, high, down), [(0, 1), (2, 3), (3, 2)]),
+            send(jnp.where(me == 0, low, across), [(0, 2), (1, 3)]))
+
+
+def seen_rows(me, own, got):
+    across, down, across_again, down_again = got
     mine = [block_of(own, i) for i in range(NQ)]
-    pair = pick_by(me, mine[0], mine[0], mine[2], mine[0])
-    cross = send(pair, [(1, 0), (2, 3), (3, 2)])
-    down = [send(mine[i], [(0, 1)]) for i in range(NQ)]
-    side = [send(pick_by(me, mine[i], mine[0], mine[i], mine[i]), [(0, 2)] + ([(1, 3)] if i == 0 else []))
-            for i in range(NQ)]
-    last = side[0]
-    prompt = []
-    first_relay = send(down[0], [(1, 3)])
-    second_relay = send(side[1], [(2, 3)])
-    half = QB // 2
-    third_a = send(down[2][:half], [(1, 3)])
-    third_b = send(side[2][half:], [(2, 3)])
-    fourth = send(last, [(3, 2)])
-    relays = [first_relay, second_relay, jnp.concatenate([third_a, third_b], axis=0)]
-    for i in range(NQ):
-        prompt.append(pick_by(me, mine[i], down[i], side[i], relays[i]))
-    prompt.append(pick_by(me, cross, mine[0], fourth, last))
+    low, high = own[:ROWS // 2], own[ROWS // 2:]
+    prompt = [
+        pick_by(me, low, across, down_again, down_again),
+        pick_by(me, high, across_again, down, across_again),
+        pick_by(me, across[:QB], mine[0], across_again[:QB], down[:QB]),
+    ]
     slots = [
-        pick_by(me, mine[0], mine[1], mine[0], cross),
+        pick_by(me, mine[0], mine[1], mine[0], across[ROWS // 2 - QB:]),
         pick_by(me, mine[1], mine[2], mine[1], mine[0]),
         pick_by(me, mine[1], mine[1], mine[2], mine[1]),
-        pick_by(me, mine[2], mine[2], cross, mine[2]),
+        pick_by(me, mine[2], mine[2], across[:QB], mine[2]),
     ]
     return jnp.concatenate(prompt + slots, axis=0)
+
+
+def halve(rows, bit, axis, pairs):
+    n, r, c = rows.shape
+    parts = rows.reshape(n, 2, r // 2, c)
+    away = lax.dynamic_index_in_dim(parts, 1 - bit, 1, keepdims=False)
+    kept = lax.dynamic_index_in_dim(parts, bit, 1, keepdims=False)
+    got = lax.ppermute(away, axis, pairs)
+    return (kept.astype(f32) + got.astype(f32)).astype(bf16)
+
+
+def join(rows, bit, axis, pairs):
+    got = lax.ppermute(rows, axis, pairs)
+    return jnp.concatenate([jnp.where(bit == 0, rows, got), jnp.where(bit == 0, got, rows)], axis=-2)
+
+
+def seq_bits(me, order):
+    steps = {"x": (me % 2, [(i, i ^ 1) for i in range(4)]), "y": (me // 2, [(i, i ^ 2) for i in range(4)])}
+    return [steps[name] for name in order]
+
+
+class Owned:
+    def __init__(self, grad, me, order):
+        self.step, self.steps = 0, seq_bits(me, order)
+        self.rows = grad
+        if lax.axis_size("wshard") != 8:
+            self.rows = quarter_sum(lax.psum_scatter(grad, "wshard", scatter_dimension=0, tiled=True))
+            self.step = 5
+
+    def advance(self):
+        place = lax.axis_index("wshard")
+        flip = lambda bit: [(i, i ^ bit) for i in range(8)]
+        step, rows = self.step, self.rows
+        if step == 0:
+            rows = halve(rows.reshape(4, -1, rows.shape[1]), place % 2, "wshard", flip(1))
+        elif step in (1, 2):
+            rows = halve(rows, self.steps[step - 1][0], "seq", self.steps[step - 1][1])
+        elif step == 3:
+            rows = halve(rows.reshape(1, -1, rows.shape[2]), place // 4, "wshard", flip(4))
+        elif step == 4:
+            rows = halve(rows, place // 2 % 2, "wshard", flip(2))[0]
+        self.step, self.rows = step + 1, rows
+
+    def finish(self):
+        while self.step < 5:
+            self.advance()
+        return self.rows
+
+
+def beside(rows, bit, axis, pairs, dim):
+    got = lax.ppermute(rows, axis, pairs)
+    return jnp.stack([jnp.where(bit == 0, rows, got), jnp.where(bit == 0, got, rows)], axis=dim)
+
+
+class Gathered:
+    def __init__(self, me, w_ff, w_out):
+        self.plain = lax.axis_size("wshard") != 8
+        if self.plain:
+            self.state = [lax.all_gather(w, "wshard", axis=0, tiled=True) for w in (w_ff, w_out)]
+            return
+        place = lax.axis_index("wshard")
+        self.core, self.depth = place % 2, place // 2
+        self.n, self.m = w_ff.shape[0] // 4, w_out.shape[0] // 4
+        self.cut = 2 * self.n // 3
+        quarter = jnp.concatenate([lax.dynamic_slice_in_dim(w_ff, me * self.n, self.n, 0),
+                                   lax.dynamic_slice_in_dim(w_out, me * self.m, self.m, 0)], axis=0)
+        self.state = [quarter] + [
+            lax.ppermute(quarter, "wshard", [(i, ((i // 2 + k) % 4) * 2 + i % 2) for i in range(8)])
+            for k in range(1, 4)]
+        self.steps = [seq_bits(me, "xy"), seq_bits(me, "yx")]
+
+    def exchange(self, i):
+        if self.plain:
+            return
+        if i == 0:
+            rows = jnp.stack([pick_by((self.depth - d) % 4, *self.state) for d in range(4)])
+            self.state = [rows[:, :self.cut], rows[:, self.cut:]]
+        self.state = [beside(rows, steps[i][0], "seq", steps[i][1], dim)
+                      for rows, steps, dim in zip(self.state, self.steps, (1, 1 + i))]
+
+    def cores(self):
+        if not self.plain:
+            self.state = [beside(rows, self.core, "wshard", [(i, i ^ 1) for i in range(8)], 1)
+                          for rows in self.state]
+
+    def tie(self, others):
+        others, self.state = lax.optimization_barrier((others, self.state))
+        return others
+
+    def whole(self):
+        if self.plain:
+            return self.state
+        first, last = self.state
+        c = first.shape[-1]
+        keep = self.n - self.cut
+        w_ff = jnp.concatenate([first, last[..., :keep, :]], axis=-2).reshape(32 * self.n, c)
+        return w_ff, last[..., keep:, :].reshape(32 * self.m, c)
+
+
+def quarter_sum(rows):
+    parts = lax.all_to_all(rows.reshape(4, -1, rows.shape[1]), "seq", split_axis=0, concat_axis=0, tiled=True)
+    return jnp.sum(parts.astype(f32), axis=0).astype(bf16)
+
+
+def join_quarters(rows, me):
+    steps = seq_bits(me, "xy")
+    rows = beside(rows, *steps[0][:1], "seq", steps[0][1], 0)
+    return beside(rows, steps[1][0], "seq", steps[1][1], 0).reshape((4,) + rows.shape[1:])
 
 
 def sum_prompt(me, partial):
@@ -444,9 +586,18 @@
     return jnp.concatenate(rows, axis=0)
 
 
+CHUNKS = (4, 2)
+
+
+def interleave(key_part, value_part):
+    r, w = key_part.shape
+    both = jnp.stack([key_part.reshape(r, w // TILE, TILE), value_part.reshape(r, w // TILE, TILE)], axis=2)
+    return both.reshape(r, 2 * w)
+
+
 def local(tokens, teacher, lengths, w_query, w_key, w_value, w_out, w_in, w_ff, gain_attn, gain_ff, bias_table):
     me = lax.axis_index("seq")
-    own = tokens[0]
+    own = by_rows(tokens[0])
     inputs = own.astype(f32)
     targets = teacher[0].astype(f32)
     spans = lengths[0]
@@ -456,22 +607,34 @@
     def gather(w):
         return lax.all_gather(w, "wshard", axis=0, tiled=True)
 
-    full_qkv = gather(jnp.concatenate([w_query, w_key, w_value], axis=1))
-    full_out, full_in, full_ff = gather(w_out), gather(w_in), gather(w_ff)
-    gains = gather(jnp.stack([gain_attn, gain_ff], axis=1)).astype(f32).T
+    w_kv = interleave(w_key, w_value)
+    gain_columns = jnp.pad(jnp.stack([gain_attn, gain_ff], axis=1), ((0, 0), (0, TILE - 2)))
+    first = gather(jnp.concatenate([w_query, w_kv, gain_columns], axis=1))
+    full_query, full_kv = first[:, :width], first[:, width:3 * width]
+    gains = first[:, 3 * width:3 * width + 2].astype(f32).T
     gain_one, gain_two = gains[0], gains[1]
-    meta, qaug, kaug, far = placement(me, spans)
-    bias = bias_tiles(bias_table)
-    seen = gather_rows(me, own)
+    gathered = Gathered(me, w_ff, w_out)
+    full_in = gather(w_in)
+    got = exchange_rows(me, own)
+    got, spans, table = gathered.tie((got, spans, bias_table))
+    got = got + exchange_again(me, own, *got)
+    gathered.exchange(0)
+    prepared = setup(me, spans, table)
     inverse_one = rms(inputs)
-    normed_own = (inputs * inverse_one * gain_one).astype(bf16)
-    normed_seen = normed_rows(seen, gain_one)
-    queries = jnp.dot(normed_own, full_qkv[:, :width], preferred_element_type=f32).astype(bf16)
-    keys_values = jnp.dot(normed_seen, full_qkv[:, width:], preferred_element_type=f32).astype(bf16)
-    context, rest, lse = attention_forward(meta, queries, keys_values, qaug, kaug, bias)
-    middle = inputs + jnp.dot(context, full_out, preferred_element_type=f32)
+    got, prepared, inverse_one = gathered.tie((got, prepared, inverse_one))
+    meta, bias, qaug, kaug, far = prepared
+    gathered.exchange(1)
+    normed_own = by_rows((inputs * inverse_one * gain_one).astype(bf16))
+    normed_seen = by_rows(normed_rows(by_rows(seen_rows(me, own, got)), gain_one))
+    queries = jnp.dot(normed_own, full_query, preferred_element_type=f32).astype(bf16)
+    keys_values = jnp.dot(normed_seen, full_kv, preferred_element_type=f32).astype(bf16)
+    queries, keys_values = gathered.tie((queries, keys_values))
+    gathered.cores()
+    context, rest, lse = gathered.tie(attention_forward(meta, queries, keys_values, qaug, kaug, bias, 0, pairs))
+    full_ff, full_out = gathered.whole()
+    middle = by_rows(inputs + jnp.dot(context, full_out, preferred_element_type=f32))
     inverse_two = rms(middle)
-    normed_two = (middle * inverse_two * gain_two).astype(bf16)
+    normed_two = by_rows((middle * inverse_two * gain_two).astype(bf16))
     hidden_act = jnp.maximum(jnp.dot(normed_two, full_in, preferred_element_type=f32), 0.0).astype(bf16)
     final_rows = middle + jnp.dot(hidden_act, full_ff, preferred_element_type=f32)
     local_rows = inputs.shape[0]
@@ -483,57 +646,121 @@
     row_count = PLEN + jnp.sum(spans).astype(f32)
     factor = (PLEN + CONT * CLEN) / row_count
     d_final = jnp.where(valid_rows[:, None], factor * (final_rows - targets), 0.0)
-    d_branch_two = d_final.astype(bf16)
-    grad_ff = contract_rows(hidden_act, d_branch_two)
+    d_final = by_rows(d_final)
+    d_branch_two = by_rows(d_final.astype(bf16))
+
+    def owners(g):
+        return lax.psum_scatter(g, "wshard", scatter_dimension=0, tiled=True)
+
+    size = gain_attn.shape[0]
+    owned_ff = Owned(contract_rows(hidden_act, d_branch_two).astype(bf16), me, "yx")
+    owned_ff.advance()
     d_pre = jnp.where(hidden_act > 0, dot_nt(d_branch_two, full_ff), 0.0).astype(bf16)
-    grad_in = contract_rows(normed_two, d_pre)
-    d_middle, grad_gain2 = norm_backward(middle, inverse_two, gain_two, dot_nt(d_pre, full_in))
-    d_middle = d_final + d_middle
-    d_branch_one = d_middle.astype(bf16)
-    grad_out = contract_rows(context, d_branch_one)
+    grad_in = contract_rows(normed_two, d_pre).astype(bf16)
+    d_normed_two = by_rows(dot_nt(d_pre, full_in))
+    d_normed_two, owned_ff.rows = lax.optimization_barrier((d_normed_two, owned_ff.rows))
+    owned_ff.advance()
+    scaled_two = middle * inverse_two
+    d_scaled_two = d_normed_two * gain_two
+    d_middle = d_final + inverse_two * (
+        d_scaled_two - scaled_two * jnp.mean(d_scaled_two * scaled_two, axis=1, keepdims=True))
+    d_middle = by_rows(d_middle)
+    d_branch_one = by_rows(d_middle.astype(bf16))
+    grad_out = contract_rows(context, d_branch_one).astype(bf16)
     d_context = dot_nt(d_branch_one, full_out).astype(bf16)
-    d_queries, d_keys, d_values, near = attention_backward(
-        meta, queries, keys_values, d_context, context, rest, lse, qaug, kaug, bias, far)
-    d_kv = sum_prompt(me, jnp.concatenate([d_keys, d_values], axis=1))
-    prompt_start = jnp.array(OWNER_BLOCK, jnp.int32)[me] * QB
-    normed_sum = jnp.concatenate([lax.dynamic_slice_in_dim(normed_seen, prompt_start, QB, 0), normed_own], axis=0)
-    d_qkv = jnp.concatenate([
-        jnp.concatenate([jnp.zeros((QB, width), bf16), d_queries], axis=0), d_kv], axis=1)
-    grad_qkv = contract_rows(normed_sum, d_qkv)
-    f_rows = dot_nt(d_qkv, full_qkv)
-    f_first = f_rows[:QB]
-    f_sent = f_first.astype(bf16)
-    from_two = send(f_sent, [(2, 0)]).astype(f32)
-    from_three = send(f_sent, [(3, 0)]).astype(f32)
-    f_own = f_rows[QB:] + jnp.concatenate([jnp.where(me < 2, f_first, 0.0), from_two, from_three], axis=0)
-    d_inputs, grad_gain1 = norm_backward(inputs, inverse_one, gain_one, f_own)
-    d_tokens = d_middle + d_inputs
-
-    def reduce(g):
-        share = lax.psum_scatter(g.astype(bf16), "wshard", scatter_dimension=0, tiled=True)
-        return lax.psum(share, "seq").astype(f32)
-
-    share_ff, share_in, share_out, share_qkv = reduce(grad_ff), reduce(grad_in), reduce(grad_out), reduce(grad_qkv)
+    share_in = owners(grad_in)
+    d_context, grad_out = lax.optimization_barrier((d_context, grad_out))
+
+    starts = [sum(CHUNKS[:i]) for i in range(len(CHUNKS))]
+    cuts = [(starts[i] * TILE, (starts[i] + CHUNKS[i]) * TILE) for i in range(len(CHUNKS))]
+
+    def backward(meta, i):
+        return attention_backward(meta, queries, keys_values, d_context, context, rest, lse, qaug, kaug, bias, far,
+                                  starts[i], CHUNKS[i])
+
+    def weight_grad(d_q, d_kv):
+        return jnp.concatenate([by_rows(contract_rows(normed_own, d_q).astype(bf16)),
+                                by_rows(contract_rows(normed_seen, d_kv).astype(bf16))], axis=1)
+
+    def back_to_rows(i, d_q, d_kv):
+        lo, hi = cuts[i]
+        return by_rows(dot_nt(d_q, full_query[:, lo:hi])), by_rows(dot_nt(d_kv, full_kv[:, 2 * lo:2 * hi]))
+
+    first = backward(meta, 0)
+    meta, first, owned_ff.rows, share_in = lax.optimization_barrier((meta, first, owned_ff.rows, share_in))
+    owned_ff.advance()
+    grad_first = jnp.concatenate([weight_grad(*first[:2]), grad_out], axis=1)
+    f_first = back_to_rows(0, *first[:2])
+    meta, grad_first, f_first = lax.optimization_barrier((meta, grad_first, f_first))
+    share_first = owners(grad_first)
+    second = backward(meta, 1)
+    second, owned_ff.rows, share_first = lax.optimization_barrier((second, owned_ff.rows, share_first))
+    grad_second = weight_grad(*second[:2])
     heads = bias_table.shape[1]
-    bias_local = jnp.dot(jnp.sum(near, axis=3).reshape(heads, 8 * TILE), jnp.asarray(bias_spread()),
-                         precision=lax.Precision.HIGHEST)
-    small = jnp.concatenate([grad_gain1, grad_gain2, bias_local.reshape(-1)])
-    small = lax.psum(small, ("seq", "wshard"))
-    mine = lax.axis_index("wshard")
-    part = gain_attn.shape[0]
-    gain_share = [lax.dynamic_slice_in_dim(small, i * width + mine * part, part) for i in range(2)]
-    bias_grad = small[2 * width:].reshape(heads, NB).T
+    near = jnp.sum(jnp.concatenate([first[2], second[2]], axis=0), axis=3).reshape(heads, 8 * TILE)
+    bias_local = jnp.dot(near, jnp.asarray(bias_spread()), precision=lax.Precision.HIGHEST).reshape(1, -1)
+    bias_top = bias_local.astype(bf16)
+    bias_rest = (bias_local - bias_top.astype(f32)).astype(bf16)
+    n_bias = bias_local.shape[1]
+    n_last = grad_second.shape[1]
+    bias_rows = jnp.pad(jnp.concatenate([bias_top, bias_rest], axis=1), ((0, 7), (0, n_last - 2 * n_bias)))
+    blocks = grad_second.reshape(-1, size, n_last)
+    bias_rows = jnp.broadcast_to(bias_rows[None], (blocks.shape[0],) + bias_rows.shape)
+    last = jnp.concatenate([blocks, bias_rows], axis=1).reshape(-1, n_last)
+    share_last = owners(last)
+    f_second = back_to_rows(1, *second[:2])
+    f_query = f_first[0] + f_second[0]
+    f_summed = by_rows(sum_prompt(me, by_rows((f_first[1] + f_second[1]).astype(bf16))))
+    quarter_ff = owned_ff.finish()
+    shares_out = jnp.concatenate([share.reshape(-1, width) for share in (share_in, share_first)], axis=0)
+    quarter_out = quarter_sum(shares_out)
+    share_last, f_summed, quarter_ff, quarter_out = lax.optimization_barrier(
+        (share_last, f_summed, quarter_ff, quarter_out))
+    quarters = [quarter_ff, quarter_out]
+    f_block = f_summed[:QB]
+    from_two = send(f_block, [(2, 0)])
+    from_three = send(f_block, [(3, 0)])
+    f_own = f_query + (f_summed[QB:] + jnp.concatenate(
+        [jnp.where(me < 2, f_block, jnp.zeros_like(f_block)), from_two, from_three], axis=0)).astype(f32)
+    scaled_one = inputs * inverse_one
+    d_scaled_one = f_own * gain_one
+    d_tokens = d_middle + inverse_one * (
+        d_scaled_one - scaled_one * jnp.mean(d_scaled_one * scaled_one, axis=1, keepdims=True))
+
+    size = gain_attn.shape[0]
+    n_quarter = quarter_ff.shape[0]
+    early = join_quarters(jnp.concatenate(quarters, axis=0), me)
+    share_ff = early[:, :n_quarter].reshape(-1, width).astype(f32)
+    others = early[:, n_quarter:].reshape(-1, width).astype(f32)
+    n_in = share_in.shape[0] * share_in.shape[1] // width
+    share_in = others[:n_in].reshape(size, -1)
+    share_first = others[n_in:].reshape(size, -1)
+    share_out = share_first[:, -width:]
+    late = join_quarters(quarter_sum(share_last.reshape(-1, width)), me).reshape(-1, n_last).astype(f32)
+    shares = [share_first[:, :-width], late[:size]]
+    bias_grad = (late[size, :n_bias] + late[size, n_bias:2 * n_bias]).reshape(heads, NB).T
+    share_query = jnp.concatenate(
+        [share[:, :count * TILE] for share, count in zip(shares, CHUNKS)], axis=1)
+    share_kv = jnp.concatenate(
+        [share[:, count * TILE:] for share, count in zip(shares, CHUNKS)], axis=1)
+    share_kv = share_kv.reshape(share_kv.shape[0], pairs, 2, TILE)
+    share_key = share_kv[:, :, 0].reshape(-1, width)
+    share_value = share_kv[:, :, 1].reshape(-1, width)
+    gain_grad_one = (jnp.sum(share_query * w_query.astype(f32), axis=1)
+                     + jnp.sum(share_key * w_key.astype(f32), axis=1)
+                     + jnp.sum(share_value * w_value.astype(f32), axis=1)) / gain_attn.astype(f32)
+    gain_grad_two = jnp.sum(share_in * w_in.astype(f32), axis=1) / gain_ff.astype(f32)
     return (
         final_rows.astype(bf16)[None],
         d_tokens[None],
-        share_qkv[:, :width],
-        share_qkv[:, width:2 * width],
-        share_qkv[:, 2 * width:],
+        share_query,
+        share_key,
+        share_value,
         share_out,
         share_in,
         share_ff,
-        gain_share[0],
-        gain_share[1],
+        gain_grad_one,
+        gain_grad_two,
         bias_grad,
     )
 

time: 599 us -> 469 us (0.78)
  waiting for transfers between devices: 197 us -> 105 us
  blocking collectives: 50 us -> 0 us
  starting transfers between devices: 30.5 us -> 52.7 us
  Pallas kernels: 97.6 us -> 109 us
  other arithmetic: 67.6 us -> 56.6 us
    reduce_scatter x4 -> x3, waiting for transfers between devices: 117 us -> 29.5 us  [owners(): return lax.psum_scatter(g, 'wshard', scatter_dimension=0, tiled=True)]
    ppermute x0 -> x18, waiting for transfers between devices: none -> 58.3 us  [the longest x10 42.1 us: beside(): got = lax.ppermute(rows, axis, pairs)]
    ppermute x18 -> x10, waiting for transfers between devices: 62.3 us -> 14.8 us  [send(): return lax.ppermute(rows, 'seq', pairs)]
    psum x1 -> x0, blocking collectives: 38 us -> none  [local(): small = lax.psum(small, ('seq', 'wshard'))]
    ppermute x0 -> x18, starting transfers between devices: none -> 24.9 us  [the longest x10 13.9 us: beside(): got = lax.ppermute(rows, axis, pairs)]
    select_n x8 -> x7, other arithmetic: 22.2 us -> 4.28 us  [the longest x1 1.13 us: exchange_again(): jnp.where(me == 0, low, across)]
    another operation x0 -> x23, other arithmetic: none -> 13.3 us  [the longest x19 11.2 us: beside(): jnp.stack([jnp.where(bit == 0, rows, got), jnp.where(bit == 0, got, rows)...]
    convert_element_type x10 -> x8, other arithmetic: 18.6 us -> 5.35 us  [the longest x4 3.96 us: halve(): return (kept.astype(f32) + got.astype(f32)).astype(bf16)]
  transfers between devices with their start and end apart: 27 -> 35, of which waited for: 10 -> 13; matrix products, arithmetic and copies ran while one was open for 24% -> 21% of each run, Pallas kernels for 6% -> 24%
where the time goes in v2:
time: 469 us; the launch traced here: 464 us
  Pallas kernels  109 us (23%)
  waiting for transfers between devices  105 us (22%)
  matrix products  88 us (19%)
  other arithmetic  56.6 us (12%)
  starting transfers between devices  52.7 us (11%)
  local copies, waits for them, and re-layouts  34.1 us (7%)
  between operations  18.8 us (4%)
    pallas_call x2, Pallas kernels, attention_backward(): pl.pallas_call(backward_kernel, grid_spec=pltpu.PrefetchScalarGridSpec(nu...  68.2 us
    ppermute x10, waiting for transfers between devices, beside(): got = lax.ppermute(rows, axis, pairs)  42.1 us
    dot_general x7, matrix products, dot_nt(): lax.dot_general(a, b, (((1,), (1,)), ((), ())), preferred_element_type=f32)  34.3 us
    pallas_call x1, Pallas kernels, attention_forward(): pl.pallas_call(forward_kernel, grid_spec=pltpu.PrefetchScalarGridSpec(num...  33.7 us
    reduce_scatter x3, waiting for transfers between devices, owners(): return lax.psum_scatter(g, 'wshard', scatter_dimension=0, tiled=True)  29.5 us
    dot_general x7, matrix products, contract_rows(): lax.dot_general(left, right, (((0,), (0,)), ((), ())), preferred_element_...  27.7 us
    ppermute x10, starting transfers between devices, send(): return lax.ppermute(rows, 'seq', pairs)  19 us
    ppermute x10, waiting for transfers between devices, send(): return lax.ppermute(rows, 'seq', pairs)  14.8 us
  transfers between devices with their start and end apart: 35, of which 13 were waited for; matrix products, arithmetic and copies ran while one was open for 21% of the time, Pallas kernels for 24%

profile of v2, /device:TPU:0, one launch (start us, length us, event | category | flops | bytes accessed | tf_op | source)
XLA Modules:
  0.0 464.3 jit_solution(4828554140646644519)
XLA Ops:
  22.2 3.4 collective-permute-start.1
  26.9 11.1 %collective-permute-done.3 = bf16[120,768]{1,0:T(8,128)(2,1)S(1)} collective-permute-done((bf16[120,768]{1,0:T(8,128)(2,1)S(1)}, bf16[120,768]{1,0:T(8,128)(2,1)S(1)}, u32[]{:S(2)}, u32[]{:S(2)}) %collective-permute-start.3) | collective-permute-done | bytes 184352 | tf_op jit(solution)/shard_map/ppermute | solution.py:523
  44.1 4.2 collective-permute-start.5
  54.3 7.5 %setup.1 = (f32[12,640,128]{2,1,0:T(8,128)}, bf16[768,128]{1,0:T(8,128)(2,1)}, bf16[2048,128]{1,0:T(8,128)(2,1)}, f32[2,2,16,8,128]{4,3,2,1,0:T(8,128)}) custom-call(s32[6]{0:T(128)} %pad_add_fusion.meta, s32[3]{0:T(128)} %broadcast_select_fusion.6.limit, f32[384]{0:T(512)} %reshape.282.table), custom_call_target="tpu_custom_call" | custom-call | flops 30000000 | bytes 5000000 | tf_op jit(solution)/shard_map/setup/pallas_call | solution.py:376
  63.9 4.6 collective-permute-done.7
  79.6 12.1 %collective-permute-done.10 = bf16[4,2,56,768]{3,2,1,0:T(8,128)(2,1)} collective-permute-done((bf16[4,2,56,768]{3,2,1,0:T(8,128)(2,1)}, bf16[4,2,56,768]{3,2,1,0:T(8,128)(2,1)}, u32[]{:S(2)}, u32[]{:S(2)}) %collective-permute-start.10) | collective-permute-done | bytes 688160 | tf_op jit(solution)/shard_map/ppermute | solution.py:506
  97.1 3.6 convolution_convert_fusion.6.q_ref
  100.8 7.0 %convolution_convert_fusion.k_ref.v_ref = bf16[2048,1536]{1,0:T(8,128)(2,1)} fusion(bf16[768,2432]{1,0:T(8,128)(2,1)S(1)} %copy-done.25, bf16[2048,768]{1,0:T(8,128)(2,1)S(1)} %copy-done.14, f32[768]{0:T(1024)S(1)} %get-tuple-element.144, f32[2048]{0:T(1024)S(1)} %add_rsqrt_fusion), kind=kOutput, calls=%fused_computation.4 | convolution fusion | flops 4841275392 | bytes 11808768 | tf_op jit(solution)/shard_map/dot_general | solution.py:630
  108.4 33.7 %attention_forward.1 = (bf16[768,768]{1,0:T(8,128)(2,1)}, bf16[768,768]{1,0:T(8,128)(2,1)}, f32[6,2,768]{2,1,0:T(2,128)}) custom-call(s32[6]{0:T(128)} %pad_add_fusion.meta, bf16[768,768]{1,0:T(8,128)(2,1)} %convolution_convert_fusion.6.q_ref, bf16[2048,1536]{1,0:T(8,128)(2,1)} %convolution_convert_fusion.k_ref.v_ref, ...), custom_call_target="tpu_custom_call" | custom-call | flops 30000001024 | bytes 12000000 | tf_op jit(solution)/shard_map/attention_forward/pallas_call | solution.py:96
  150.0 7.1 %maximum_convert_fusion = bf16[768,3072]{1,0:T(8,128)(2,1)S(1)} fusion(bf16[768,3072]{1,0:T(8,128)(2,1)} %all-gather.5.cloned.1.call-done, f32[768,768]{1,0:T(8,128)} %get-tuple-element.198, f32[768]{0:T(1024)S(1)} %get-tuple-element.143, f32[768]{0:T(1024)S(1)} %add_rsqrt_fusion.1), kind=kOutput, calls=%fused_computation.1 | convolution fusion | flops 3630366720 | bytes 11802624 | tf_op jit(solution)/shard_map/dot_general | solution.py:638
  157.1 5.3 %fusion.20 = (bf16[768,768]{1,0:T(8,128)(2,1)S(1)}, f32[768,768]{1,0:T(8,128)}) fusion(bf16[1,768,768]{2,1,0:T(8,128)(2,1)S(1)} %copy-done.20, f32[]{:T(128)S(6)} %div.81, pred[768]{0:T(1024)(128)(4,1)S(1)} %fusion.51, f32[768,768]{1,0:T(8,128)S(1)} %copy-done.6, bf16[768,3072]{1,0:T(8,128)(2,1)S(1)} %maximum_convert_fusion, bf16[3072,768]{1,0:T(8,128)(2,1)S(1)} %bitcast.180), kind=kOutput, calls=%fused_computation.59 | convolution fusion | flops 3627417600 | bytes 16515844 | tf_op jit(solution)/shard_map/dot_general | solution.py:639
  162.4 4.1 select_convert_fusion
  168.7 5.9 %convolution_convert_fusion.1 = bf16[768,3072]{1,0:T(8,128)(2,1)} fusion(bf16[768,3072]{1,0:T(8,128)(2,1)S(1)} %select_convert_fusion, f32[768,768]{1,0:T(8,128)S(1)} %copy-done.6, f32[768]{0:T(1024)S(1)} %get-tuple-element.143, f32[768]{0:T(1024)S(1)} %add_rsqrt_fusion.1), kind=kOutput, calls=%fused_computation.9 | convolution fusion | flops 3628007424 | bytes 11802624 | tf_op jit(solution)/shard_map/dot_general | solution.py:410
  174.9 6.6 %convolution_convert_fusion.2 = bf16[3072,768]{1,0:T(8,128)(2,1)S(1)} fusion(bf16[768,3072]{1,0:T(8,128)(2,1)} %copy-done.48, bf16[768,768]{1,0:T(8,128)(2,1)} %copy-done.49), kind=kOutput, calls=%fused_computation.10 | convolution fusion | flops 3626237952 | bytes 10616832 | tf_op jit(solution)/shard_map/dot_general | solution.py:410
  184.4 7.3 %fusion.65 = f32[768,768]{1,0:T(8,128)S(1)} fusion(bf16[768,3072]{1,0:T(8,128)(2,1)} %copy-done.44, bf16[768,3072]{1,0:T(8,128)(2,1)} %all-gather.5.cloned.1.call-done), kind=kOutput, calls=%fused_computation.207 | convolution fusion | flops 3623878656 | bytes 11796480 | tf_op jit(solution)/shard_map/dot_general | solution.py:26
  203.4 44.2 %attention_backward.2 = (bf16[768,512]{1,0:T(8,128)(2,1)}, bf16[2048,1024]{1,0:T(8,128)(2,1)}, f32[4,2,8,8,128]{4,3,2,1,0:T(8,128)}) custom-call(s32[6]{0:T(128)} %pad_add_fusion.meta, bf16[768,768]{1,0:T(8,128)(2,1)} %convolution_convert_fusion.6.q_ref, bf16[2048,1536]{1,0:T(8,128)(2,1)} %convolution_convert_fusion.k_ref.v_ref, ...), custom_call_target="tpu_custom_call" | custom-call | flops 40000000000 | bytes 12000000 | tf_op jit(solution)/shard_map/attention_backward/pallas_call | solution.py:258
  248.0 6.9 %convolution_convert_fusion.3 = bf16[768,1024]{1,0:T(8,128)(2,1)S(1)} fusion(bf16[2048,1024]{1,0:T(8,128)(2,1)} %get-tuple-element.120, bf16[2048,768]{1,0:T(8,128)(2,1)} %copy-done.13, f32[768]{0:T(1024)S(1)} %get-tuple-element.144, f32[2048]{0:T(1024)S(1)} %add_rsqrt_fusion), kind=kOutput, calls=%fused_computation.42 | convolution fusion | flops 3228303360 | bytes 8924160 | tf_op jit(solution)/shard_map/dot_general | solution.py:410
  258.1 3.6 fusion.25
  261.6 8.8 %fusion.18 = f32[2048,768]{1,0:T(8,128)} fusion(bf16[2048,1024]{1,0:T(8,128)(2,1)} %get-tuple-element.120, bf16[768,2432]{1,0:T(8,128)(2,1)} %all-gather.3.cloned.1.call-done), kind=kOutput, calls=%fused_computation.44 | convolution fusion | flops 3221225472 | bytes 12058624 | tf_op jit(solution)/shard_map/dot_general | solution.py:26
  272.1 24.0 %attention_backward.3 = (bf16[768,256]{1,0:T(8,128)(2,1)}, bf16[2048,512]{1,0:T(8,128)(2,1)}, f32[2,2,8,8,128]{4,3,2,1,0:T(8,128)}) custom-call(s32[6]{0:T(128)} %pad_add_fusion.meta, bf16[768,768]{1,0:T(8,128)(2,1)} %convolution_convert_fusion.6.q_ref, bf16[2048,1536]{1,0:T(8,128)(2,1)} %convolution_convert_fusion.k_ref.v_ref, ...), custom_call_target="tpu_custom_call" | custom-call | flops 20000000000 | bytes 6000000 | tf_op jit(solution)/shard_map/attention_backward/pallas_call | solution.py:258
  296.3 29.5 %reduce-scatter.6.cloned.1.call-done = bf16[96,2304]{1,0:T(8,128)(2,1)} async-done(((bf16[768,2304]{1,0:T(8,128)(2,1)}), bf16[96,2304]{1,0:T(8,128)(2,1)}) %reduce-scatter.6.cloned.1.call-update) | async-done | bytes 442384 | tf_op jit(solution)/shard_map/reduce_scatter | solution.py:653
  327.5 4.5 convolution_convert_fusion.7
  334.7 5.6 %add_convert_fusion = bf16[2048,768]{1,0:T(8,128)(2,1)S(1)} fusion(f32[2048,768]{1,0:T(8,128)} %fusion.18, bf16[2048,512]{1,0:T(8,128)(2,1)} %get-tuple-element.130, bf16[768,2432]{1,0:T(8,128)(2,1)} %all-gather.3.cloned.1.call-done), kind=kOutput, calls=%fused_computation.8 | convolution fusion | flops 1613758464 | bytes 12320768 | tf_op jit(solution)/shard_map/dot_general | solution.py:26
  348.3 5.0 %all-to-all-start = ((bf16[4,168,768]{2,1,0:T(8,128)(2,1)}), bf16[4,168,768]{2,1,0:T(8,128)(2,1)S(1)}, u32[]{:S(2)}, u32[]{:S(2)}) async-start(bf16[4,168,768]{2,1,0:T(8,128)(2,1)} %bitcast.184), calls=%async_computation.3 | async-start | bytes 2064384 | tf_op jit(solution)/shard_map/all_to_all | solution.py:556
  356.1 3.4 constant_dynamic-slice_fusion.2
  365.2 3.3 collective-permute-done.21
  369.8 7.9 %collective-permute-done.18 = bf16[256,768]{1,0:T(8,128)(2,1)} collective-permute-done((bf16[256,768]{1,0:T(8,128)(2,1)}, bf16[256,768]{1,0:T(8,128)(2,1)}, u32[]{:S(2)}, u32[]{:S(2)}) %collective-permute-start.18) | collective-permute-done | bytes 393248 | tf_op jit(solution)/shard_map/ppermute | solution.py:418
  377.7 7.0 %collective-permute-done.17 = bf16[256,768]{1,0:T(8,128)(2,1)} collective-permute-done((bf16[256,768]{1,0:T(8,128)(2,1)}, bf16[256,768]{1,0:T(8,128)(2,1)}, u32[]{:S(2)}, u32[]{:S(2)}) %collective-permute-start.17) | collective-permute-done | bytes 393248 | tf_op jit(solution)/shard_map/ppermute | solution.py:418
  389.1 3.4 all-to-all-start.1
  401.9 7.0 %collective-permute-start.27 = (bf16[2,26,768]{2,1,0:T(8,128)(2,1)S(1)}, bf16[2,26,768]{2,1,0:T(8,128)(2,1)S(1)}, u32[]{:S(2)}, u32[]{:S(2)}) collective-permute-start(bf16[2,26,768]{2,1,0:T(8,128)(2,1)S(1)} %pad_maximum_fusion.20), channel_id=1, source_target_pairs={{0,16},{8,24},{16,0},{24,8},{1,17},{9,25},{17,1},{25,9},{2,18},{10... | collective-permute-start | bytes 239624 | tf_op jit(solution)/shard_map/ppermute | solution.py:506
  409.7 8.0 %collective-permute-done.27 = bf16[2,26,768]{2,1,0:T(8,128)(2,1)S(1)} collective-permute-done((bf16[2,26,768]{2,1,0:T(8,128)(2,1)S(1)}, bf16[2,26,768]{2,1,0:T(8,128)(2,1)S(1)}, u32[]{:S(2)}, u32[]{:S(2)}) %collective-permute-start.27) | collective-permute-done | bytes 79904 | tf_op jit(solution)/shard_map/ppermute | solution.py:506
  429.8 14.9 %collective-permute-done.25 = bf16[2,264,768]{2,1,0:T(8,128)(2,1)S(1)} collective-permute-done((bf16[2,264,768]{2,1,0:T(8,128)(2,1)S(1)}, bf16[2,264,768]{2,1,0:T(8,128)(2,1)S(1)}, u32[]{:S(2)}, u32[]{:S(2)}) %collective-permute-start.25) | collective-permute-done | bytes 811040 | tf_op jit(solution)/shard_map/ppermute | solution.py:506
  (305 shorter events, 134.8 us)
Async XLA Ops:
  7.2 88.5 %all-gather.3.cloned.1.call-start = ((), (), s32[]{:S(2)}) async-start(), calls=%async_computation.5 | async-start | bytes 4202496 | tf_op jit(solution)/shard_map/all_gather | solution.py:608
  11.9 138.0 %all-gather.5.cloned.1.call-start = ((), (), s32[]{:S(2)}) async-start(), calls=%async_computation.6 | async-start | bytes 5308416 | tf_op jit(solution)/shard_map/all_gather | solution.py:608
  12.8 14.1 %collective-permute-start.2 = (bf16[120,768]{1,0:T(8,128)(2,1)S(1)}, bf16[120,768]{1,0:T(8,128)(2,1)S(1)}, u32[]{:S(2)}, u32[]{:S(2)}) collective-permute-start(bf16[120,768]{1,0:T(8,128)(2,1)S(1)} %pad_maximum_fusion.19), channel_id=1, source_target_pairs={{0,2},{1,3},{2,4},{3,5},{4,6},{5,7},{6,0},{7,1},{8,10},{9,11},{10,... | collective-permute-start | bytes 552968 | tf_op jit(solution)/shard_map/ppermute | solution.py:523
  15.9 22.1 %collective-permute-start.3 = (bf16[120,768]{1,0:T(8,128)(2,1)S(1)}, bf16[120,768]{1,0:T(8,128)(2,1)S(1)}, u32[]{:S(2)}, u32[]{:S(2)}) collective-permute-start(bf16[120,768]{1,0:T(8,128)(2,1)S(1)} %pad_maximum_fusion.19), channel_id=1, source_target_pairs={{0,4},{1,5},{2,6},{3,7},{4,0},{5,1},{6,2},{7,3},{8,12},{9,13},{10,... | collective-permute-start | bytes 552968 | tf_op jit(solution)/shard_map/ppermute | solution.py:523
  18.4 19.5 %collective-permute-start.4 = (bf16[120,768]{1,0:T(8,128)(2,1)S(1)}, bf16[120,768]{1,0:T(8,128)(2,1)}, u32[]{:S(2)}, u32[]{:S(2)}) collective-permute-start(bf16[120,768]{1,0:T(8,128)(2,1)S(1)} %pad_maximum_fusion.19), channel_id=1, source_target_pairs={{0,6},{1,7},{2,0},{3,1},{4,2},{5,3},{6,4},{7,5},{8,14},{9,15},{10,... | collective-permute-start | bytes 552968 | tf_op jit(solution)/shard_map/ppermute | solution.py:523
  20.7 17.3 %collective-permute-start = (bf16[384,768]{1,0:T(8,128)(2,1)}, bf16[384,768]{1,0:T(8,128)(2,1)S(1)}, u32[]{:S(2)}, u32[]{:S(2)}) collective-permute-start(bf16[384,768]{1,0:T(8,128)(2,1)} %get-tuple-element.176), channel_id=1, source_target_pairs={{0,8},{8,0},{16,24},{24,16},{1,9},{9,1},{17,25},{25,17},{2,10},{10... | collective-permute-start | bytes 1769480 | tf_op jit(solution)/shard_map/ppermute | solution.py:418
  22.2 15.8 %collective-permute-start.1 = (bf16[384,768]{1,0:T(8,128)(2,1)S(1)}, bf16[384,768]{1,0:T(8,128)(2,1)S(1)}, u32[]{:S(2)}, u32[]{:S(2)}) collective-permute-start(bf16[384,768]{1,0:T(8,128)(2,1)S(1)} %get-tuple-element.175), channel_id=1, source_target_pairs={{0,16},{8,24},{1,17},{9,25},{2,18},{10,26},{3,19},{11,27},{4,20},{... | collective-permute-start | bytes 1769480 | tf_op jit(solution)/shard_map/ppermute | solution.py:418
  25.7 222.3 %reduce-scatter.4.cloned.1.call-start = ((), (), s32[]{:S(2)}) async-start(), calls=%async_computation.7 | async-start | bytes 5308416 | tf_op jit(solution)/shard_map/reduce_scatter | solution.py:653
  40.7 21.1 %collective-permute-start.8 = (bf16[4,56,768]{2,1,0:T(8,128)(2,1)}, bf16[4,56,768]{2,1,0:T(8,128)(2,1)}, u32[]{:S(2)}, u32[]{:S(2)}) collective-permute-start(bf16[4,56,768]{2,1,0:T(8,128)(2,1)} %pad_maximum_fusion.17), channel_id=1, source_target_pairs={{0,16},{8,24},{16,0},{24,8},{1,17},{9,25},{17,1},{25,9},{2,18},{10... | collective-permute-start | bytes 1032200 | tf_op jit(solution)/shard_map/ppermute | solution.py:506
  44.1 25.6 %collective-permute-start.5 = (bf16[384,768]{1,0:T(8,128)(2,1)}, bf16[384,768]{1,0:T(8,128)(2,1)}, u32[]{:S(2)}, u32[]{:S(2)}) collective-permute-start(bf16[384,768]{1,0:T(8,128)(2,1)} %get-tuple-element.174), channel_id=1, source_target_pairs={{0,8},{16,24},{24,16},{1,9},{17,25},{25,17},{2,10},{18,26},{26,18}... | collective-permute-start | bytes 1769480 | tf_op jit(solution)/shard_map/ppermute | solution.py:418
  48.4 21.3 %collective-permute-start.6 = (bf16[384,768]{1,0:T(8,128)(2,1)}, bf16[384,768]{1,0:T(8,128)(2,1)}, u32[]{:S(2)}, u32[]{:S(2)}) collective-permute-start(bf16[384,768]{1,0:T(8,128)(2,1)} %get-tuple-element.173), channel_id=1, source_target_pairs={{0,16},{8,24},{1,17},{9,25},{2,18},{10,26},{3,19},{11,27},{4,20},{... | collective-permute-start | bytes 1769480 | tf_op jit(solution)/shard_map/ppermute | solution.py:418
  51.5 17.0 %collective-permute-start.7 = (bf16[4,64,768]{2,1,0:T(8,128)(2,1)}, bf16[4,64,768]{2,1,0:T(8,128)(2,1)}, u32[]{:S(2)}, u32[]{:S(2)}) collective-permute-start(bf16[4,64,768]{2,1,0:T(8,128)(2,1)} %slice.181), channel_id=1, source_target_pairs={{0,8},{8,0},{16,24},{24,16},{1,9},{9,1},{17,25},{25,17},{2,10},{10... | collective-permute-start | bytes 1179656 | tf_op jit(solution)/shard_map/ppermute | solution.py:506
  74.0 20.3 %collective-permute-start.9 = (bf16[4,2,64,768]{3,2,0,1:T(8,128)(2,1)S(1)}, bf16[4,2,64,768]{3,2,0,1:T(8,128)(2,1)}, u32[]{:S(2)}, u32[]{:S(2)}) collective-permute-start(bf16[4,2,64,768]{3,2,0,1:T(8,128)(2,1)S(1)} %pad_maximum_fusion.12), channel_id=1, source_target_pairs={{0,16},{8,24},{16,0},{24,8},{1,17},{9,25},{17,1},{25,9},{2,18},{10... | collective-permute-start | bytes 2359304 | tf_op jit(solution)/shard_map/ppermute | solution.py:506
  75.7 16.0 %collective-permute-start.10 = (bf16[4,2,56,768]{3,2,1,0:T(8,128)(2,1)}, bf16[4,2,56,768]{3,2,1,0:T(8,128)(2,1)}, u32[]{:S(2)}, u32[]{:S(2)}) collective-permute-start(bf16[4,2,56,768]{3,2,1,0:T(8,128)(2,1)} %pad_maximum_fusion.14), channel_id=1, source_target_pairs={{0,8},{8,0},{16,24},{24,16},{1,9},{9,1},{17,25},{25,17},{2,10},{10... | collective-permute-start | bytes 2064392 | tf_op jit(solution)/shard_map/ppermute | solution.py:506
  107.8 36.0 %collective-permute-start.11 = (bf16[4,2,2,64,768]{4,3,0,2,1:T(8,128)(2,1)S(1)}, bf16[4,2,2,64,768]{4,3,0,2,1:T(8,128)(2,1)S(1)}, u32[]{:S(2)}, u32[]{:S(2)}) collective-permute-start(bf16[4,2,2,64,768]{4,3,0,2,1:T(8,128)(2,1)S(1)} %pad_maximum_fusion.5), channel_id=1, source_target_pairs={{0,1},{1,0},{2,3},{3,2},{4,5},{5,4},{6,7},{7,6},{8,9},{9,8},{10,11... | collective-permute-start | bytes 4718600 | tf_op jit(solution)/shard_map/ppermute | solution.py:506
  107.8 34.2 %collective-permute-start.12 = (bf16[4,2,2,56,768]{4,3,2,1,0:T(8,128)(2,1)S(1)}, bf16[4,2,2,56,768]{4,3,2,1,0:T(8,128)(2,1)}, u32[]{:S(2)}, u32[]{:S(2)}) collective-permute-start(bf16[4,2,2,56,768]{4,3,2,1,0:T(8,128)(2,1)S(1)} %copy-done.9), channel_id=1, source_target_pairs={{0,1},{1,0},{2,3},{3,2},{4,5},{5,4},{6,7},{7,6},{8,9},{9,8},{10,11... | collective-permute-start | bytes 4128776 | tf_op jit(solution)/shard_map/ppermute | solution.py:506
  174.6 151.2 %reduce-scatter.6.cloned.1.call-start = ((), (), s32[]{:S(2)}) async-start(), calls=%async_computation.8 | async-start | bytes 3981312 | tf_op jit(solution)/shard_map/reduce_scatter | solution.py:653
  202.4 45.2 %collective-permute-start.14 = (bf16[4,192,768]{2,1,0:T(8,128)(2,1)S(1)}, bf16[4,192,768]{2,1,0:T(8,128)(2,1)S(1)}, u32[]{:S(2)}, u32[]{:S(2)}) collective-permute-start(bf16[4,192,768]{2,1,0:T(8,128)(2,1)S(1)} %dynamic-slice_bitcast_fusion.1), channel_id=1, source_target_pairs={{0,16},{8,24},{16,0},{24,8},{1,17},{9,25},{17,1},{25,9},{2,18},{10... | collective-permute-start | bytes 3538952 | tf_op jit(solution)/shard_map/ppermute | solution.py:463
  270.5 117.0 %reduce-scatter.8.cloned.1.call-start = ((), (), s32[]{:S(2)}) async-start(), calls=%async_computation.9 | async-start | bytes 1437696 | tf_op jit(solution)/shard_map/reduce_scatter | solution.py:653
  270.6 25.5 %collective-permute-start.15 = (bf16[4,96,768]{2,1,0:T(8,128)(2,1)S(1)}, bf16[4,96,768]{2,1,0:T(8,128)(2,1)S(1)}, u32[]{:S(2)}, u32[]{:S(2)}) collective-permute-start(bf16[4,96,768]{2,1,0:T(8,128)(2,1)S(1)} %dynamic-slice_bitcast_fusion.2), channel_id=1, source_target_pairs={{0,8},{8,0},{16,24},{24,16},{1,9},{9,1},{17,25},{25,17},{2,10},{10... | collective-permute-start | bytes 1769480 | tf_op jit(solution)/shard_map/ppermute | solution.py:463
  334.7 20.3 %collective-permute-start.20 = (bf16[1,192,768]{2,1,0:T(8,128)(2,1)}, bf16[1,192,768]{2,1,0:T(8,128)(2,1)}, u32[]{:S(2)}, u32[]{:S(2)}) collective-permute-start(bf16[1,192,768]{2,1,0:T(8,128)(2,1)} %dynamic-slice_bitcast_fusion.3), channel_id=1, source_target_pairs={{0,4},{1,5},{2,6},{3,7},{4,0},{5,1},{6,2},{7,3},{8,12},{9,13},{10,... | collective-permute-start | bytes 884744 | tf_op jit(solution)/shard_map/ppermute | solution.py:463
  342.7 13.4 %collective-permute-start.19 = (bf16[256,768]{1,0:T(8,128)(2,1)}, bf16[256,768]{1,0:T(8,128)(2,1)}, u32[]{:S(2)}, u32[]{:S(2)}) collective-permute-start(bf16[256,768]{1,0:T(8,128)(2,1)} %broadcast_select_fusion.5), channel_id=1, source_target_pairs={{16,24},{24,16},{17,25},{25,17},{18,26},{26,18},{19,27},{27,19},{2... | collective-permute-start | bytes 1179656 | tf_op jit(solution)/shard_map/ppermute | solution.py:418
  348.3 20.6 %all-to-all-start = ((bf16[4,168,768]{2,1,0:T(8,128)(2,1)}), bf16[4,168,768]{2,1,0:T(8,128)(2,1)S(1)}, u32[]{:S(2)}, u32[]{:S(2)}) async-start(bf16[4,168,768]{2,1,0:T(8,128)(2,1)} %bitcast.184), calls=%async_computation.3 | async-start | bytes 2064384 | tf_op jit(solution)/shard_map/all_to_all | solution.py:556
  359.5 18.2 %collective-permute-start.18 = (bf16[256,768]{1,0:T(8,128)(2,1)}, bf16[256,768]{1,0:T(8,128)(2,1)}, u32[]{:S(2)}, u32[]{:S(2)}) collective-permute-start(bf16[256,768]{1,0:T(8,128)(2,1)} %get-tuple-element.157), channel_id=1, source_target_pairs={{0,24},{8,16},{16,8},{24,0},{1,25},{9,17},{17,9},{25,1},{2,26},{10... | collective-permute-start | bytes 1179656 | tf_op jit(solution)/shard_map/ppermute | solution.py:418
  362.3 22.3 %collective-permute-start.17 = (bf16[256,768]{1,0:T(8,128)(2,1)}, bf16[256,768]{1,0:T(8,128)(2,1)}, u32[]{:S(2)}, u32[]{:S(2)}) collective-permute-start(bf16[256,768]{1,0:T(8,128)(2,1)} %get-tuple-element.158), channel_id=1, source_target_pairs={{0,16},{8,24},{16,0},{24,8},{1,17},{9,25},{17,1},{25,9},{2,18},{10... | collective-permute-start | bytes 1179656 | tf_op jit(solution)/shard_map/ppermute | solution.py:418
  362.3 22.3 %collective-permute-start.16 = (bf16[256,768]{1,0:T(8,128)(2,1)}, bf16[256,768]{1,0:T(8,128)(2,1)}, u32[]{:S(2)}, u32[]{:S(2)}) collective-permute-start(bf16[256,768]{1,0:T(8,128)(2,1)} %get-tuple-element.153), channel_id=1, source_target_pairs={{0,8},{8,0},{16,24},{24,16},{1,9},{9,1},{17,25},{25,17},{2,10},{10... | collective-permute-start | bytes 1179656 | tf_op jit(solution)/shard_map/ppermute | solution.py:418
  389.1 8.5 %all-to-all-start.1 = ((bf16[4,26,768]{2,1,0:T(8,128)(2,1)}), bf16[4,26,768]{2,1,0:T(8,128)(2,1)S(1)}, u32[]{:S(2)}, u32[]{:S(2)}) async-start(bf16[4,26,768]{2,1,0:T(8,128)(2,1)} %reshape.278), calls=%async_computation.4 | async-start | bytes 393216 | tf_op jit(solution)/shard_map/all_to_all | solution.py:556
  393.4 31.2 %collective-permute-start.23 = (bf16[256,768]{1,0:T(8,128)(2,1)}, bf16[256,768]{1,0:T(8,128)(2,1)}, u32[]{:S(2)}, u32[]{:S(2)}) collective-permute-start(bf16[256,768]{1,0:T(8,128)(2,1)} %get-tuple-element.168), channel_id=1, source_target_pairs={{24,0},{25,1},{26,2},{27,3},{28,4},{29,5},{30,6},{31,7}} | collective-permute-start | bytes 1179656 | tf_op jit(solution)/shard_map/ppermute | solution.py:418
  394.7 29.9 %collective-permute-start.22 = (bf16[256,768]{1,0:T(8,128)(2,1)}, bf16[256,768]{1,0:T(8,128)(2,1)}, u32[]{:S(2)}, u32[]{:S(2)}) collective-permute-start(bf16[256,768]{1,0:T(8,128)(2,1)} %get-tuple-element.168), channel_id=1, source_target_pairs={{16,0},{17,1},{18,2},{19,3},{20,4},{21,5},{22,6},{23,7}} | collective-permute-start | bytes 1179656 | tf_op jit(solution)/shard_map/ppermute | solution.py:418
  401.9 15.8 %collective-permute-start.27 = (bf16[2,26,768]{2,1,0:T(8,128)(2,1)S(1)}, bf16[2,26,768]{2,1,0:T(8,128)(2,1)S(1)}, u32[]{:S(2)}, u32[]{:S(2)}) collective-permute-start(bf16[2,26,768]{2,1,0:T(8,128)(2,1)S(1)} %pad_maximum_fusion.20), channel_id=1, source_target_pairs={{0,16},{8,24},{16,0},{24,8},{1,17},{9,25},{17,1},{25,9},{2,18},{10... | collective-permute-start | bytes 239624 | tf_op jit(solution)/shard_map/ppermute | solution.py:506
  409.7 13.5 %collective-permute-start.24 = (bf16[264,768]{1,0:T(8,128)(2,1)}, bf16[264,768]{1,0:T(8,128)(2,1)}, u32[]{:S(2)}, u32[]{:S(2)}) collective-permute-start(bf16[264,768]{1,0:T(8,128)(2,1)} %constant_dynamic-update-slice_fusion), channel_id=1, source_target_pairs={{0,8},{8,0},{16,24},{24,16},{1,9},{9,1},{17,25},{25,17},{2,10},{10... | collective-permute-start | bytes 1216520 | tf_op jit(solution)/shard_map/ppermute | solution.py:506
  424.6 20.2 %collective-permute-start.25 = (bf16[2,264,768]{2,1,0:T(8,128)(2,1)S(1)}, bf16[2,264,768]{2,1,0:T(8,128)(2,1)S(1)}, u32[]{:S(2)}, u32[]{:S(2)}) collective-permute-start(bf16[2,264,768]{2,1,0:T(8,128)(2,1)S(1)} %pad_maximum_fusion.11), channel_id=1, source_target_pairs={{0,16},{8,24},{16,0},{24,8},{1,17},{9,25},{17,1},{25,9},{2,18},{10... | collective-permute-start | bytes 2433032 | tf_op jit(solution)/shard_map/ppermute | solution.py:506
  (57 other events, 332.2 us)
Sparse Core Ops, SparseCore 0:
  12.0 53.8 all-gather.2
  67.6 51.3 all-gather.4
  174.7 65.5 reduce-scatter.3
  270.6 55.1 reduce-scatter.5
  334.1 32.7 reduce-scatter.7

commit v3 on v2

--- a/solution.py
+++ b/solution.py
@@ -586,6 +586,7 @@
     return jnp.concatenate(rows, axis=0)
 
 
+FORWARD_SPLIT = 4
 CHUNKS = (4, 2)
 
 
@@ -616,21 +617,27 @@
     gathered = Gathered(me, w_ff, w_out)
     full_in = gather(w_in)
     got = exchange_rows(me, own)
-    got, spans, table = gathered.tie((got, spans, bias_table))
+    got, spans, table = lax.optimization_barrier((got, spans, bias_table))
     got = got + exchange_again(me, own, *got)
-    gathered.exchange(0)
     prepared = setup(me, spans, table)
     inverse_one = rms(inputs)
     got, prepared, inverse_one = gathered.tie((got, prepared, inverse_one))
     meta, bias, qaug, kaug, far = prepared
-    gathered.exchange(1)
+    gathered.exchange(0)
     normed_own = by_rows((inputs * inverse_one * gain_one).astype(bf16))
     normed_seen = by_rows(normed_rows(by_rows(seen_rows(me, own, got)), gain_one))
     queries = jnp.dot(normed_own, full_query, preferred_element_type=f32).astype(bf16)
     keys_values = jnp.dot(normed_seen, full_kv, preferred_element_type=f32).astype(bf16)
-    queries, keys_values = gathered.tie((queries, keys_values))
+    meta, queries, keys_values = gathered.tie((meta, queries, keys_values))
+    gathered.exchange(1)
+    parts = [attention_forward(meta, queries, keys_values, qaug, kaug, bias, 0, FORWARD_SPLIT)]
+    meta, parts = gathered.tie((meta, parts))
     gathered.cores()
-    context, rest, lse = gathered.tie(attention_forward(meta, queries, keys_values, qaug, kaug, bias, 0, pairs))
+    parts.append(attention_forward(meta, queries, keys_values, qaug, kaug, bias, FORWARD_SPLIT,
+                                   pairs - FORWARD_SPLIT))
+    parts = gathered.tie(parts)
+    context, rest = (jnp.concatenate([part[i] for part in parts], axis=1) for i in range(2))
+    lse = jnp.concatenate([part[2] for part in parts], axis=0)
     full_ff, full_out = gathered.whole()
     middle = by_rows(inputs + jnp.dot(context, full_out, preferred_element_type=f32))
     inverse_two = rms(middle)
@@ -653,13 +660,10 @@
         return lax.psum_scatter(g, "wshard", scatter_dimension=0, tiled=True)
 
     size = gain_attn.shape[0]
-    owned_ff = Owned(contract_rows(hidden_act, d_branch_two).astype(bf16), me, "yx")
-    owned_ff.advance()
+    share_ff = owners(by_rows(contract_rows(hidden_act, d_branch_two).astype(bf16)))
     d_pre = jnp.where(hidden_act > 0, dot_nt(d_branch_two, full_ff), 0.0).astype(bf16)
-    grad_in = contract_rows(normed_two, d_pre).astype(bf16)
+    share_in = owners(by_rows(contract_rows(normed_two, d_pre).astype(bf16)))
     d_normed_two = by_rows(dot_nt(d_pre, full_in))
-    d_normed_two, owned_ff.rows = lax.optimization_barrier((d_normed_two, owned_ff.rows))
-    owned_ff.advance()
     scaled_two = middle * inverse_two
     d_scaled_two = d_normed_two * gain_two
     d_middle = d_final + inverse_two * (
@@ -668,7 +672,6 @@
     d_branch_one = by_rows(d_middle.astype(bf16))
     grad_out = contract_rows(context, d_branch_one).astype(bf16)
     d_context = dot_nt(d_branch_one, full_out).astype(bf16)
-    share_in = owners(grad_in)
     d_context, grad_out = lax.optimization_barrier((d_context, grad_out))
 
     starts = [sum(CHUNKS[:i]) for i in range(len(CHUNKS))]
@@ -679,66 +682,76 @@
                                   starts[i], CHUNKS[i])
 
     def weight_grad(d_q, d_kv):
-        return jnp.concatenate([by_rows(contract_rows(normed_own, d_q).astype(bf16)),
-                                by_rows(contract_rows(normed_seen, d_kv).astype(bf16))], axis=1)
-
-    def back_to_rows(i, d_q, d_kv):
-        lo, hi = cuts[i]
-        return by_rows(dot_nt(d_q, full_query[:, lo:hi])), by_rows(dot_nt(d_kv, full_kv[:, 2 * lo:2 * hi]))
+        return [by_rows(contract_rows(normed_own, d_q).astype(bf16)),
+                by_rows(contract_rows(normed_seen, d_kv).astype(bf16))]
+
+    def query_rows(i, d_q):
+        return by_rows(dot_nt(d_q, full_query[:, cuts[i][0]:cuts[i][1]]))
+
+    def key_rows(i, d_kv):
+        return by_rows(dot_nt(d_kv, full_kv[:, 2 * cuts[i][0]:2 * cuts[i][1]]))
 
     first = backward(meta, 0)
-    meta, first, owned_ff.rows, share_in = lax.optimization_barrier((meta, first, owned_ff.rows, share_in))
-    owned_ff.advance()
-    grad_first = jnp.concatenate([weight_grad(*first[:2]), grad_out], axis=1)
-    f_first = back_to_rows(0, *first[:2])
-    meta, grad_first, f_first = lax.optimization_barrier((meta, grad_first, f_first))
-    share_first = owners(grad_first)
+    meta, first, share_ff = lax.optimization_barrier((meta, first, share_ff))
+    share_first = owners(jnp.concatenate(weight_grad(*first[:2]) + [grad_out], axis=1))
+    f_query = query_rows(0, first[0])
+    f_part = by_rows(key_rows(0, first[1]).astype(bf16))
+    meta, f_query, f_part = lax.optimization_barrier((meta, f_query, f_part))
+    f_first = sum_prompt(me, f_part)
     second = backward(meta, 1)
-    second, owned_ff.rows, share_first = lax.optimization_barrier((second, owned_ff.rows, share_first))
-    grad_second = weight_grad(*second[:2])
+    second, f_first, share_in = lax.optimization_barrier((second, f_first, share_in))
     heads = bias_table.shape[1]
     near = jnp.sum(jnp.concatenate([first[2], second[2]], axis=0), axis=3).reshape(heads, 8 * TILE)
-    bias_local = jnp.dot(near, jnp.asarray(bias_spread()), precision=lax.Precision.HIGHEST).reshape(1, -1)
+    bias_local = jnp.dot(near, jnp.asarray(bias_spread()), precision=lax.Precision.HIGHEST).reshape(-1, TILE)
     bias_top = bias_local.astype(bf16)
     bias_rest = (bias_local - bias_top.astype(f32)).astype(bf16)
-    n_bias = bias_local.shape[1]
-    n_last = grad_second.shape[1]
-    bias_rows = jnp.pad(jnp.concatenate([bias_top, bias_rest], axis=1), ((0, 7), (0, n_last - 2 * n_bias)))
-    blocks = grad_second.reshape(-1, size, n_last)
-    bias_rows = jnp.broadcast_to(bias_rows[None], (blocks.shape[0],) + bias_rows.shape)
-    last = jnp.concatenate([blocks, bias_rows], axis=1).reshape(-1, n_last)
-    share_last = owners(last)
-    f_second = back_to_rows(1, *second[:2])
-    f_query = f_first[0] + f_second[0]
-    f_summed = by_rows(sum_prompt(me, by_rows((f_first[1] + f_second[1]).astype(bf16))))
-    quarter_ff = owned_ff.finish()
-    shares_out = jnp.concatenate([share.reshape(-1, width) for share in (share_in, share_first)], axis=0)
-    quarter_out = quarter_sum(shares_out)
-    share_last, f_summed, quarter_ff, quarter_out = lax.optimization_barrier(
-        (share_last, f_summed, quarter_ff, quarter_out))
-    quarters = [quarter_ff, quarter_out]
-    f_block = f_summed[:QB]
+    n_bias = bias_local.shape[0]
+    size = gain_attn.shape[0]
+    bias_columns = jnp.pad(jnp.concatenate([bias_top, bias_rest], axis=0), ((0, max(0, size - 2 * n_bias)), (0, 0)))
+    bias_rows = bias_columns.shape[0]
+    blocks = jnp.concatenate(weight_grad(*second[:2]), axis=1)
+    n_last = blocks.shape[1]
+    blocks = blocks.reshape(-1, size, n_last)
+    if bias_rows > size:
+        blocks = jnp.pad(blocks, ((0, 0), (0, bias_rows - size), (0, 0)))
+    last = jnp.concatenate([blocks, jnp.broadcast_to(bias_columns[None], (blocks.shape[0],) + bias_columns.shape)],
+                           axis=2).reshape(-1, n_last + TILE)
+    owned_last = Owned(by_rows(last), me, "yx")
+    owned_last.advance()
+    f_query = f_query + query_rows(1, second[0])
+    d_kv = sum_prompt(me, second[1])
+    owned_last.advance()
+    x_step, y_step = [(bit, "seq", pairs) for bit, pairs in seq_bits(me, "xy")]
+
+    def flat(*shares):
+        return jnp.concatenate([share.reshape(-1, width) for share in shares], axis=0)
+
+    quarter_early = quarter_sum(flat(share_ff, share_in))
+    f_total = f_first.astype(f32) + key_rows(1, d_kv)
+    f_block = f_total[:QB].astype(bf16)
+    owned_last.advance()
+    owned_last.advance()
+    owned_last.advance()
+    quarter_first = quarter_sum(flat(share_first))
+    owned_last.rows, quarter_early, quarter_first, f_total = lax.optimization_barrier((owned_last.rows, quarter_early, quarter_first, f_total))
     from_two = send(f_block, [(2, 0)])
     from_three = send(f_block, [(3, 0)])
-    f_own = f_query + (f_summed[QB:] + jnp.concatenate(
-        [jnp.where(me < 2, f_block, jnp.zeros_like(f_block)), from_two, from_three], axis=0)).astype(f32)
+    f_own = f_query + f_total[QB:] + jnp.concatenate(
+        [jnp.where(me < 2, f_block, jnp.zeros_like(f_block)), from_two, from_three], axis=0).astype(f32)
     scaled_one = inputs * inverse_one
     d_scaled_one = f_own * gain_one
     d_tokens = d_middle + inverse_one * (
         d_scaled_one - scaled_one * jnp.mean(d_scaled_one * scaled_one, axis=1, keepdims=True))
 
-    size = gain_attn.shape[0]
-    n_quarter = quarter_ff.shape[0]
-    early = join_quarters(jnp.concatenate(quarters, axis=0), me)
-    share_ff = early[:, :n_quarter].reshape(-1, width).astype(f32)
-    others = early[:, n_quarter:].reshape(-1, width).astype(f32)
-    n_in = share_in.shape[0] * share_in.shape[1] // width
-    share_in = others[:n_in].reshape(size, -1)
-    share_first = others[n_in:].reshape(size, -1)
+    half_early = beside(quarter_early, *x_step, 0)
+    early = beside(half_early, *y_step, 0).reshape(-1, width).astype(f32)
+    n_ff = share_ff.shape[0]
+    share_ff, share_in = early[:n_ff], early[n_ff:].reshape(size, -1)
+    late = join_quarters(owned_last.finish(), me).reshape(bias_rows if bias_rows > size else size, -1).astype(f32)
+    share_first = join_quarters(quarter_first, me).reshape(size, -1).astype(f32)
     share_out = share_first[:, -width:]
-    late = join_quarters(quarter_sum(share_last.reshape(-1, width)), me).reshape(-1, n_last).astype(f32)
-    shares = [share_first[:, :-width], late[:size]]
-    bias_grad = (late[size, :n_bias] + late[size, n_bias:2 * n_bias]).reshape(heads, NB).T
+    shares = [share_first[:, :-width], late[:size, :n_last]]
+    bias_grad = (late[:n_bias, n_last:] + late[n_bias:2 * n_bias, n_last:]).reshape(heads, NB).T
     share_query = jnp.concatenate(
         [share[:, :count * TILE] for share, count in zip(shares, CHUNKS)], axis=1)
     share_kv = jnp.concatenate(

time: 469 us -> 420 us (0.90)
  waiting for transfers between devices: 105 us -> 62.5 us
  other arithmetic: 56.6 us -> 47.1 us
  starting transfers between devices: 52.7 us -> 61.8 us
  matrix products: 88 us -> 82.6 us
    ppermute x10 -> x12, waiting for transfers between devices: 42.1 us -> 10.3 us  [beside(): got = lax.ppermute(rows, axis, pairs)]
    reduce_scatter x3, waiting for transfers between devices: 29.5 us -> 0.04 us  [owners(): return lax.psum_scatter(g, 'wshard', scatter_dimension=0, tiled=True)]
    ppermute x10 -> x14, waiting for transfers between devices: 14.8 us -> 28.9 us  [send(): return lax.ppermute(rows, 'seq', pairs)]
    ppermute x10 -> x14, starting transfers between devices: 19 us -> 30.1 us  [send(): return lax.ppermute(rows, 'seq', pairs)]
    all_to_all x2, waiting for transfers between devices: 2.04 us -> 10.6 us  [quarter_sum(): lax.all_to_all(rows.reshape(4, -1, rows.shape[1]), 'seq', split_axis=0, c...]
    ppermute x3, waiting for transfers between devices: 11.1 us -> 3.44 us  [__init__(): lax.ppermute(quarter, 'wshard', [(i, (i // 2 + k) % 4 * 2 + i % 2) for i...]
    ppermute x10 -> x12, starting transfers between devices: 13.9 us -> 6.95 us  [beside(): got = lax.ppermute(rows, axis, pairs)]
    dot_general x7, matrix products: 27.7 us -> 21.8 us  [contract_rows(): lax.dot_general(left, right, (((0,), (0,)), ((), ())), preferred_element_...]
  transfers between devices with their start and end apart: 35 -> 41, of which waited for: 13 -> 14; matrix products, arithmetic and copies ran while one was open for 21% -> 29% of each run, Pallas kernels for 24% -> 27%
where the time goes in v3:
time: 420 us; the launch traced here: 416 us
  Pallas kernels  112 us (27%)
  matrix products  82.6 us (20%)
  waiting for transfers between devices  62.5 us (15%)
  starting transfers between devices  61.8 us (15%)
  other arithmetic  47.1 us (11%)
  local copies, waits for them, and re-layouts  30.5 us (7%)
  between operations  19.1 us (5%)
    pallas_call x2, Pallas kernels, attention_backward(): pl.pallas_call(backward_kernel, grid_spec=pltpu.PrefetchScalarGridSpec(nu...  68.1 us
    pallas_call x2, Pallas kernels, attention_forward(): pl.pallas_call(forward_kernel, grid_spec=pltpu.PrefetchScalarGridSpec(num...  37.1 us
    dot_general x7, matrix products, dot_nt(): lax.dot_general(a, b, (((1,), (1,)), ((), ())), preferred_element_type=f32)  34.8 us
    ppermute x14, starting transfers between devices, send(): return lax.ppermute(rows, 'seq', pairs)  30.1 us
    ppermute x14, waiting for transfers between devices, send(): return lax.ppermute(rows, 'seq', pairs)  28.9 us
    dot_general x7, matrix products, contract_rows(): lax.dot_general(left, right, (((0,), (0,)), ((), ())), preferred_element_...  21.8 us
    unnamed x137, local copies, waits for them, and re-layouts  11.9 us
    all_to_all x2, waiting for transfers between devices, quarter_sum(): lax.all_to_all(rows.reshape(4, -1, rows.shape[1]), 'seq', split_axis=0, c...  10.6 us
  transfers between devices with their start and end apart: 41, of which 14 were waited for; matrix products, arithmetic and copies ran while one was open for 29% of the time, Pallas kernels for 27%

profile of v3, /device:TPU:0, one launch (start us, length us, event | category | flops | bytes accessed | tf_op | source)
XLA Modules:
  0.0 415.6 jit_solution(12189746776095622705)
XLA Ops:
  13.0 4.9 %collective-permute-start.1 = (bf16[384,768]{1,0:T(8,128)(2,1)}, bf16[384,768]{1,0:T(8,128)(2,1)S(1)}, u32[]{:S(2)}, u32[]{:S(2)}) collective-permute-start(bf16[384,768]{1,0:T(8,128)(2,1)} %get-tuple-element.199), channel_id=1, source_target_pairs={{0,16},{8,24},{1,17},{9,25},{2,18},{10,26},{3,19},{11,27},{4,20},{... | collective-permute-start | bytes 1769480 | tf_op jit(solution)/shard_map/ppermute | solution.py:418
  20.3 3.7 collective-permute-start.6
  25.4 5.4 %collective-permute-done.1 = bf16[384,768]{1,0:T(8,128)(2,1)S(1)} collective-permute-done((bf16[384,768]{1,0:T(8,128)(2,1)}, bf16[384,768]{1,0:T(8,128)(2,1)S(1)}, u32[]{:S(2)}, u32[]{:S(2)}) %collective-permute-start.1) | collective-permute-done | bytes 589856 | tf_op jit(solution)/shard_map/ppermute | solution.py:418
  37.0 3.9 collective-permute-start.2
  43.2 7.0 %setup.1 = (f32[12,640,128]{2,1,0:T(8,128)}, bf16[768,128]{1,0:T(8,128)(2,1)}, bf16[2048,128]{1,0:T(8,128)(2,1)}, f32[2,2,16,8,128]{4,3,2,1,0:T(8,128)}) custom-call(s32[6]{0:T(128)} %pad_add_fusion.meta, s32[3]{0:T(128)} %broadcast_select_fusion.7.limit, f32[384]{0:T(512)} %reshape.236.table), custom_call_target="tpu_custom_call" | custom-call | flops 30000000 | bytes 5000000 | tf_op jit(solution)/shard_map/setup/pallas_call | solution.py:376
  67.1 3.7 all-gather.3.cloned.1.call-done
  72.2 3.6 convolution_convert_fusion.7.q_ref
  75.9 7.1 %convolution_convert_fusion.k_ref.v_ref = bf16[2048,1536]{1,0:T(8,128)(2,1)} fusion(bf16[768,2432]{1,0:T(8,128)(2,1)S(1)} %copy-done.39, bf16[2048,768]{1,0:T(8,128)(2,1)S(1)} %copy-done.10, f32[768]{0:T(1024)S(1)} %get-tuple-element.158, f32[2048]{0:T(1024)S(1)} %add_rsqrt_fusion), kind=kOutput, calls=%fused_computation.4 | convolution fusion | flops 4841275392 | bytes 11808768 | tf_op jit(solution)/shard_map/dot_general | solution.py:630
  83.5 23.7 %attention_forward.2 = (bf16[768,512]{1,0:T(8,128)(2,1)}, bf16[768,512]{1,0:T(8,128)(2,1)}, f32[4,2,768]{2,1,0:T(2,128)}) custom-call(s32[6]{0:T(128)} %pad_add_fusion.meta, bf16[768,768]{1,0:T(8,128)(2,1)} %convolution_convert_fusion.7.q_ref, bf16[2048,1536]{1,0:T(8,128)(2,1)} %convolution_convert_fusion.k_ref.v_ref, ...), custom_call_target="tpu_custom_call" | custom-call | flops 20000000000 | bytes 8000000 | tf_op jit(solution)/shard_map/attention_forward/pallas_call | solution.py:96
  110.8 13.4 %attention_forward.3 = (bf16[768,256]{1,0:T(8,128)(2,1)}, bf16[768,256]{1,0:T(8,128)(2,1)}, f32[2,2,768]{2,1,0:T(2,128)}) custom-call(s32[6]{0:T(128)} %pad_add_fusion.meta, bf16[768,768]{1,0:T(8,128)(2,1)} %convolution_convert_fusion.7.q_ref, bf16[2048,1536]{1,0:T(8,128)(2,1)} %convolution_convert_fusion.k_ref.v_ref, ...), custom_call_target="tpu_custom_call" | custom-call | flops 10000000000 | bytes 4000000 | tf_op jit(solution)/shard_map/attention_forward/pallas_call | solution.py:96
  134.4 7.1 %maximum_convert_fusion = bf16[768,3072]{1,0:T(8,128)(2,1)S(1)} fusion(bf16[768,3072]{1,0:T(8,128)(2,1)} %all-gather.5.cloned.1.call-done, f32[768,768]{1,0:T(8,128)} %get-tuple-element.224, f32[768]{0:T(1024)S(1)} %get-tuple-element.157, f32[768]{0:T(1024)S(1)} %add_rsqrt_fusion.1), kind=kOutput, calls=%fused_computation.1 | convolution fusion | flops 3630366720 | bytes 11802624 | tf_op jit(solution)/shard_map/dot_general | solution.py:645
  141.5 5.4 %fusion.18 = (bf16[768,768]{1,0:T(8,128)(2,1)S(1)}, f32[768,768]{1,0:T(8,128)}) fusion(bf16[1,768,768]{2,1,0:T(8,128)(2,1)S(1)} %copy-done.25, f32[]{:T(128)S(6)} %div.82, pred[768]{0:T(1024)(128)(4,1)S(1)} %fusion.57, f32[768,768]{1,0:T(8,128)S(1)} %copy-done.16, bf16[768,3072]{1,0:T(8,128)(2,1)S(1)} %maximum_convert_fusion, ...), kind=kOutput, calls=%fused_computation.56 | convolution fusion | flops 3627417600 | bytes 16515844 | tf_op jit(solution)/shard_map/dot_general | solution.py:646
  147.9 5.7 %convolution_convert_fusion.2 = bf16[3072,768]{1,0:T(8,128)(2,1)} fusion(bf16[768,3072]{1,0:T(8,128)(2,1)S(1)} %maximum_convert_fusion, bf16[768,768]{1,0:T(8,128)(2,1)S(1)} %get-tuple-element.225), kind=kOutput, calls=%fused_computation.9 | convolution fusion | flops 3626237952 | bytes 10616832 | tf_op jit(solution)/shard_map/dot_general | solution.py:410
  157.4 8.1 %select_convert_fusion = bf16[768,3072]{1,0:T(8,128)(2,1)S(1)} fusion(bf16[768,3072]{1,0:T(8,128)(2,1)} %copy-done.61, bf16[768,768]{1,0:T(8,128)(2,1)} %copy-done.63, bf16[3072,768]{1,0:T(8,128)(2,1)} %bitcast.179), kind=kOutput, calls=%fused_computation | convolution fusion | flops 3630956544 | bytes 15335424 | tf_op jit(solution)/shard_map/dot_general | solution.py:26
  167.7 5.9 %convolution_convert_fusion.1 = bf16[768,3072]{1,0:T(8,128)(2,1)} fusion(bf16[768,3072]{1,0:T(8,128)(2,1)S(1)} %select_convert_fusion, f32[768,768]{1,0:T(8,128)S(1)} %copy-done.17, f32[768]{0:T(1024)S(1)} %get-tuple-element.157, f32[768]{0:T(1024)S(1)} %add_rsqrt_fusion.1), kind=kOutput, calls=%fused_computation.8 | convolution fusion | flops 3628007424 | bytes 11802624 | tf_op jit(solution)/shard_map/dot_general | solution.py:410
  173.8 8.8 %multiply_reduce_fusion = (f32[768]{0:T(1024)S(1)}, f32[768,768]{1,0:T(8,128)S(1)}) fusion(f32[768,768]{1,0:T(8,128)} %get-tuple-element.224, f32[768]{0:T(1024)S(1)} %get-tuple-element.157, f32[768]{0:T(1024)S(1)} %add_rsqrt_fusion.1, bf16[768,3072]{1,0:T(8,128)(2,1)} %copy-done.60, bf16[768,3072]{1,0:T(8,128)(2,1)} %all-gather.5.cloned.1.call-done), kind=kOutput, calls=%fused_computation.35 | convolution fusion | flops 3626237184 | bytes 14164992 | tf_op jit(solution)/shard_map/dot_general | solution.py:26
  189.8 43.9 %attention_backward.2 = (bf16[768,512]{1,0:T(8,128)(2,1)}, bf16[2048,1024]{1,0:T(8,128)(2,1)}, f32[4,2,8,8,128]{4,3,2,1,0:T(8,128)}) custom-call(s32[6]{0:T(128)} %pad_add_fusion.meta, bf16[768,768]{1,0:T(8,128)(2,1)} %convolution_convert_fusion.7.q_ref, bf16[2048,1536]{1,0:T(8,128)(2,1)} %convolution_convert_fusion.k_ref.v_ref, ...), custom_call_target="tpu_custom_call" | custom-call | flops 40000000000 | bytes 12000000 | tf_op jit(solution)/shard_map/attention_backward/pallas_call | solution.py:258
  233.8 3.6 fusion.29
  237.4 6.2 %convolution_convert_fusion.3 = bf16[2048,768]{1,0:T(8,128)(2,1)S(1)} fusion(bf16[2048,1024]{1,0:T(8,128)(2,1)} %get-tuple-element.136, bf16[768,2432]{1,0:T(8,128)(2,1)} %all-gather.3.cloned.1.call-done), kind=kOutput, calls=%fused_computation.15 | convolution fusion | flops 3222798336 | bytes 8912896 | tf_op jit(solution)/shard_map/dot_general | solution.py:26
  248.7 4.2 %collective-permute-start.15 = (bf16[256,768]{1,0:T(8,128)(2,1)}, bf16[256,768]{1,0:T(8,128)(2,1)}, u32[]{:S(2)}, u32[]{:S(2)}) collective-permute-start(bf16[256,768]{1,0:T(8,128)(2,1)} %get-tuple-element.174), channel_id=1, source_target_pairs={{0,24},{8,16},{16,8},{24,0},{1,25},{9,17},{17,9},{25,1},{2,26},{10... | collective-permute-start | bytes 1179656 | tf_op jit(solution)/shard_map/ppermute | solution.py:418
  254.8 3.8 convolution_convert_fusion.4
  260.8 24.1 %attention_backward.3 = (bf16[768,256]{1,0:T(8,128)(2,1)}, bf16[2048,512]{1,0:T(8,128)(2,1)}, f32[2,2,8,8,128]{4,3,2,1,0:T(8,128)}) custom-call(s32[6]{0:T(128)} %pad_add_fusion.meta, bf16[768,768]{1,0:T(8,128)(2,1)} %convolution_convert_fusion.7.q_ref, bf16[2048,1536]{1,0:T(8,128)(2,1)} %convolution_convert_fusion.k_ref.v_ref, ...), custom_call_target="tpu_custom_call" | custom-call | flops 20000000000 | bytes 6000000 | tf_op jit(solution)/shard_map/attention_backward/pallas_call | solution.py:258
  291.5 3.6 convolution_convert_fusion.8
  299.9 4.3 %all-to-all-start = ((bf16[4,192,768]{2,1,0:T(8,128)(2,1)}), bf16[4,192,768]{2,1,0:T(8,128)(2,1)}, u32[]{:S(2)}, u32[]{:S(2)}) async-start(bf16[4,192,768]{2,1,0:T(8,128)(2,1)} %bitcast.183), calls=%async_computation.2 | async-start | bytes 2359296 | tf_op jit(solution)/shard_map/all_to_all | solution.py:556
  308.9 4.2 %collective-permute-start.24 = (bf16[256,512]{1,0:T(8,128)(2,1)S(1)}, bf16[256,512]{1,0:T(8,128)(2,1)S(1)}, u32[]{:S(2)}, u32[]{:S(2)}) collective-permute-start(bf16[256,512]{1,0:T(8,128)(2,1)S(1)} %get-tuple-element.189), channel_id=1, source_target_pairs={{0,24},{8,16},{16,8},{24,0},{1,25},{9,17},{17,9},{25,1},{2,26},{10... | collective-permute-start | bytes 786440 | tf_op jit(solution)/shard_map/ppermute | solution.py:418
  316.7 9.4 %collective-permute-done.22 = bf16[256,512]{1,0:T(8,128)(2,1)S(1)} collective-permute-done((bf16[256,512]{1,0:T(8,128)(2,1)S(1)}, bf16[256,512]{1,0:T(8,128)(2,1)S(1)}, u32[]{:S(2)}, u32[]{:S(2)}) %collective-permute-start.22) | collective-permute-done | bytes 262176 | tf_op jit(solution)/shard_map/ppermute | solution.py:418
  326.1 11.9 %collective-permute-done.24 = bf16[256,512]{1,0:T(8,128)(2,1)S(1)} collective-permute-done((bf16[256,512]{1,0:T(8,128)(2,1)S(1)}, bf16[256,512]{1,0:T(8,128)(2,1)S(1)}, u32[]{:S(2)}, u32[]{:S(2)}) %collective-permute-start.24) | collective-permute-done | bytes 262176 | tf_op jit(solution)/shard_map/ppermute | solution.py:418
  344.9 6.0 %collective-permute-start.20 = (bf16[1,48,896]{2,1,0:T(8,128)(2,1)S(1)}, bf16[1,48,896]{2,1,0:T(8,128)(2,1)S(1)}, u32[]{:S(2)}, u32[]{:S(2)}) collective-permute-start(bf16[1,48,896]{2,1,0:T(8,128)(2,1)S(1)} %dynamic-slice_bitcast_fusion.3), channel_id=1, source_target_pairs={{0,4},{1,5},{2,6},{3,7},{4,0},{5,1},{6,2},{7,3},{8,12},{9,13},{10,... | collective-permute-start | bytes 258056 | tf_op jit(solution)/shard_map/ppermute | solution.py:463
  356.4 5.6 %all-to-all-start.1 = ((bf16[4,72,768]{2,1,0:T(8,128)(2,1)}), bf16[4,72,768]{2,1,0:T(8,128)(2,1)S(1)}, u32[]{:S(2)}, u32[]{:S(2)}) async-start(bf16[4,72,768]{2,1,0:T(8,128)(2,1)} %reshape_reshape.13), calls=%async_computation.4 | async-start | bytes 884736 | tf_op jit(solution)/shard_map/all_to_all | solution.py:556
  366.0 10.6 %all-to-all-done.1 = bf16[4,72,768]{2,1,0:T(8,128)(2,1)S(1)} async-done(((bf16[4,72,768]{2,1,0:T(8,128)(2,1)}), bf16[4,72,768]{2,1,0:T(8,128)(2,1)S(1)}, u32[]{:S(2)}, u32[]{:S(2)}) %all-to-all-start.1) | async-done | bytes 442400 | tf_op jit(solution)/shard_map/all_to_all | solution.py:556
  378.8 3.7 fusion.7
  398.7 5.5 %collective-permute-done.33 = bf16[2,192,768]{2,1,0:T(8,128)(2,1)} collective-permute-done((bf16[2,192,768]{2,1,0:T(8,128)(2,1)}, bf16[2,192,768]{2,1,0:T(8,128)(2,1)}, u32[]{:S(2)}, u32[]{:S(2)}) %collective-permute-start.33) | collective-permute-done | bytes 589856 | tf_op jit(solution)/shard_map/ppermute | solution.py:506
  (348 shorter events, 128.6 us)
Async XLA Ops:
  7.2 63.6 %all-gather.3.cloned.1.call-start = ((), (), s32[]{:S(2)}) async-start(), calls=%async_computation.5 | async-start | bytes 4202496 | tf_op jit(solution)/shard_map/all_gather | solution.py:609
  11.9 122.5 %all-gather.5.cloned.1.call-start = ((), (), s32[]{:S(2)}) async-start(), calls=%async_computation.6 | async-start | bytes 5308416 | tf_op jit(solution)/shard_map/all_gather | solution.py:609
  13.0 17.8 %collective-permute-start.1 = (bf16[384,768]{1,0:T(8,128)(2,1)}, bf16[384,768]{1,0:T(8,128)(2,1)S(1)}, u32[]{:S(2)}, u32[]{:S(2)}) collective-permute-start(bf16[384,768]{1,0:T(8,128)(2,1)} %get-tuple-element.199), channel_id=1, source_target_pairs={{0,16},{8,24},{1,17},{9,25},{2,18},{10,26},{3,19},{11,27},{4,20},{... | collective-permute-start | bytes 1769480 | tf_op jit(solution)/shard_map/ppermute | solution.py:418
  17.9 15.1 %collective-permute-start = (bf16[384,768]{1,0:T(8,128)(2,1)}, bf16[384,768]{1,0:T(8,128)(2,1)S(1)}, u32[]{:S(2)}, u32[]{:S(2)}) collective-permute-start(bf16[384,768]{1,0:T(8,128)(2,1)} %get-tuple-element.200), channel_id=1, source_target_pairs={{0,8},{8,0},{16,24},{24,16},{1,9},{9,1},{17,25},{25,17},{2,10},{10... | collective-permute-start | bytes 1769480 | tf_op jit(solution)/shard_map/ppermute | solution.py:418
  20.3 29.9 %collective-permute-start.6 = (bf16[120,768]{1,0:T(8,128)(2,1)S(1)}, bf16[120,768]{1,0:T(8,128)(2,1)S(1)}, u32[]{:S(2)}, u32[]{:S(2)}) collective-permute-start(bf16[120,768]{1,0:T(8,128)(2,1)S(1)} %pad_maximum_fusion.18), channel_id=1, source_target_pairs={{0,6},{1,7},{2,0},{3,1},{4,2},{5,3},{6,4},{7,5},{8,14},{9,15},{10,... | collective-permute-start | bytes 552968 | tf_op jit(solution)/shard_map/ppermute | solution.py:523
  24.0 29.7 %collective-permute-start.5 = (bf16[120,768]{1,0:T(8,128)(2,1)S(1)}, bf16[120,768]{1,0:T(8,128)(2,1)S(1)}, u32[]{:S(2)}, u32[]{:S(2)}) collective-permute-start(bf16[120,768]{1,0:T(8,128)(2,1)S(1)} %pad_maximum_fusion.18), channel_id=1, source_target_pairs={{0,4},{1,5},{2,6},{3,7},{4,0},{5,1},{6,2},{7,3},{8,12},{9,13},{10,... | collective-permute-start | bytes 552968 | tf_op jit(solution)/shard_map/ppermute | solution.py:523
  24.0 29.7 %collective-permute-start.4 = (bf16[120,768]{1,0:T(8,128)(2,1)S(1)}, bf16[120,768]{1,0:T(8,128)(2,1)}, u32[]{:S(2)}, u32[]{:S(2)}) collective-permute-start(bf16[120,768]{1,0:T(8,128)(2,1)S(1)} %pad_maximum_fusion.18), channel_id=1, source_target_pairs={{0,2},{1,3},{2,4},{3,5},{4,6},{5,7},{6,0},{7,1},{8,10},{9,11},{10,... | collective-permute-start | bytes 552968 | tf_op jit(solution)/shard_map/ppermute | solution.py:523
  25.0 208.8 %reduce-scatter.4.cloned.1.call-start = ((), (), s32[]{:S(2)}) async-start(), calls=%async_computation.7 | async-start | bytes 5308416 | tf_op jit(solution)/shard_map/reduce_scatter | solution.py:660
  34.1 19.5 %collective-permute-start.3 = (bf16[384,768]{1,0:T(8,128)(2,1)}, bf16[384,768]{1,0:T(8,128)(2,1)}, u32[]{:S(2)}, u32[]{:S(2)}) collective-permute-start(bf16[384,768]{1,0:T(8,128)(2,1)} %get-tuple-element.197), channel_id=1, source_target_pairs={{0,16},{8,24},{1,17},{9,25},{2,18},{10,26},{3,19},{11,27},{4,20},{... | collective-permute-start | bytes 1769480 | tf_op jit(solution)/shard_map/ppermute | solution.py:418
  37.0 16.6 %collective-permute-start.2 = (bf16[384,768]{1,0:T(8,128)(2,1)}, bf16[384,768]{1,0:T(8,128)(2,1)S(1)}, u32[]{:S(2)}, u32[]{:S(2)}) collective-permute-start(bf16[384,768]{1,0:T(8,128)(2,1)} %get-tuple-element.198), channel_id=1, source_target_pairs={{0,8},{16,24},{24,16},{1,9},{17,25},{25,17},{2,10},{18,26},{26,18}... | collective-permute-start | bytes 1769480 | tf_op jit(solution)/shard_map/ppermute | solution.py:418
  82.9 24.2 %collective-permute-start.10 = (bf16[4,2,56,768]{3,2,1,0:T(8,128)(2,1)S(1)}, bf16[4,2,56,768]{3,2,1,0:T(8,128)(2,1)S(1)}, u32[]{:S(2)}, u32[]{:S(2)}) collective-permute-start(bf16[4,2,56,768]{3,2,1,0:T(8,128)(2,1)S(1)} %pad_maximum_fusion.11), channel_id=1, source_target_pairs={{0,8},{8,0},{16,24},{24,16},{1,9},{9,1},{17,25},{25,17},{2,10},{10... | collective-permute-start | bytes 2064392 | tf_op jit(solution)/shard_map/ppermute | solution.py:506
  83.5 25.0 %collective-permute-start.9 = (bf16[4,2,64,768]{3,2,0,1:T(8,128)(2,1)S(1)}, bf16[4,2,64,768]{3,2,0,1:T(8,128)(2,1)S(1)}, u32[]{:S(2)}, u32[]{:S(2)}) collective-permute-start(bf16[4,2,64,768]{3,2,0,1:T(8,128)(2,1)S(1)} %pad_maximum_fusion.9), channel_id=1, source_target_pairs={{0,16},{8,24},{16,0},{24,8},{1,17},{9,25},{17,1},{25,9},{2,18},{10... | collective-permute-start | bytes 2359304 | tf_op jit(solution)/shard_map/ppermute | solution.py:506
  108.7 15.5 %collective-permute-start.12 = (bf16[4,2,2,56,768]{4,3,2,1,0:T(8,128)(2,1)}, bf16[4,2,2,56,768]{4,3,2,1,0:T(8,128)(2,1)}, u32[]{:S(2)}, u32[]{:S(2)}) collective-permute-start(bf16[4,2,2,56,768]{4,3,2,1,0:T(8,128)(2,1)} %pad_maximum_fusion.6), channel_id=1, source_target_pairs={{0,1},{1,0},{2,3},{3,2},{4,5},{5,4},{6,7},{7,6},{8,9},{9,8},{10,11... | collective-permute-start | bytes 4128776 | tf_op jit(solution)/shard_map/ppermute | solution.py:506
  108.9 17.5 %collective-permute-start.11 = (bf16[4,2,2,64,768]{4,3,0,2,1:T(8,128)(2,1)S(1)}, bf16[4,2,2,64,768]{4,3,0,2,1:T(8,128)(2,1)}, u32[]{:S(2)}, u32[]{:S(2)}) collective-permute-start(bf16[4,2,2,64,768]{4,3,0,2,1:T(8,128)(2,1)S(1)} %pad_maximum_fusion.4), channel_id=1, source_target_pairs={{0,1},{1,0},{2,3},{3,2},{4,5},{5,4},{6,7},{7,6},{8,9},{9,8},{10,11... | collective-permute-start | bytes 4718600 | tf_op jit(solution)/shard_map/ppermute | solution.py:506
  153.6 135.4 %reduce-scatter.6.cloned.1.call-start = ((), (), s32[]{:S(2)}) async-start(), calls=%async_computation.8 | async-start | bytes 5308416 | tf_op jit(solution)/shard_map/reduce_scatter | solution.py:660
  173.7 180.7 %reduce-scatter.8.cloned.1.call-start = ((), (), s32[]{:S(2)}) async-start(), calls=%async_computation.9 | async-start | bytes 3981312 | tf_op jit(solution)/shard_map/reduce_scatter | solution.py:660
  245.8 40.4 %collective-permute-start.13 = (bf16[256,768]{1,0:T(8,128)(2,1)}, bf16[256,768]{1,0:T(8,128)(2,1)}, u32[]{:S(2)}, u32[]{:S(2)}) collective-permute-start(bf16[256,768]{1,0:T(8,128)(2,1)} %get-tuple-element.171), channel_id=1, source_target_pairs={{0,8},{8,0},{16,24},{24,16},{1,9},{9,1},{17,25},{25,17},{2,10},{10... | collective-permute-start | bytes 1179656 | tf_op jit(solution)/shard_map/ppermute | solution.py:418
  247.3 37.7 %collective-permute-start.16 = (bf16[256,768]{1,0:T(8,128)(2,1)}, bf16[256,768]{1,0:T(8,128)(2,1)}, u32[]{:S(2)}, u32[]{:S(2)}) collective-permute-start(bf16[256,768]{1,0:T(8,128)(2,1)} %get-tuple-element.172), channel_id=1, source_target_pairs={{16,24},{24,16},{17,25},{25,17},{18,26},{26,18},{19,27},{27,19},{2... | collective-permute-start | bytes 1179656 | tf_op jit(solution)/shard_map/ppermute | solution.py:418
  248.7 37.5 %collective-permute-start.15 = (bf16[256,768]{1,0:T(8,128)(2,1)}, bf16[256,768]{1,0:T(8,128)(2,1)}, u32[]{:S(2)}, u32[]{:S(2)}) collective-permute-start(bf16[256,768]{1,0:T(8,128)(2,1)} %get-tuple-element.174), channel_id=1, source_target_pairs={{0,24},{8,16},{16,8},{24,0},{1,25},{9,17},{17,9},{25,1},{2,26},{10... | collective-permute-start | bytes 1179656 | tf_op jit(solution)/shard_map/ppermute | solution.py:418
  252.9 33.3 %collective-permute-start.14 = (bf16[256,768]{1,0:T(8,128)(2,1)S(1)}, bf16[256,768]{1,0:T(8,128)(2,1)}, u32[]{:S(2)}, u32[]{:S(2)}) collective-permute-start(bf16[256,768]{1,0:T(8,128)(2,1)S(1)} %get-tuple-element.175), channel_id=1, source_target_pairs={{0,16},{8,24},{16,0},{24,8},{1,17},{9,25},{17,1},{25,9},{2,18},{10... | collective-permute-start | bytes 1179656 | tf_op jit(solution)/shard_map/ppermute | solution.py:418
  296.2 16.9 %collective-permute-start.17 = (bf16[4,96,896]{2,1,0:T(8,128)(2,1)}, bf16[4,96,896]{2,1,0:T(8,128)(2,1)}, u32[]{:S(2)}, u32[]{:S(2)}) collective-permute-start(bf16[4,96,896]{2,1,0:T(8,128)(2,1)} %dynamic-slice_bitcast_fusion), channel_id=1, source_target_pairs={{0,1},{1,0},{2,3},{3,2},{4,5},{5,4},{6,7},{7,6},{8,9},{9,8},{10,11... | collective-permute-start | bytes 2064392 | tf_op jit(solution)/shard_map/ppermute | solution.py:463
  299.9 56.5 %all-to-all-start = ((bf16[4,192,768]{2,1,0:T(8,128)(2,1)}), bf16[4,192,768]{2,1,0:T(8,128)(2,1)}, u32[]{:S(2)}, u32[]{:S(2)}) async-start(bf16[4,192,768]{2,1,0:T(8,128)(2,1)} %bitcast.183), calls=%async_computation.2 | async-start | bytes 2359296 | tf_op jit(solution)/shard_map/all_to_all | solution.py:556
  305.9 20.1 %collective-permute-start.22 = (bf16[256,512]{1,0:T(8,128)(2,1)S(1)}, bf16[256,512]{1,0:T(8,128)(2,1)S(1)}, u32[]{:S(2)}, u32[]{:S(2)}) collective-permute-start(bf16[256,512]{1,0:T(8,128)(2,1)S(1)} %get-tuple-element.186), channel_id=1, source_target_pairs={{0,8},{8,0},{16,24},{24,16},{1,9},{9,1},{17,25},{25,17},{2,10},{10... | collective-permute-start | bytes 786440 | tf_op jit(solution)/shard_map/ppermute | solution.py:418
  308.9 29.0 %collective-permute-start.24 = (bf16[256,512]{1,0:T(8,128)(2,1)S(1)}, bf16[256,512]{1,0:T(8,128)(2,1)S(1)}, u32[]{:S(2)}, u32[]{:S(2)}) collective-permute-start(bf16[256,512]{1,0:T(8,128)(2,1)S(1)} %get-tuple-element.189), channel_id=1, source_target_pairs={{0,24},{8,16},{16,8},{24,0},{1,25},{9,17},{17,9},{25,1},{2,26},{10... | collective-permute-start | bytes 786440 | tf_op jit(solution)/shard_map/ppermute | solution.py:418
  313.1 24.8 %collective-permute-start.23 = (bf16[256,512]{1,0:T(8,128)(2,1)S(1)}, bf16[256,512]{1,0:T(8,128)(2,1)S(1)}, u32[]{:S(2)}, u32[]{:S(2)}) collective-permute-start(bf16[256,512]{1,0:T(8,128)(2,1)S(1)} %get-tuple-element.190), channel_id=1, source_target_pairs={{0,16},{8,24},{16,0},{24,8},{1,17},{9,25},{17,1},{25,9},{2,18},{10... | collective-permute-start | bytes 786440 | tf_op jit(solution)/shard_map/ppermute | solution.py:418
  314.4 24.2 %collective-permute-start.18 = (bf16[4,48,896]{2,1,0:T(8,128)(2,1)S(1)}, bf16[4,48,896]{2,1,0:T(8,128)(2,1)S(1)}, u32[]{:S(2)}, u32[]{:S(2)}) collective-permute-start(bf16[4,48,896]{2,1,0:T(8,128)(2,1)S(1)} %dynamic-slice_bitcast_fusion.1), channel_id=1, source_target_pairs={{0,16},{8,24},{16,0},{24,8},{1,17},{9,25},{17,1},{25,9},{2,18},{10... | collective-permute-start | bytes 1032200 | tf_op jit(solution)/shard_map/ppermute | solution.py:463
  344.9 9.4 %collective-permute-start.20 = (bf16[1,48,896]{2,1,0:T(8,128)(2,1)S(1)}, bf16[1,48,896]{2,1,0:T(8,128)(2,1)S(1)}, u32[]{:S(2)}, u32[]{:S(2)}) collective-permute-start(bf16[1,48,896]{2,1,0:T(8,128)(2,1)S(1)} %dynamic-slice_bitcast_fusion.3), channel_id=1, source_target_pairs={{0,4},{1,5},{2,6},{3,7},{4,0},{5,1},{6,2},{7,3},{8,12},{9,13},{10,... | collective-permute-start | bytes 258056 | tf_op jit(solution)/shard_map/ppermute | solution.py:463
  351.7 27.1 %collective-permute-start.26 = (bf16[256,768]{1,0:T(8,128)(2,1)}, bf16[256,768]{1,0:T(8,128)(2,1)S(1)}, u32[]{:S(2)}, u32[]{:S(2)}) collective-permute-start(bf16[256,768]{1,0:T(8,128)(2,1)} %get-tuple-element.166), channel_id=1, source_target_pairs={{16,0},{17,1},{18,2},{19,3},{20,4},{21,5},{22,6},{23,7}} | collective-permute-start | bytes 1179656 | tf_op jit(solution)/shard_map/ppermute | solution.py:418
  353.0 25.8 %collective-permute-start.27 = (bf16[256,768]{1,0:T(8,128)(2,1)}, bf16[256,768]{1,0:T(8,128)(2,1)}, u32[]{:S(2)}, u32[]{:S(2)}) collective-permute-start(bf16[256,768]{1,0:T(8,128)(2,1)} %get-tuple-element.166), channel_id=1, source_target_pairs={{24,0},{25,1},{26,2},{27,3},{28,4},{29,5},{30,6},{31,7}} | collective-permute-start | bytes 1179656 | tf_op jit(solution)/shard_map/ppermute | solution.py:418
  356.4 20.2 %all-to-all-start.1 = ((bf16[4,72,768]{2,1,0:T(8,128)(2,1)}), bf16[4,72,768]{2,1,0:T(8,128)(2,1)S(1)}, u32[]{:S(2)}, u32[]{:S(2)}) async-start(bf16[4,72,768]{2,1,0:T(8,128)(2,1)} %reshape_reshape.13), calls=%async_computation.4 | async-start | bytes 884736 | tf_op jit(solution)/shard_map/all_to_all | solution.py:556
  378.7 11.2 %collective-permute-start.32 = (bf16[192,768]{1,0:T(8,128)(2,1)S(1)}, bf16[192,768]{1,0:T(8,128)(2,1)}, u32[]{:S(2)}, u32[]{:S(2)}) collective-permute-start(bf16[192,768]{1,0:T(8,128)(2,1)S(1)} %reduce_sum.149), channel_id=1, source_target_pairs={{0,8},{8,0},{16,24},{24,16},{1,9},{9,1},{17,25},{25,17},{2,10},{10... | collective-permute-start | bytes 884744 | tf_op jit(solution)/shard_map/ppermute | solution.py:506
  391.8 12.4 %collective-permute-start.33 = (bf16[2,192,768]{2,1,0:T(8,128)(2,1)}, bf16[2,192,768]{2,1,0:T(8,128)(2,1)}, u32[]{:S(2)}, u32[]{:S(2)}) collective-permute-start(bf16[2,192,768]{2,1,0:T(8,128)(2,1)} %pad_maximum_fusion.13), channel_id=1, source_target_pairs={{0,16},{8,24},{16,0},{24,8},{1,17},{9,25},{17,1},{25,9},{2,18},{10... | collective-permute-start | bytes 1769480 | tf_op jit(solution)/shard_map/ppermute | solution.py:506
  (76 other events, 408.9 us)
Sparse Core Ops, SparseCore 0:
  12.0 58.7 all-gather.2
  72.5 50.9 all-gather.4
  153.7 58.8 reduce-scatter.3
  214.7 53.3 reduce-scatter.5
  270.3 42.1 reduce-scatter.7
